TPU v7x, 32 devices: a whole 2x2x4 slice. The times are simulated.
32 devices in a mesh: area: 8 (over z, y), nrn: 4 (over x, core).
Axes of the slice: x: 2, y: 2, z: 4, core: 2. Of those that a mesh axis runs over, the one named last changes fastest.
Arguments:
- history: float32 [4, 4096, 128], P(None, ('area', 'nrn')), may hold values from -1 to 1
- drive: float32 [4096, 128], P(('area', 'nrn')), may hold values from -6 to 6
- leak: float32 [4096], P(('area', 'nrn')), may hold values from 0.1 to 0.9
- w_local: float32 [4096, 512], P(('area', 'nrn')), may hold values from -0.25 to 0.25
- w_long: float32 [4096, 4, 72], P(('area', 'nrn')), may hold values from -0.75 to 0.75
- sender_rows: int32 [32, 8, 9], P(('area', 'nrn')), may hold values from 0 to 127
- delays: int32 [8, 8], P('area'), may hold values from 1 to 4
- area_sizes: int32 [8], P('area'), may hold values from 256 to 512, as said below
Outputs:
- rates: float32 [4096, 128], P(('area', 'nrn'))
Inputs may be any that keep to these rules, and one draw needn't show every extreme that they name: `area_sizes`: every area has at least half of its 512 slots live; some area has all of them live, some exactly half. `sender_rows`: indices may repeat.
All inputs are finite; a program needn't handle non-finite values.
Results may differ from a plain program's by a relative error of at most 0.0018.
Values may be sent and summed in bfloat16 or wider, within the bound.
No kernel may reach another device: no remote copies, remote signals or barrier semaphores. Data moves between devices by JAX's collectives and lax.ppermute only.
A program may use at most 64 MiB of HBM per device.

v0:
```python
import jax
import jax.numpy as jnp
from jax import lax
from jax.sharding import PartitionSpec as P

STEPS = 6


def unround(values):
    return lax.optimization_barrier(values).astype(jnp.float32)


def local(history, drive, leak, w_local, w_long, sender_rows, delays, area_sizes):
    history_depth, block_rows, stimuli = history.shape
    area_count = sender_rows.shape[1]
    proj_count = sender_rows.shape[2]
    offsets = lax.axis_index("nrn") * block_rows + jnp.arange(block_rows, dtype=jnp.int32)
    active = (offsets < area_sizes[0]).astype(jnp.float32)[:, None]
    states = history * active[None]
    picked = ((delays[0] - 1)[:, None] * block_rows + sender_rows[0]).reshape(-1)
    long_flat = w_long.reshape(block_rows, -1)
    for iteration in range(STEPS):
        flat_states = states.reshape(history_depth * block_rows, stimuli)
        outgoing = flat_states[picked].astype(jnp.bfloat16).reshape(area_count, proj_count, stimuli)
        incoming = lax.all_to_all(outgoing, "area", split_axis=0, concat_axis=0, tiled=True)
        current = states[0].astype(jnp.bfloat16)
        all_rows, local_all = (
            lax.all_gather(incoming, "nrn", axis=0, tiled=True),
            lax.all_gather(current, "nrn", axis=0, tiled=True),
        )
        long_term = jnp.dot(
            long_flat,
            unround(all_rows).reshape(-1, stimuli),
            precision=lax.Precision.HIGHEST,
            preferred_element_type=jnp.float32,
        )
        inputs = (
            long_term
            + jnp.dot(
                w_local,
                unround(local_all),
                precision=lax.Precision.HIGHEST,
                preferred_element_type=jnp.float32,
            )
            + drive
        )
        updated = active * (states[0] + leak[:, None] * (jnp.tanh(inputs) - states[0]))
        states = jnp.concatenate([updated[None], states[:-1]], axis=0)
    return states[0]


def solution(mesh):
    placed = (
        P(None, ("area", "nrn"), None),
        P(("area", "nrn"), None),
        P(("area", "nrn")),
        P(("area", "nrn"), None),
        P(("area", "nrn"), None, None),
        P(("area", "nrn"), None, None),
        P("area", None),
        P("area"),
    )
    return jax.shard_map(
        local, mesh=mesh, in_specs=placed, out_specs=P(("area", "nrn"), None), check_vma=False
    )
```

profile of v0, /device:TPU:0, one launch (start us, length us, event | category | flops | bytes accessed | tf_op | source)
XLA Modules:
  0.0 119.0 jit_solution(2239176635262761381)
XLA Ops:
  0.0 0.0 copy-start
  0.0 0.0 copy-start.5
  0.7 0.0 copy-done.5
  0.7 0.0 copy-start.4
  0.7 0.1 add.127
  0.8 0.1 add.128
  0.9 0.5 copy-done.4
  1.4 0.1 squeeze.14
  1.5 1.0 broadcast_multiply_fusion
  2.6 0.6 gather_fusion
  3.2 0.6 convert_element_type.85
  3.8 7.3 %all-to-all-start = ((bf16[8,9,128]{2,1,0:T(8,128)(2,1)}), bf16[8,9,128]{2,1,0:T(8,128)(2,1)S(1)}, u32[]{:S(2)}, u32[]{:S(2)}) async-start(bf16[8,9,128]{2,1,0:T(8,128)(2,1)} %convert_element_type.85), calls=%async_computation | async-start | bytes 65536 | tf_op jit(solution)/shard_map/all_to_all | solution.py:25
  11.1 5.4 %all_gather.37 = bf16[512,128]{1,0:T(8,128)(2,1)S(1)} all-gather(bf16[128,128]{1,0:T(8,128)(2,1)S(1)} %fusion.46), channel_id=1, replica_groups=mesh['area'=8,'nrn'=4] {'nrn'}, dimensions={0}, use_global_device_ids=true | all-gather | bytes 163840 | tf_op jit(solution)/shard_map/all_gather | solution.py:29
  16.6 0.0 copy-done
  16.6 0.3 fusion.53
  16.9 1.0 all-to-all-done
  17.8 5.3 %all_gather.36 = bf16[32,9,128]{2,0,1:T(8,128)(2,1)S(1)} all-gather(bf16[8,9,128]{2,0,1:T(8,128)(2,1)S(1)} %copy.13), channel_id=1, replica_groups=mesh['area'=8,'nrn'=4] {'nrn'}, dimensions={0}, use_global_device_ids=true | all-gather | bytes 92160 | tf_op jit(solution)/shard_map/all_gather | solution.py:28
  23.1 0.0 copy-start.2
  23.2 0.0 copy-start.1
  23.2 0.0 copy-start.3
  23.2 0.7 copy-done.2
  24.0 0.1 copy-done.1
  24.1 0.0 copy-done.3
  24.1 0.4 fusion.48
  24.5 0.6 gather_fusion.1
  25.1 0.6 convert_element_type.88
  25.8 5.0 %all-to-all-start.1 = ((bf16[8,9,128]{2,1,0:T(8,128)(2,1)}), bf16[8,9,128]{2,1,0:T(8,128)(2,1)S(1)}, u32[]{:S(2)}, u32[]{:S(2)}) async-start(bf16[8,9,128]{2,1,0:T(8,128)(2,1)} %convert_element_type.88), calls=%async_computation.1 | async-start | bytes 65536 | tf_op jit(solution)/shard_map/all_to_all | solution.py:25
  30.8 5.4 %all_gather.39 = bf16[512,128]{1,0:T(8,128)(2,1)S(1)} all-gather(bf16[128,128]{1,0:T(8,128)(2,1)S(1)} %get-tuple-element.5), channel_id=1, replica_groups=mesh['area'=8,'nrn'=4] {'nrn'}, dimensions={0}, use_global_device_ids=true | all-gather | bytes 163840 | tf_op jit(solution)/shard_map/all_gather | solution.py:29
  36.2 0.3 fusion.54
  36.5 1.0 all-to-all-done.1
  37.5 5.3 %all_gather.38 = bf16[32,9,128]{2,0,1:T(8,128)(2,1)S(1)} all-gather(bf16[8,9,128]{2,0,1:T(8,128)(2,1)S(1)} %copy.15), channel_id=1, replica_groups=mesh['area'=8,'nrn'=4] {'nrn'}, dimensions={0}, use_global_device_ids=true | all-gather | bytes 92160 | tf_op jit(solution)/shard_map/all_gather | solution.py:28
  42.9 0.4 fusion.49
  43.3 0.6 gather_fusion.2
  43.9 0.6 convert_element_type.91
  44.6 5.0 %all-to-all-start.2 = ((bf16[8,9,128]{2,1,0:T(8,128)(2,1)}), bf16[8,9,128]{2,1,0:T(8,128)(2,1)S(1)}, u32[]{:S(2)}, u32[]{:S(2)}) async-start(bf16[8,9,128]{2,1,0:T(8,128)(2,1)} %convert_element_type.91), calls=%async_computation.2 | async-start | bytes 65536 | tf_op jit(solution)/shard_map/all_to_all | solution.py:25
  49.6 5.4 %all_gather.41 = bf16[512,128]{1,0:T(8,128)(2,1)S(1)} all-gather(bf16[128,128]{1,0:T(8,128)(2,1)S(1)} %get-tuple-element.7), channel_id=1, replica_groups=mesh['area'=8,'nrn'=4] {'nrn'}, dimensions={0}, use_global_device_ids=true | all-gather | bytes 163840 | tf_op jit(solution)/shard_map/all_gather | solution.py:29
  55.0 0.3 fusion.55
  55.3 1.0 all-to-all-done.2
  56.3 5.3 %all_gather.40 = bf16[32,9,128]{2,0,1:T(8,128)(2,1)S(1)} all-gather(bf16[8,9,128]{2,0,1:T(8,128)(2,1)S(1)} %copy.17), channel_id=1, replica_groups=mesh['area'=8,'nrn'=4] {'nrn'}, dimensions={0}, use_global_device_ids=true | all-gather | bytes 92160 | tf_op jit(solution)/shard_map/all_gather | solution.py:28
  61.7 0.4 fusion.50
  62.1 0.6 gather_fusion.3
  62.7 0.6 convert_element_type.94
  63.4 5.0 %all-to-all-start.3 = ((bf16[8,9,128]{2,1,0:T(8,128)(2,1)}), bf16[8,9,128]{2,1,0:T(8,128)(2,1)S(1)}, u32[]{:S(2)}, u32[]{:S(2)}) async-start(bf16[8,9,128]{2,1,0:T(8,128)(2,1)} %convert_element_type.94), calls=%async_computation.3 | async-start | bytes 65536 | tf_op jit(solution)/shard_map/all_to_all | solution.py:25
  68.4 5.4 %all_gather.43 = bf16[512,128]{1,0:T(8,128)(2,1)S(1)} all-gather(bf16[128,128]{1,0:T(8,128)(2,1)S(1)} %get-tuple-element.9), channel_id=1, replica_groups=mesh['area'=8,'nrn'=4] {'nrn'}, dimensions={0}, use_global_device_ids=true | all-gather | bytes 163840 | tf_op jit(solution)/shard_map/all_gather | solution.py:29
  73.8 0.3 fusion.56
  74.1 1.0 all-to-all-done.3
  75.1 5.3 %all_gather.42 = bf16[32,9,128]{2,0,1:T(8,128)(2,1)S(1)} all-gather(bf16[8,9,128]{2,0,1:T(8,128)(2,1)S(1)} %copy.19), channel_id=1, replica_groups=mesh['area'=8,'nrn'=4] {'nrn'}, dimensions={0}, use_global_device_ids=true | all-gather | bytes 92160 | tf_op jit(solution)/shard_map/all_gather | solution.py:28
  80.4 0.4 fusion.51
  80.8 0.6 gather_fusion.4
  81.5 0.6 convert_element_type.97
  82.1 5.0 %all-to-all-start.4 = ((bf16[8,9,128]{2,1,0:T(8,128)(2,1)}), bf16[8,9,128]{2,1,0:T(8,128)(2,1)S(1)}, u32[]{:S(2)}, u32[]{:S(2)}) async-start(bf16[8,9,128]{2,1,0:T(8,128)(2,1)} %convert_element_type.97), calls=%async_computation.4 | async-start | bytes 65536 | tf_op jit(solution)/shard_map/all_to_all | solution.py:25
  87.1 5.4 %all_gather.45 = bf16[512,128]{1,0:T(8,128)(2,1)S(1)} all-gather(bf16[128,128]{1,0:T(8,128)(2,1)S(1)} %get-tuple-element.11), channel_id=1, replica_groups=mesh['area'=8,'nrn'=4] {'nrn'}, dimensions={0}, use_global_device_ids=true | all-gather | bytes 163840 | tf_op jit(solution)/shard_map/all_gather | solution.py:29
  92.5 0.3 fusion.57
  92.8 1.0 all-to-all-done.4
  93.8 5.3 %all_gather.44 = bf16[32,9,128]{2,0,1:T(8,128)(2,1)S(1)} all-gather(bf16[8,9,128]{2,0,1:T(8,128)(2,1)S(1)} %copy.21), channel_id=1, replica_groups=mesh['area'=8,'nrn'=4] {'nrn'}, dimensions={0}, use_global_device_ids=true | all-gather | bytes 92160 | tf_op jit(solution)/shard_map/all_gather | solution.py:28
  99.2 0.4 fusion.52
  99.6 0.6 gather_fusion.5
  100.3 0.6 convert_element_type.100
  100.9 5.0 %all-to-all-start.5 = ((bf16[8,9,128]{2,1,0:T(8,128)(2,1)}), bf16[8,9,128]{2,1,0:T(8,128)(2,1)S(1)}, u32[]{:S(2)}, u32[]{:S(2)}) async-start(bf16[8,9,128]{2,1,0:T(8,128)(2,1)} %convert_element_type.100), calls=%async_computation.5 | async-start | bytes 65536 | tf_op jit(solution)/shard_map/all_to_all | solution.py:25
  105.9 5.4 %all_gather.47 = bf16[512,128]{1,0:T(8,128)(2,1)S(1)} all-gather(bf16[128,128]{1,0:T(8,128)(2,1)S(1)} %get-tuple-element.13), channel_id=1, replica_groups=mesh['area'=8,'nrn'=4] {'nrn'}, dimensions={0}, use_global_device_ids=true | all-gather | bytes 163840 | tf_op jit(solution)/shard_map/all_gather | solution.py:29
  111.3 0.3 fusion.58
  111.6 1.0 all-to-all-done.5
  112.6 5.3 %all_gather.46 = bf16[32,9,128]{2,0,1:T(8,128)(2,1)S(1)} all-gather(bf16[8,9,128]{2,0,1:T(8,128)(2,1)S(1)} %copy.23), channel_id=1, replica_groups=mesh['area'=8,'nrn'=4] {'nrn'}, dimensions={0}, use_global_device_ids=true | all-gather | bytes 92160 | tf_op jit(solution)/shard_map/all_gather | solution.py:28
  118.0 1.0 fusion.41
  (33 shorter events, 0.7 us)
Async XLA Ops:
  0.0 16.6 %copy-start = (f32[128,512]{1,0:T(8,128)S(1)}, f32[128,512]{1,0:T(8,128)}, u32[]{:S(2)}) copy-start(f32[128,512]{1,0:T(8,128)} %param.11) | copy-start | bytes 786436
  0.0 0.7 copy-start.5
  0.7 0.7 copy-start.4
  3.8 14.0 %all-to-all-start = ((bf16[8,9,128]{2,1,0:T(8,128)(2,1)}), bf16[8,9,128]{2,1,0:T(8,128)(2,1)S(1)}, u32[]{:S(2)}, u32[]{:S(2)}) async-start(bf16[8,9,128]{2,1,0:T(8,128)(2,1)} %convert_element_type.85), calls=%async_computation | async-start | bytes 65536 | tf_op jit(solution)/shard_map/all_to_all | solution.py:25
  23.1 0.8 copy-start.2
  23.2 0.9 copy-start.1
  23.2 0.9 copy-start.3
  25.8 11.7 %all-to-all-start.1 = ((bf16[8,9,128]{2,1,0:T(8,128)(2,1)}), bf16[8,9,128]{2,1,0:T(8,128)(2,1)S(1)}, u32[]{:S(2)}, u32[]{:S(2)}) async-start(bf16[8,9,128]{2,1,0:T(8,128)(2,1)} %convert_element_type.88), calls=%async_computation.1 | async-start | bytes 65536 | tf_op jit(solution)/shard_map/all_to_all | solution.py:25
  44.6 11.7 %all-to-all-start.2 = ((bf16[8,9,128]{2,1,0:T(8,128)(2,1)}), bf16[8,9,128]{2,1,0:T(8,128)(2,1)S(1)}, u32[]{:S(2)}, u32[]{:S(2)}) async-start(bf16[8,9,128]{2,1,0:T(8,128)(2,1)} %convert_element_type.91), calls=%async_computation.2 | async-start | bytes 65536 | tf_op jit(solution)/shard_map/all_to_all | solution.py:25
  63.4 11.7 %all-to-all-start.3 = ((bf16[8,9,128]{2,1,0:T(8,128)(2,1)}), bf16[8,9,128]{2,1,0:T(8,128)(2,1)S(1)}, u32[]{:S(2)}, u32[]{:S(2)}) async-start(bf16[8,9,128]{2,1,0:T(8,128)(2,1)} %convert_element_type.94), calls=%async_computation.3 | async-start | bytes 65536 | tf_op jit(solution)/shard_map/all_to_all | solution.py:25
  82.1 11.7 %all-to-all-start.4 = ((bf16[8,9,128]{2,1,0:T(8,128)(2,1)}), bf16[8,9,128]{2,1,0:T(8,128)(2,1)S(1)}, u32[]{:S(2)}, u32[]{:S(2)}) async-start(bf16[8,9,128]{2,1,0:T(8,128)(2,1)} %convert_element_type.97), calls=%async_computation.4 | async-start | bytes 65536 | tf_op jit(solution)/shard_map/all_to_all | solution.py:25
  100.9 11.7 %all-to-all-start.5 = ((bf16[8,9,128]{2,1,0:T(8,128)(2,1)}), bf16[8,9,128]{2,1,0:T(8,128)(2,1)S(1)}, u32[]{:S(2)}, u32[]{:S(2)}) async-start(bf16[8,9,128]{2,1,0:T(8,128)(2,1)} %convert_element_type.100), calls=%async_computation.5 | async-start | bytes 65536 | tf_op jit(solution)/shard_map/all_to_all | solution.py:25
where the time goes:
time: 120 us; the launch traced here: 119 us
  blocking collectives  64.2 us (54%)
  starting transfers between devices  32.4 us (27%)
  local copies, waits for them, and re-layouts  9.83 us (8%)
  waiting for transfers between devices  6 us (5%)
  matrix products  4.36 us (4%)
  other arithmetic  1.2 us (1%)
    all_gather x6, blocking collectives, local(): lax.all_gather(current, 'nrn', axis=0, tiled=True)  32.4 us
    all_to_all x6, starting transfers between devices, local(): lax.all_to_all(outgoing, 'area', split_axis=0, concat_axis=0, tiled=True)  32.4 us
    all_gather x6, blocking collectives, local(): lax.all_gather(incoming, 'nrn', axis=0, tiled=True)  31.7 us
    all_to_all x6, waiting for transfers between devices, local(): lax.all_to_all(outgoing, 'area', split_axis=0, concat_axis=0, tiled=True)  6 us
    gather x6, local copies, waits for them, and re-layouts, local(): flat_states[picked].astype(jnp.bfloat16)  3.83 us
    convert_element_type x6, local copies, waits for them, and re-layouts, local(): flat_states[picked].astype(jnp.bfloat16)  3.82 us
    dot_general x6, matrix products, local(): jnp.dot(long_flat, unround(all_rows).reshape(-1, stimuli), precision=lax....  2.84 us
  transfers between devices with their start and end apart: 6, of which 6 were waited for; matrix products, arithmetic and copies ran while one was open for 1% of the time, Pallas kernels for 0%

commit v1 on v0

v1 whole, which is shorter than its diff:
```python
import functools
import math

import jax
import jax.numpy as jnp
from jax import lax
from jax.experimental import pallas as pl
from jax.experimental.pallas import tpu as pltpu
from jax.sharding import PartitionSpec as P

STEPS = 6
SLOT = 16
SCALE = 2.0**15
F32, BF16 = jnp.float32, jnp.bfloat16
VMEM = pl.BlockSpec(memory_space=pltpu.VMEM)
SMEM = pl.BlockSpec(memory_space=pltpu.SMEM)


def split(values):
    high = lax.reduce_precision(values, 8, 7)
    return high.astype(BF16), (values - high).astype(BF16)


def rows_of(index, count):
    return pl.ds(pl.multiple_of(index * count, count), count)


def choices(meta, columns, width):
    picks = []
    lanes = lax.broadcasted_iota(jnp.int32, (meta.shape[0], width), 1).astype(F32)
    for column in range(columns):
        row = meta[:, 2 + column : 3 + column].astype(F32)
        lag = meta[:, 2 + columns + column : 3 + columns + column].astype(F32)
        picks.append((lanes == row + lag * meta.shape[0]).astype(F32).astype(BF16))
    return jnp.concatenate(picks, axis=0)


def first_kernel(group, columns, misc_ref, out_ref):
    block = misc_ref.shape[0]
    depth = 4
    past = jnp.concatenate([misc_ref[:, i * block : (i + 1) * block] for i in range(depth)], axis=0)
    chosen = choices(misc_ref[:, (depth + 3) * block :], columns, depth * block)
    picked = jnp.dot(chosen, past, preferred_element_type=F32).astype(BF16)
    areas = out_ref.shape[0] // group
    for area in range(areas):
        for member in range(group):
            out_ref[area * group + member] = picked[area * SLOT : (area + 1) * SLOT]


def prepare_kernel(group, columns, me_ref, *refs):
    misc = refs[:group]
    state_ref, drive_ref, rate_ref, choice_ref = refs[group : group + 4]
    past = refs[group + 4 :]
    block = misc[0].shape[0]
    for slot in range(group):
        piece = misc[slot]
        owner = rows_of(me_ref[0] ^ slot, block)
        for age, ref in enumerate(past):
            ref[owner, :] = piece[:, age * block : (age + 1) * block]
        take = lambda i: piece[:, i * block : (i + 1) * block].astype(F32)
        state_ref[slot] = take(0) + take(len(past))
        drive_ref[slot] = take(len(past) + 1) + take(len(past) + 2)
        meta = piece[:, (len(past) + 3) * block :]
        rate = meta[:, 0:1].astype(F32) + meta[:, 1:2].astype(F32)
        rate_ref[slot] = jnp.broadcast_to(rate, rate_ref.shape[1:])
        choice_ref[slot] = choices(meta, columns, len(past) * block)


def step_kernel(group, last, me_ref, *refs):
    high, low = refs[:group], refs[group : 2 * group]
    received, state_ref, drive_ref, rate_ref, choice_ref = refs[2 * group : 2 * group + 5]
    past = refs[2 * group + 5 : 2 * group + 9]
    outs = refs[2 * group + 9 :]
    block, stimuli = state_ref.shape[1:]
    local = group * block
    for slot in range(1 if last else group):
        total = jnp.dot(high[slot][:, :local], past[0][...], preferred_element_type=F32)
        total += jnp.dot(low[slot][:, :local], past[0][...], preferred_element_type=F32)
        total += jnp.dot(high[slot][:, local:], received[...], preferred_element_type=F32)
        total += jnp.dot(low[slot][:, local:], received[...], preferred_element_type=F32)
        inputs = total * (1.0 / SCALE) + drive_ref[slot]
        state = state_ref[slot]
        new = state + rate_ref[slot] * (jnp.tanh(inputs) - state)
        if last:
            outs[0][...] = new
            continue
        new_state_ref, new_past_ref, out_ref = outs
        owner = me_ref[0] ^ slot
        rounded = new.astype(BF16)
        new_state_ref[slot] = new
        new_past_ref[rows_of(owner, block), :] = rounded
        older = [past[age][rows_of(owner, block), :] for age in range(len(past) - 1)]
        recent = jnp.concatenate([rounded] + older, axis=0)
        picked = jnp.dot(choice_ref[slot], recent, preferred_element_type=F32).astype(BF16)
        for area in range(out_ref.shape[0]):
            out_ref[area, rows_of(owner, SLOT), :] = picked[area * SLOT : (area + 1) * SLOT]


def call(kernel, out_shape, operands, index=None):
    shapes = out_shape if isinstance(out_shape, list) else [out_shape]
    held = sum(math.prod(v.shape) * v.dtype.itemsize for v in [*shapes, *operands])
    scalars = [] if index is None else [index]
    return pl.pallas_call(
        kernel,
        out_shape=out_shape,
        in_specs=[SMEM] * len(scalars) + [VMEM] * len(operands),
        out_specs=[VMEM] * len(shapes) if isinstance(out_shape, list) else VMEM,
        compiler_params=pltpu.CompilerParams(vmem_limit_bytes=held + (4 << 20)),
    )(*scalars, *operands)


def local(group, history, drive, leak, w_local, w_long, sender_rows, delays, area_sizes):
    depth, block, stimuli = history.shape
    areas, senders = sender_rows.shape[1:]
    me = lax.axis_index("nrn")
    offsets = me * block + jnp.arange(block, dtype=jnp.int32)
    active = (offsets < area_sizes[0]).astype(F32)
    states = history * active[None, :, None]

    long = w_long.reshape(block, group, areas, senders).transpose(0, 2, 1, 3)
    long = jnp.pad(long, ((0, 0), (0, 0), (0, 0), (0, SLOT - senders))).reshape(block, -1)
    weights = jnp.concatenate([w_local, long], axis=1) * SCALE
    shipped = weights.astype(jnp.float16)

    columns = areas * SLOT // block
    spread = lambda table, fill: jnp.pad(
        table, ((0, 0), (0, SLOT - senders)), constant_values=fill
    ).reshape(columns, block).T.astype(BF16)
    rate_high, rate_low = split(active * leak)
    meta = jnp.concatenate(
        [
            rate_high[:, None],
            rate_low[:, None],
            spread(sender_rows[0], 0),
            spread(jnp.broadcast_to(delays[0][:, None] - 1, (areas, senders)), depth),
        ],
        axis=1,
    )
    meta = jnp.pad(meta, ((0, 0), (0, -meta.shape[1] % 128)))
    now_high, now_low = split(states[0])
    drive_high, drive_low = split(drive)
    misc = jnp.concatenate(
        [now_high]
        + [states[i].astype(BF16) for i in range(1, depth)]
        + [now_low, drive_high, drive_low, meta],
        axis=1,
    )

    swap = lambda values, bit: lax.ppermute(
        values, "nrn", [(i, i ^ bit) for i in range(group)]
    )
    ship = [(shipped, misc)]
    bit = group // 2
    ship += [jax.tree.map(lambda v: swap(v, bit), ship[0])]
    first = call(
        functools.partial(first_kernel, group, columns),
        jax.ShapeDtypeStruct((areas * group, SLOT, stimuli), BF16),
        [misc],
    )
    received = lax.all_to_all(first, ("area", "nrn"), split_axis=0, concat_axis=0, tiled=True)
    pieces = {0: ship[0], bit: ship[1]}
    while bit > 1:
        bit //= 2
        for slot in list(pieces):
            pieces[slot ^ bit] = jax.tree.map(lambda v: swap(v, bit), pieces[slot])
    highs, lows = [], []
    for slot in range(group):
        whole = weights if slot == 0 else pieces[slot][0].astype(F32)
        high, low = split(whole)
        highs.append(high)
        lows.append(low)
    miscs = [pieces[slot][1] for slot in range(group)]
    index = me.astype(jnp.int32).reshape(1)
    cube = jax.ShapeDtypeStruct((group, block, stimuli), F32)
    flat = jax.ShapeDtypeStruct((group * block, stimuli), BF16)
    prepared = call(
        functools.partial(prepare_kernel, group, columns),
        [cube, cube, cube, jax.ShapeDtypeStruct((group, areas * SLOT, depth * block), BF16)]
        + [flat] * depth,
        miscs,
        index,
    )
    state, drives, rates, chosen = prepared[:4]
    past = list(prepared[4:])
    for iteration in range(STEPS):
        final = iteration == STEPS - 1
        if final:
            shapes = jax.ShapeDtypeStruct((block, stimuli), F32)
        else:
            shapes = [cube, flat, jax.ShapeDtypeStruct((areas, group * SLOT, stimuli), BF16)]
        result = call(
            functools.partial(step_kernel, group, final),
            shapes,
            [*highs, *lows, received.reshape(-1, stimuli), state, drives, rates, chosen, *past],
            index,
        )
        if final:
            return result
        state, newest, outgoing = result
        past = [newest] + past[:-1]
        received = lax.all_to_all(outgoing, "area", split_axis=0, concat_axis=0, tiled=True)


def solution(mesh):
    placed = (
        P(None, ("area", "nrn"), None),
        P(("area", "nrn"), None),
        P(("area", "nrn")),
        P(("area", "nrn"), None),
        P(("area", "nrn"), None, None),
        P(("area", "nrn"), None, None),
        P("area", None),
        P("area"),
    )
    return jax.shard_map(
        functools.partial(local, mesh.shape["nrn"]),
        mesh=mesh,
        in_specs=placed,
        out_specs=P(("area", "nrn"), None),
        check_vma=False,
    )
```

time: 120 us -> 90 us (0.75)
  starting transfers between devices: 32.4 us -> 10.4 us
  blocking collectives: 64.2 us -> 53.1 us
  Pallas kernels: 0 us -> 10.4 us
  matrix products: 4.36 us -> 0 us
  waiting for transfers between devices: 6 us -> 2.97 us
  other arithmetic: 1.2 us -> 2.5 us
    all_gather x12 -> x0, blocking collectives: 64.2 us -> none  [the longest x6 32.4 us: local(): lax.all_gather(current, 'nrn', axis=0, tiled=True)]
    all_to_all x0 -> x5, blocking collectives: none -> 53.1 us  [local(): lax.all_to_all(outgoing, 'area', split_axis=0, concat_axis=0, tiled=True)]
    all_to_all x6 -> x1, starting transfers between devices: 32.4 us -> 6.43 us  [local(): lax.all_to_all(first, ('area', 'nrn'), split_axis=0, concat_axis=0, tiled...]
    pallas_call x0 -> x8, Pallas kernels: none -> 10.4 us  [call(): pl.pallas_call(kernel, out_shape=out_shape, in_specs=[SMEM] * len(scalars...]
    unnamed x12 -> x29, local copies, waits for them, and re-layouts: 1.39 us -> 8.51 us
    all_to_all x6 -> x1, waiting for transfers between devices: 6 us -> 0.44 us  [local(): lax.all_to_all(first, ('area', 'nrn'), split_axis=0, concat_axis=0, tiled...]
    dot_general x12 -> x0, matrix products: 4.36 us -> none  [the longest x6 2.84 us: local(): jnp.dot(long_flat, unround(all_rows).reshape(-1, stimuli), precision=lax....]
    ppermute x0 -> x6, starting transfers between devices: none -> 3.92 us  [local(): lax.ppermute(values, 'nrn', [(i, i ^ bit) for i in range(group)])]
  transfers between devices with their start and end apart: 6 -> 7, of which waited for: 6 -> 2; matrix products, arithmetic and copies ran while one was open for 1% -> 2% of each run, Pallas kernels for 0% -> 2%
where the time goes in v1:
time: 90 us; the launch traced here: 89.4 us
  blocking collectives  53.1 us (59%)
  starting transfers between devices  10.4 us (12%)
  Pallas kernels  10.4 us (12%)
  local copies, waits for them, and re-layouts  9.08 us (10%)
  waiting for transfers between devices  2.97 us (3%)
  other arithmetic  2.5 us (3%)
  between operations  0.91 us (1%)
    all_to_all x5, blocking collectives, local(): lax.all_to_all(outgoing, 'area', split_axis=0, concat_axis=0, tiled=True)  53.1 us
    pallas_call x8, Pallas kernels, call(): pl.pallas_call(kernel, out_shape=out_shape, in_specs=[SMEM] * len(scalars...  10.4 us
    unnamed x29, local copies, waits for them, and re-layouts  8.51 us
    all_to_all x1, starting transfers between devices, local(): lax.all_to_all(first, ('area', 'nrn'), split_axis=0, concat_axis=0, tiled...  6.43 us
    ppermute x6, starting transfers between devices, local(): lax.ppermute(values, 'nrn', [(i, i ^ bit) for i in range(group)])  3.92 us
    ppermute x6, waiting for transfers between devices, local(): lax.ppermute(values, 'nrn', [(i, i ^ bit) for i in range(group)])  2.53 us
  transfers between devices with their start and end apart: 7, of which 2 were waited for; matrix products, arithmetic and copies ran while one was open for 2% of the time, Pallas kernels for 2%

profile of v1, /device:TPU:0, one launch (start us, length us, event | category | flops | bytes accessed | tf_op | source)
XLA Modules:
  0.0 89.4 jit_solution(1392443907446652233)
XLA Ops:
  0.7 1.1 %fusion.17 = (bf16[4,128,128]{2,1,0:T(8,128)(2,1)S(1)}, f32[4,128,128]{2,1,0:T(8,128)S(1)}) fusion(f32[4,128,128]{2,1,0:T(8,128)} %param.8, f32[128]{0:T(128)S(1)} %compare_convert_fusion), kind=kLoop, calls=%fused_computation.44 | loop fusion | flops 131072 | bytes 655872 | tf_op jit(solution)/shard_map/convert.7
  1.8 0.0 copy-start.7
  1.8 0.8 copy-done.7
  2.6 0.0 copy-start.8
  2.7 0.0 copy-start.10
  2.7 0.7 copy-done.10
  3.4 0.0 copy-start.11
  3.4 0.6 copy-done.11
  4.0 0.1 broadcast_in_dim.14
  4.1 0.0 copy-start.9
  4.1 0.1 convert_element_type.124
  4.2 0.6 copy-done.9
  4.8 0.1 convert_element_type.123
  4.9 0.1 copy.24
  5.1 3.0 %collective-permute-start.4 = (bf16[128,1024]{1,0:T(8,128)(2,1)S(1)}, bf16[128,1024]{1,0:T(8,128)(2,1)S(1)}, u32[]{:S(2)}, u32[]{:S(2)}) collective-permute-start(bf16[128,1024]{1,0:T(8,128)(2,1)S(1)} %pad_dynamic-update-slice_fusion.misc_ref.refs_0_), channel_id=1, source_target_pairs={{0,2},{1,3},{2,0},{3,1},{4,6},{5,7},{6,4},{7,5},{8,10},{9,11},{10,... | collective-permute-start | bytes 786440 | tf_op jit(solution)/shard_map/ppermute | solution.py:149
  8.1 0.0 copy-done.8
  8.2 0.0 copy-start.6
  8.2 0.1 copy.23
  8.4 0.8 copy-done.6
  9.2 0.1 fusion
  9.3 0.1 collective-permute-start.1
  9.4 0.1 collective-permute-start
  9.5 0.5 collective-permute-start.3
  10.0 1.0 %shard_map.82 = bf16[32,16,128]{2,1,0:T(8,128)(2,1)} custom-call(bf16[128,1024]{1,0:T(8,128)(2,1)S(1)} %pad_dynamic-update-slice_fusion.misc_ref.refs_0_), custom_call_target="tpu_custom_call" | custom-call | tf_op jit(solution)/shard_map/pallas_call | solution.py:103
  10.9 6.4 %all-to-all-start = ((bf16[32,16,128]{2,1,0:T(8,128)(2,1)}), bf16[32,16,128]{2,1,0:T(8,128)(2,1)}, u32[]{:S(2)}, u32[]{:S(2)}) async-start(bf16[32,16,128]{2,1,0:T(8,128)(2,1)} %shard_map.82), calls=%async_computation | async-start | bytes 262144 | tf_op jit(solution)/shard_map/all_to_all | solution.py:160
  17.4 0.0 collective-permute-done.4.refs_2_
  17.4 0.2 collective-permute-start.5
  17.6 2.5 %collective-permute-done.1 = f16[128,1024]{1,0:T(8,128)(2,1)} collective-permute-done((f16[128,1024]{1,0:T(8,128)(2,1)S(1)}, f16[128,1024]{1,0:T(8,128)(2,1)}, u32[]{:S(2)}, u32[]{:S(2)}) %collective-permute-start.1) | collective-permute-done | bytes 262176 | tf_op jit(solution)/shard_map/ppermute | solution.py:149
  20.1 0.0 collective-permute-start.2
  20.1 1.0 %fusion.2 = (bf16[128,1024]{1,0:T(8,128)(2,1)S(1)}, bf16[128,1024]{1,0:T(8,128)(2,1)S(1)}) fusion(f16[128,1024]{1,0:T(8,128)(2,1)} %collective-permute-done.1), kind=kLoop, calls=%fused_computation.10 | loop fusion | flops 655360 | bytes 786432 | tf_op jit(solution)/shard_map/convert_element_type | solution.py:21
  21.2 0.0 collective-permute-done
  21.2 0.1 fusion.1
  21.3 0.0 collective-permute-done.3.refs_1_
  21.3 0.0 copy-start.2
  21.3 0.7 copy-done.2
  22.0 0.0 collective-permute-done.5.refs_3_
  22.0 0.0 copy-start.3
  22.0 0.9 %copy-done.3 = bf16[128,1024]{1,0:T(8,128)(2,1)S(1)} copy-done((bf16[128,1024]{1,0:T(8,128)(2,1)S(1)}, bf16[128,1024]{1,0:T(8,128)(2,1)}, u32[]{:S(2)}) %copy-start.3) | copy-done | bytes 262168
  23.0 0.7 shard_map.83
  23.7 0.0 copy-start
  23.7 0.7 copy-done
  24.4 0.0 copy-start.4
  24.4 0.6 copy-done.4
  25.0 0.0 collective-permute-done.2
  25.0 0.1 fusion.3
  25.1 0.4 all-to-all-done
  25.5 0.0 copy-start.1
  25.6 0.9 %copy-done.1 = f32[4,128,128]{2,1,0:T(8,128)S(1)} copy-done((f32[4,128,128]{2,1,0:T(8,128)S(1)}, f32[4,128,128]{2,1,0:T(8,128)}, u32[]{:S(2)}) %copy-start.1) | copy-done | bytes 262168
  26.5 0.0 copy-start.5
  26.5 0.9 %copy-done.5 = bf16[512,128]{1,0:T(8,128)(2,1)S(1)} copy-done((bf16[512,128]{1,0:T(8,128)(2,1)S(1)}, bf16[512,128]{1,0:T(8,128)(2,1)}, u32[]{:S(2)}) %copy-start.5) | copy-done | bytes 131096
  27.4 2.3 %shard_map.84 = (f32[4,128,128]{2,1,0:T(8,128)S(1)}, bf16[512,128]{1,0:T(8,128)(2,1)S(1)}, bf16[8,64,128]{2,1,0:T(8,128)(2,1)S(1)}) custom-call(s32[1]{0:T(128)} %bitcast.me_ref, bf16[128,1024]{1,0:T(8,128)(2,1)S(1)} %get-tuple-element.57.refs_0_, bf16[128,1024]{1,0:T(8,128)(2,1)S(1)} %get-tuple-element.63.refs_1_, ...), custom_call_target="tpu_custom_call" | custom-call | tf_op jit(solution)/shard_map/pallas_call | solution.py:103
  29.7 14.1 %all_to_all.30 = bf16[8,64,128]{2,1,0:T(8,128)(2,1)S(1)} all-to-all(bf16[8,64,128]{2,1,0:T(8,128)(2,1)S(1)} %get-tuple-element.36), channel_id=1, replica_groups=mesh['area'=8,'nrn'=4] {'area'}, dimensions={0} | all-to-all | bytes 262144 | tf_op jit(solution)/shard_map/all_to_all | solution.py:201
  43.7 1.4 %shard_map.85 = (f32[4,128,128]{2,1,0:T(8,128)S(1)}, bf16[512,128]{1,0:T(8,128)(2,1)S(1)}, bf16[8,64,128]{2,1,0:T(8,128)(2,1)S(1)}) custom-call(s32[1]{0:T(128)} %bitcast.me_ref, bf16[128,1024]{1,0:T(8,128)(2,1)S(1)} %get-tuple-element.57.refs_0_, bf16[128,1024]{1,0:T(8,128)(2,1)S(1)} %get-tuple-element.63.refs_1_, ...), custom_call_target="tpu_custom_call" | custom-call | tf_op jit(solution)/shard_map/pallas_call | solution.py:103
  45.1 9.9 %all_to_all.31 = bf16[8,64,128]{2,1,0:T(8,128)(2,1)S(1)} all-to-all(bf16[8,64,128]{2,1,0:T(8,128)(2,1)S(1)} %get-tuple-element.39), channel_id=1, replica_groups=mesh['area'=8,'nrn'=4] {'area'}, dimensions={0} | all-to-all | bytes 262144 | tf_op jit(solution)/shard_map/all_to_all | solution.py:201
  55.0 1.4 %shard_map.86 = (f32[4,128,128]{2,1,0:T(8,128)S(1)}, bf16[512,128]{1,0:T(8,128)(2,1)S(1)}, bf16[8,64,128]{2,1,0:T(8,128)(2,1)S(1)}) custom-call(s32[1]{0:T(128)} %bitcast.me_ref, bf16[128,1024]{1,0:T(8,128)(2,1)S(1)} %get-tuple-element.57.refs_0_, bf16[128,1024]{1,0:T(8,128)(2,1)S(1)} %get-tuple-element.63.refs_1_, ...), custom_call_target="tpu_custom_call" | custom-call | tf_op jit(solution)/shard_map/pallas_call | solution.py:103
  56.4 9.7 %all_to_all.32 = bf16[8,64,128]{2,1,0:T(8,128)(2,1)S(1)} all-to-all(bf16[8,64,128]{2,1,0:T(8,128)(2,1)S(1)} %get-tuple-element.42), channel_id=1, replica_groups=mesh['area'=8,'nrn'=4] {'area'}, dimensions={0} | all-to-all | bytes 262144 | tf_op jit(solution)/shard_map/all_to_all | solution.py:201
  66.1 1.4 %shard_map.87 = (f32[4,128,128]{2,1,0:T(8,128)S(1)}, bf16[512,128]{1,0:T(8,128)(2,1)S(1)}, bf16[8,64,128]{2,1,0:T(8,128)(2,1)S(1)}) custom-call(s32[1]{0:T(128)} %bitcast.me_ref, bf16[128,1024]{1,0:T(8,128)(2,1)S(1)} %get-tuple-element.57.refs_0_, bf16[128,1024]{1,0:T(8,128)(2,1)S(1)} %get-tuple-element.63.refs_1_, ...), custom_call_target="tpu_custom_call" | custom-call | tf_op jit(solution)/shard_map/pallas_call | solution.py:103
  67.5 9.7 %all_to_all.33 = bf16[8,64,128]{2,1,0:T(8,128)(2,1)S(1)} all-to-all(bf16[8,64,128]{2,1,0:T(8,128)(2,1)S(1)} %get-tuple-element.45), channel_id=1, replica_groups=mesh['area'=8,'nrn'=4] {'area'}, dimensions={0} | all-to-all | bytes 262144 | tf_op jit(solution)/shard_map/all_to_all | solution.py:201
  77.3 1.4 %shard_map.88 = (f32[4,128,128]{2,1,0:T(8,128)S(1)}, bf16[512,128]{1,0:T(8,128)(2,1)S(1)}, bf16[8,64,128]{2,1,0:T(8,128)(2,1)S(1)}) custom-call(s32[1]{0:T(128)} %bitcast.me_ref, bf16[128,1024]{1,0:T(8,128)(2,1)S(1)} %get-tuple-element.57.refs_0_, bf16[128,1024]{1,0:T(8,128)(2,1)S(1)} %get-tuple-element.63.refs_1_, ...), custom_call_target="tpu_custom_call" | custom-call | tf_op jit(solution)/shard_map/pallas_call | solution.py:103
  78.7 9.7 %all_to_all.34 = bf16[8,64,128]{2,1,0:T(8,128)(2,1)S(1)} all-to-all(bf16[8,64,128]{2,1,0:T(8,128)(2,1)S(1)} %get-tuple-element.48), channel_id=1, replica_groups=mesh['area'=8,'nrn'=4] {'area'}, dimensions={0} | all-to-all | bytes 262144 | tf_op jit(solution)/shard_map/all_to_all | solution.py:201
  88.4 0.9 %shard_map.89 = f32[128,128]{1,0:T(8,128)} custom-call(s32[1]{0:T(128)} %bitcast.me_ref, bf16[128,1024]{1,0:T(8,128)(2,1)S(1)} %get-tuple-element.57.refs_0_, bf16[128,1024]{1,0:T(8,128)(2,1)S(1)} %get-tuple-element.63.refs_1_, bf16[128,1024]{1,0:T(8,128)(2,1)S(1)} %get-tuple-element.61.refs_2_, bf16[128,1024]{1,0:T(8,128)(2,1)S(1)} %get-tuple-element.59.refs_3_, ...), custom_call_target="tpu_custom_call" | custom-call | tf_op jit(solution)/shard_map/pallas_call | solution.py:103
  (19 shorter events, 0.3 us)
Async XLA Ops:
  1.8 0.8 copy-start.7
  2.6 5.5 %copy-start.8 = (f32[128,4,72]{0,2,1:T(8,128)S(1)}, f32[128,4,72]{0,2,1:T(8,128)}, u32[]{:S(2)}) copy-start(f32[128,4,72]{0,2,1:T(8,128)} %param.12) | copy-start | bytes 442372
  2.7 0.7 copy-start.10
  3.4 0.7 copy-start.11
  4.1 0.7 copy-start.9
  5.1 12.3 %collective-permute-start.4 = (bf16[128,1024]{1,0:T(8,128)(2,1)S(1)}, bf16[128,1024]{1,0:T(8,128)(2,1)S(1)}, u32[]{:S(2)}, u32[]{:S(2)}) collective-permute-start(bf16[128,1024]{1,0:T(8,128)(2,1)S(1)} %pad_dynamic-update-slice_fusion.misc_ref.refs_0_), channel_id=1, source_target_pairs={{0,2},{1,3},{2,0},{3,1},{4,6},{5,7},{6,4},{7,5},{8,10},{9,11},{10,... | collective-permute-start | bytes 786440 | tf_op jit(solution)/shard_map/ppermute | solution.py:149
  8.2 1.0 %copy-start.6 = (f32[128,512]{1,0:T(8,128)S(1)}, f32[128,512]{1,0:T(8,128)}, u32[]{:S(2)}) copy-start(f32[128,512]{1,0:T(8,128)} %param.11) | copy-start | bytes 786436
  9.3 10.8 %collective-permute-start.1 = (f16[128,1024]{1,0:T(8,128)(2,1)S(1)}, f16[128,1024]{1,0:T(8,128)(2,1)}, u32[]{:S(2)}, u32[]{:S(2)}) collective-permute-start(f16[128,1024]{1,0:T(8,128)(2,1)S(1)} %get-tuple-element.56), channel_id=1, source_target_pairs={{0,2},{1,3},{2,0},{3,1},{4,6},{5,7},{6,4},{7,5},{8,10},{9,11},{10,... | collective-permute-start | bytes 786440 | tf_op jit(solution)/shard_map/ppermute | solution.py:149
  9.4 11.8 %collective-permute-start = (f16[128,1024]{1,0:T(8,128)(2,1)S(1)}, f16[128,1024]{1,0:T(8,128)(2,1)S(1)}, u32[]{:S(2)}, u32[]{:S(2)}) collective-permute-start(f16[128,1024]{1,0:T(8,128)(2,1)S(1)} %get-tuple-element.56), channel_id=1, source_target_pairs={{0,1},{1,0},{2,3},{3,2},{4,5},{5,4},{6,7},{7,6},{8,9},{9,8},{10,11... | collective-permute-start | bytes 786440 | tf_op jit(solution)/shard_map/ppermute | solution.py:149
  9.5 11.8 %collective-permute-start.3 = (bf16[128,1024]{1,0:T(8,128)(2,1)S(1)}, bf16[128,1024]{1,0:T(8,128)(2,1)S(1)}, u32[]{:S(2)}, u32[]{:S(2)}) collective-permute-start(bf16[128,1024]{1,0:T(8,128)(2,1)S(1)} %pad_dynamic-update-slice_fusion.misc_ref.refs_0_), channel_id=1, source_target_pairs={{0,1},{1,0},{2,3},{3,2},{4,5},{5,4},{6,7},{7,6},{8,9},{9,8},{10,11... | collective-permute-start | bytes 786440 | tf_op jit(solution)/shard_map/ppermute | solution.py:149
  10.9 14.6 %all-to-all-start = ((bf16[32,16,128]{2,1,0:T(8,128)(2,1)}), bf16[32,16,128]{2,1,0:T(8,128)(2,1)}, u32[]{:S(2)}, u32[]{:S(2)}) async-start(bf16[32,16,128]{2,1,0:T(8,128)(2,1)} %shard_map.82), calls=%async_computation | async-start | bytes 262144 | tf_op jit(solution)/shard_map/all_to_all | solution.py:160
  17.4 4.6 %collective-permute-start.5 = (bf16[128,1024]{1,0:T(8,128)(2,1)S(1)}, bf16[128,1024]{1,0:T(8,128)(2,1)S(1)}, u32[]{:S(2)}, u32[]{:S(2)}) collective-permute-start(bf16[128,1024]{1,0:T(8,128)(2,1)S(1)} %collective-permute-done.4.refs_2_), channel_id=1, source_target_pairs={{0,1},{1,0},{2,3},{3,2},{4,5},{5,4},{6,7},{7,6},{8,9},{9,8},{10,11... | collective-permute-start | bytes 786440 | tf_op jit(solution)/shard_map/ppermute | solution.py:149
  20.1 4.9 %collective-permute-start.2 = (f16[128,1024]{1,0:T(8,128)(2,1)}, f16[128,1024]{1,0:T(8,128)(2,1)S(1)}, u32[]{:S(2)}, u32[]{:S(2)}) collective-permute-start(f16[128,1024]{1,0:T(8,128)(2,1)} %collective-permute-done.1), channel_id=1, source_target_pairs={{0,1},{1,0},{2,3},{3,2},{4,5},{5,4},{6,7},{7,6},{8,9},{9,8},{10,11... | collective-permute-start | bytes 786440 | tf_op jit(solution)/shard_map/ppermute | solution.py:149
  21.3 0.7 copy-start.2
  22.0 1.0 %copy-start.3 = (bf16[128,1024]{1,0:T(8,128)(2,1)S(1)}, bf16[128,1024]{1,0:T(8,128)(2,1)}, u32[]{:S(2)}) copy-start(bf16[128,1024]{1,0:T(8,128)(2,1)} %copy-done.2) | copy-start | bytes 786436
  23.7 0.7 copy-start
  24.4 0.6 copy-start.4
  25.5 1.0 %copy-start.1 = (f32[4,128,128]{2,1,0:T(8,128)S(1)}, f32[4,128,128]{2,1,0:T(8,128)}, u32[]{:S(2)}) copy-start(f32[4,128,128]{2,1,0:T(8,128)} %copy-done) | copy-start | bytes 786436
  26.5 0.9 %copy-start.5 = (bf16[512,128]{1,0:T(8,128)(2,1)S(1)}, bf16[512,128]{1,0:T(8,128)(2,1)}, u32[]{:S(2)}) copy-start(bf16[512,128]{1,0:T(8,128)(2,1)} %copy-done.4) | copy-start | bytes 393220

commit v2 on v0

v2 whole, which is shorter than its diff:
```python
import functools
import math

import jax
import jax.numpy as jnp
from jax import lax
from jax.experimental import pallas as pl
from jax.experimental.pallas import tpu as pltpu
from jax.sharding import PartitionSpec as P

STEPS = 6
SLOT = 16
TERMS = 3
F32, BF16 = jnp.float32, jnp.bfloat16
VMEM = pl.BlockSpec(memory_space=pltpu.VMEM)


def iota(shape, axis):
    return lax.broadcasted_iota(jnp.int32, shape, axis)


def terms_of(values):
    terms = []
    for _ in range(TERMS):
        terms.append(values.astype(BF16))
        values = values - terms[-1].astype(F32)
    return terms


def column(line):
    width = line.shape[1]
    eye = iota((width, width), 0) == iota((width, width), 1)
    return jnp.sum(jnp.where(eye, jnp.broadcast_to(line, eye.shape), 0.0), axis=1, keepdims=True)


def send(picked, out_ref, group):
    for area in range(out_ref.shape[0] // group):
        for member in range(group):
            out_ref[area * group + member] = picked[area * SLOT : (area + 1) * SLOT]


def pack_kernel(group, senders, *refs):
    given, outs, scratch = refs[:7], refs[7:-9], refs[-9:]
    held, padded, sems = scratch[:7], scratch[7], scratch[8]
    weights, state, rate, choice, outgoing, *past = outs
    copies = [
        pltpu.make_async_copy(src, dst, sems.at[i]) for i, (src, dst) in enumerate(zip(given, held))
    ]
    for copy in copies:
        copy.start()
    for copy in copies:
        copy.wait()
    history, leak, w_local, w_long, table, lags, sizes = held
    depth, block = history.shape[:2]
    areas = table.shape[0]
    me = lax.axis_index("nrn")
    active = (iota((block, 1), 0) + me * block < sizes[0:1, 0:1]).astype(F32)
    state[...] = history[0] * active
    for age in range(depth):
        past[age][...] = (history[age] * active).astype(BF16)
    rate[...] = jnp.broadcast_to(active * column(leak[...]), rate.shape)

    lines = jnp.concatenate(
        [table[...].astype(F32), jnp.zeros((areas, SLOT - senders), F32)], axis=1
    )
    real = iota((SLOT, 1), 0) < senders
    places = []
    for area in range(areas):
        age = lags[0:1, area : area + 1].astype(F32) - 1.0
        age = jnp.where(real, jnp.broadcast_to(age, real.shape), float(depth))
        places.append(column(lines[area : area + 1]) + age * block)
    lanes = iota((areas * SLOT, depth * block), 1).astype(F32)
    choice[...] = (lanes == jnp.concatenate(places, axis=0)).astype(F32).astype(BF16)
    recent = jnp.concatenate([ref[...] for ref in past], axis=0)
    send(jnp.dot(choice[...], recent, preferred_element_type=F32).astype(BF16), outgoing, group)

    near = w_local.shape[1]
    for term, values in enumerate(terms_of(w_local[...])):
        weights[term * block : (term + 1) * block, :near] = values
    blank = jnp.zeros((SLOT - senders, block), F32)
    for area in range(areas):
        for member in range(group):
            spot = (area * group + member) * SLOT
            piece = w_long[member, area * senders : (area + 1) * senders, :]
            padded[spot : spot + SLOT, :] = jnp.concatenate([piece, blank], axis=0)
    for part in range(padded.shape[0] // block):
        tile = padded[part * block : (part + 1) * block, :].T
        for term, values in enumerate(terms_of(tile)):
            spot = near + part * block
            weights[term * block : (term + 1) * block, spot : spot + block] = values


def step_kernel(group, depth, last, *refs):
    (weights, received, state, drive, rate, choice), refs = refs[:6], refs[6:]
    mates, past, refs = refs[:group], refs[group : group + depth - 1], refs[group + depth - 1 :]
    current, outs = refs[-1], refs[:-1]
    block = state.shape[0]
    near = group * block
    me = lax.axis_index("nrn")
    for slot in range(group):
        start = pl.multiple_of((me ^ slot) * block, block)
        current[pl.ds(start, block), :] = mates[slot][...]
    total = jnp.dot(weights[:, :near], current[...], preferred_element_type=F32)
    total += jnp.dot(weights[:, near:], received[...], preferred_element_type=F32)
    parts = [total[term * block : (term + 1) * block] for term in range(TERMS)]
    inputs = functools.reduce(lambda a, b: a + b, reversed(parts)) + drive[...]
    old = state[...]
    new = old + rate[...] * (jnp.tanh(inputs) - old)
    if last:
        outs[0][...] = new
        return
    new_state, newest, outgoing = outs
    new_state[...] = new
    newest[...] = new.astype(BF16)
    recent = jnp.concatenate([new.astype(BF16), mates[0][...]] + [ref[...] for ref in past[:-1]], axis=0)
    send(jnp.dot(choice[...], recent, preferred_element_type=F32).astype(BF16), outgoing, group)


def call(kernel, out_shape, operands, scratch=(), **settings):
    size = lambda value: math.prod(value.shape) * value.dtype.itemsize
    held = sum(map(size, [*out_shape, *operands]))
    return pl.pallas_call(
        kernel,
        out_shape=out_shape,
        out_specs=[VMEM] * len(out_shape),
        compiler_params=pltpu.CompilerParams(vmem_limit_bytes=held + (4 << 20)),
        scratch_shapes=scratch,
        **{"in_specs": [VMEM] * len(operands), **settings},
    )(*operands)


def local(group, history, drive, leak, w_local, w_long, sender_rows, delays, area_sizes):
    depth, block, stimuli = history.shape
    areas, senders = sender_rows.shape[1:]
    near, far = group * block, areas * group * SLOT
    shape = jax.ShapeDtypeStruct
    tile = lambda kind: shape((block, stimuli), kind)
    sent = shape((areas * group, SLOT, stimuli), BF16)
    given = [
        history,
        leak.reshape(1, block),
        w_local,
        w_long.transpose(1, 2, 0),
        sender_rows[0],
        delays,
        area_sizes.reshape(1, 1),
    ]
    stay = lambda v: pltpu.with_memory_space_constraint(v, pltpu.HBM) if v.size > 1 else v
    weights, state, rate, choice, outgoing, *past = call(
        functools.partial(pack_kernel, group, senders),
        [
            shape((TERMS * block, near + far), BF16),
            tile(F32),
            tile(F32),
            shape((areas * SLOT, depth * block), BF16),
            sent,
            *[tile(BF16)] * depth,
        ],
        [stay(v) for v in given],
        [pltpu.VMEM(v.shape, v.dtype) for v in given]
        + [pltpu.VMEM((far, block), F32), pltpu.SemaphoreType.DMA((len(given),))],
        in_specs=[pl.BlockSpec(memory_space=pl.ANY)] * len(given),
    )
    swap = lambda v, bits: lax.ppermute(v, "nrn", [(i, i ^ bits) for i in range(group)])
    for iteration in range(STEPS):
        final = iteration == STEPS - 1
        mates = [swap(past[0], bits) for bits in range(1, group)]
        received = lax.all_to_all(outgoing, ("area", "nrn"), split_axis=0, concat_axis=0, tiled=True)
        received, mates = lax.optimization_barrier((received, mates))
        result = call(
            functools.partial(step_kernel, group, depth, final),
            [tile(F32)] if final else [tile(F32), tile(BF16), sent],
            [weights, received.reshape(far, stimuli), state, drive, rate, choice, past[0], *mates, *past[1:]],
            [pltpu.VMEM((near, stimuli), BF16)],
        )
        if final:
            return result[0]
        state, newest, outgoing = result
        past = [newest, *past[:-1]]


def solution(mesh):
    placed = (
        P(None, ("area", "nrn"), None),
        P(("area", "nrn"), None),
        P(("area", "nrn")),
        P(("area", "nrn"), None),
        P(("area", "nrn"), None, None),
        P(("area", "nrn"), None, None),
        P("area", None),
        P("area"),
    )
    return jax.shard_map(
        functools.partial(local, mesh.shape["nrn"]),
        mesh=mesh,
        in_specs=placed,
        out_specs=P(("area", "nrn"), None),
        check_vma=False,
    )
```

time: 120 us -> 79.8 us (0.66)
  blocking collectives: 64.2 us -> 0 us
  waiting for transfers between devices: 6 us -> 37.6 us
  local copies, waits for them, and re-layouts: 9.83 us -> 0.01 us
  Pallas kernels: 0 us -> 9.27 us
  matrix products: 4.36 us -> 0 us
  other arithmetic: 1.2 us -> 0 us
    all_gather x12 -> x0, blocking collectives: 64.2 us -> none  [the longest x6 32.4 us: local(): lax.all_gather(current, 'nrn', axis=0, tiled=True)]
    ppermute x0 -> x18, waiting for transfers between devices: none -> 21.7 us  [local(): lax.ppermute(v, 'nrn', [(i, i ^ bits) for i in range(group)])]
    all_to_all x6, starting transfers between devices: 32.4 us -> 20.1 us  [local(): lax.all_to_all(outgoing, ('area', 'nrn'), split_axis=0, concat_axis=0, ti...]
    ppermute x0 -> x18, starting transfers between devices: none -> 11.6 us  [local(): lax.ppermute(v, 'nrn', [(i, i ^ bits) for i in range(group)])]
    all_to_all x6, waiting for transfers between devices: 6 us -> 16 us  [local(): lax.all_to_all(outgoing, ('area', 'nrn'), split_axis=0, concat_axis=0, ti...]
    pallas_call x0 -> x7, Pallas kernels: none -> 9.27 us  [call(): pl.pallas_call(kernel, out_shape=out_shape, out_specs=[VMEM] * len(out_sh...]
    dot_general x12 -> x0, matrix products: 4.36 us -> none  [the longest x6 2.84 us: local(): jnp.dot(long_flat, unround(all_rows).reshape(-1, stimuli), precision=lax....]
    gather x6 -> x0, local copies, waits for them, and re-layouts: 3.83 us -> none  [local(): flat_states[picked].astype(jnp.bfloat16)]
  transfers between devices with their start and end apart: 6 -> 24, of which waited for: 6 -> 18; matrix products, arithmetic and copies ran while one was open for 1% -> 0% of each run, Pallas kernels for 0% -> 0%
where the time goes in v2:
time: 79.8 us; the launch traced here: 79.3 us
  waiting for transfers between devices  37.6 us (47%)
  starting transfers between devices  31.7 us (40%)
  Pallas kernels  9.27 us (12%)
    ppermute x18, waiting for transfers between devices, local(): lax.ppermute(v, 'nrn', [(i, i ^ bits) for i in range(group)])  21.7 us
    all_to_all x6, starting transfers between devices, local(): lax.all_to_all(outgoing, ('area', 'nrn'), split_axis=0, concat_axis=0, ti...  20.1 us
    all_to_all x6, waiting for transfers between devices, local(): lax.all_to_all(outgoing, ('area', 'nrn'), split_axis=0, concat_axis=0, ti...  16 us
    ppermute x18, starting transfers between devices, local(): lax.ppermute(v, 'nrn', [(i, i ^ bits) for i in range(group)])  11.6 us
    pallas_call x7, Pallas kernels, call(): pl.pallas_call(kernel, out_shape=out_shape, out_specs=[VMEM] * len(out_sh...  9.27 us
  transfers between devices with their start and end apart: 24, of which 18 were waited for; matrix products, arithmetic and copies ran while one was open for 0% of the time, Pallas kernels for 0%

profile of v2, /device:TPU:0, one launch (start us, length us, event | category | flops | bytes accessed | tf_op | source)
XLA Modules:
  0.0 79.3 jit_solution(14747081619458164298)
XLA Ops:
  0.7 2.3 %shard_map.82 = (bf16[384,1024]{1,0:T(8,128)(2,1)S(1)}, f32[128,128]{1,0:T(8,128)S(1)}, f32[128,128]{1,0:T(8,128)S(1)}, bf16[128,512]{1,0:T(8,128)(2,1)S(1)}, bf...) custom-call(f32[4,128,128]{2,1,0:T(8,128)} %refs_0_.1, ...), custom_call_target="tpu_custom_call" | custom-call | tf_op jit(solution)/shard_map/pallas_call | solution.py:122
  3.0 0.0 copy-start
  3.0 7.3 %all-to-all-start = ((bf16[32,16,128]{2,1,0:T(8,128)(2,1)}), bf16[32,16,128]{2,1,0:T(8,128)(2,1)S(1)}, u32[]{:S(2)}, u32[]{:S(2)}) async-start(bf16[32,16,128]{2,1,0:T(8,128)(2,1)} %get-tuple-element.54), calls=%async_computation | async-start | bytes 262144 | tf_op jit(solution)/shard_map/all_to_all | solution.py:168
  10.3 1.6 %collective-permute-start.2 = (bf16[128,128]{1,0:T(8,128)(2,1)S(1)}, bf16[128,128]{1,0:T(8,128)(2,1)S(1)}, u32[]{:S(2)}, u32[]{:S(2)}) collective-permute-start(bf16[128,128]{1,0:T(8,128)(2,1)S(1)} %get-tuple-element.55.refs_6_.refs_10_.refs_11_.refs_12_), channel_id=1, source_target_pairs={{0,3},{1,2},{2,1},{3,0},{4,7},{5,6},{6,5},{7,4},{8,11},{9,10},{10,... | collective-permute-start | bytes 98312 | tf_op jit(solution)/shard_map/ppermute | solution.py:164
  11.9 0.4 collective-permute-start.1
  12.3 0.0 collective-permute-start
  12.3 1.5 %collective-permute-done.2.refs_9_ = bf16[128,128]{1,0:T(8,128)(2,1)S(1)} collective-permute-done((bf16[128,128]{1,0:T(8,128)(2,1)S(1)}, bf16[128,128]{1,0:T(8,128)(2,1)S(1)}, u32[]{:S(2)}, u32[]{:S(2)}) %collective-permute-start.2) | collective-permute-done | bytes 32800 | tf_op jit(solution)/shard_map/ppermute | solution.py:164
  13.7 2.2 %collective-permute-done.1.refs_8_ = bf16[128,128]{1,0:T(8,128)(2,1)S(1)} collective-permute-done((bf16[128,128]{1,0:T(8,128)(2,1)S(1)}, bf16[128,128]{1,0:T(8,128)(2,1)S(1)}, u32[]{:S(2)}, u32[]{:S(2)}) %collective-permute-start.1) | collective-permute-done | bytes 32800 | tf_op jit(solution)/shard_map/ppermute | solution.py:164
  16.0 0.0 collective-permute-done.refs_7_
  16.0 2.6 %all-to-all-done = bf16[32,16,128]{2,1,0:T(8,128)(2,1)S(1)} async-done(((bf16[32,16,128]{2,1,0:T(8,128)(2,1)}), bf16[32,16,128]{2,1,0:T(8,128)(2,1)S(1)}, u32[]{:S(2)}, u32[]{:S(2)}) %all-to-all-start) | async-done | bytes 131104 | tf_op jit(solution)/shard_map/all_to_all | solution.py:168
  18.5 0.0 copy-done
  18.5 1.2 %shard_map.83 = (f32[128,128]{1,0:T(8,128)S(1)}, bf16[128,128]{1,0:T(8,128)(2,1)S(1)}, bf16[32,16,128]{2,1,0:T(8,128)(2,1)}) custom-call(bf16[384,1024]{1,0:T(8,128)(2,1)S(1)} %get-tuple-element.53.refs_0_, bf16[512,128]{1,0:T(8,128)(2,1)S(1)} %bitcast.12, f32[128,128]{1,0:T(8,128)S(1)} %get-tuple-element.57.refs_2_, f32[128,128]{1,0:T(8,128)S(1)} %copy-done, ...), custom_call_target="tpu_custom_call" | custom-call | tf_op jit(solution)/shard_map/pallas_call | solution.py:122
  19.7 2.6 %all-to-all-start.1 = ((bf16[32,16,128]{2,1,0:T(8,128)(2,1)}), bf16[32,16,128]{2,1,0:T(8,128)(2,1)S(1)}, u32[]{:S(2)}, u32[]{:S(2)}) async-start(bf16[32,16,128]{2,1,0:T(8,128)(2,1)} %get-tuple-element.66), calls=%async_computation.1 | async-start | bytes 262144 | tf_op jit(solution)/shard_map/all_to_all | solution.py:168
  22.3 1.4 %collective-permute-start.5 = (bf16[128,128]{1,0:T(8,128)(2,1)S(1)}, bf16[128,128]{1,0:T(8,128)(2,1)S(1)}, u32[]{:S(2)}, u32[]{:S(2)}) collective-permute-start(bf16[128,128]{1,0:T(8,128)(2,1)S(1)} %get-tuple-element.67.refs_6_.refs_10_.refs_11_.refs_12_), channel_id=1, source_target_pairs={{0,3},{1,2},{2,1},{3,0},{4,7},{5,6},{6,5},{7,4},{8,11},{9,10},{10,... | collective-permute-start | bytes 98312 | tf_op jit(solution)/shard_map/ppermute | solution.py:164
  23.7 0.4 collective-permute-start.4
  24.1 0.1 collective-permute-start.3
  24.2 1.6 %collective-permute-done.5.refs_9_ = bf16[128,128]{1,0:T(8,128)(2,1)S(1)} collective-permute-done((bf16[128,128]{1,0:T(8,128)(2,1)S(1)}, bf16[128,128]{1,0:T(8,128)(2,1)S(1)}, u32[]{:S(2)}, u32[]{:S(2)}) %collective-permute-start.5) | collective-permute-done | bytes 32800 | tf_op jit(solution)/shard_map/ppermute | solution.py:164
  25.8 2.0 %collective-permute-done.4.refs_8_ = bf16[128,128]{1,0:T(8,128)(2,1)S(1)} collective-permute-done((bf16[128,128]{1,0:T(8,128)(2,1)S(1)}, bf16[128,128]{1,0:T(8,128)(2,1)S(1)}, u32[]{:S(2)}, u32[]{:S(2)}) %collective-permute-start.4) | collective-permute-done | bytes 32800 | tf_op jit(solution)/shard_map/ppermute | solution.py:164
  27.8 0.0 collective-permute-done.3.refs_7_
  27.8 2.7 %all-to-all-done.1 = bf16[32,16,128]{2,1,0:T(8,128)(2,1)S(1)} async-done(((bf16[32,16,128]{2,1,0:T(8,128)(2,1)}), bf16[32,16,128]{2,1,0:T(8,128)(2,1)S(1)}, u32[]{:S(2)}, u32[]{:S(2)}) %all-to-all-start.1) | async-done | bytes 131104 | tf_op jit(solution)/shard_map/all_to_all | solution.py:168
  30.5 1.2 %shard_map.84 = (f32[128,128]{1,0:T(8,128)S(1)}, bf16[128,128]{1,0:T(8,128)(2,1)S(1)}, bf16[32,16,128]{2,1,0:T(8,128)(2,1)}) custom-call(bf16[384,1024]{1,0:T(8,128)(2,1)S(1)} %get-tuple-element.53.refs_0_, bf16[512,128]{1,0:T(8,128)(2,1)S(1)} %bitcast.13, f32[128,128]{1,0:T(8,128)S(1)} %get-tuple-element.69.refs_2_, f32[128,128]{1,0:T(8,128)S(1)} %copy-done, ...), custom_call_target="tpu_custom_call" | custom-call | tf_op jit(solution)/shard_map/pallas_call | solution.py:122
  31.7 2.6 %all-to-all-start.2 = ((bf16[32,16,128]{2,1,0:T(8,128)(2,1)}), bf16[32,16,128]{2,1,0:T(8,128)(2,1)S(1)}, u32[]{:S(2)}, u32[]{:S(2)}) async-start(bf16[32,16,128]{2,1,0:T(8,128)(2,1)} %get-tuple-element.73), calls=%async_computation.2 | async-start | bytes 262144 | tf_op jit(solution)/shard_map/all_to_all | solution.py:168
  34.3 1.4 %collective-permute-start.8 = (bf16[128,128]{1,0:T(8,128)(2,1)S(1)}, bf16[128,128]{1,0:T(8,128)(2,1)S(1)}, u32[]{:S(2)}, u32[]{:S(2)}) collective-permute-start(bf16[128,128]{1,0:T(8,128)(2,1)S(1)} %get-tuple-element.74.refs_6_.refs_10_.refs_11_.refs_12_), channel_id=1, source_target_pairs={{0,3},{1,2},{2,1},{3,0},{4,7},{5,6},{6,5},{7,4},{8,11},{9,10},{10,... | collective-permute-start | bytes 98312 | tf_op jit(solution)/shard_map/ppermute | solution.py:164
  35.7 0.4 collective-permute-start.7
  36.1 0.1 collective-permute-start.6
  36.2 1.6 %collective-permute-done.8.refs_9_ = bf16[128,128]{1,0:T(8,128)(2,1)S(1)} collective-permute-done((bf16[128,128]{1,0:T(8,128)(2,1)S(1)}, bf16[128,128]{1,0:T(8,128)(2,1)S(1)}, u32[]{:S(2)}, u32[]{:S(2)}) %collective-permute-start.8) | collective-permute-done | bytes 32800 | tf_op jit(solution)/shard_map/ppermute | solution.py:164
  37.8 2.0 %collective-permute-done.7.refs_8_ = bf16[128,128]{1,0:T(8,128)(2,1)S(1)} collective-permute-done((bf16[128,128]{1,0:T(8,128)(2,1)S(1)}, bf16[128,128]{1,0:T(8,128)(2,1)S(1)}, u32[]{:S(2)}, u32[]{:S(2)}) %collective-permute-start.7) | collective-permute-done | bytes 32800 | tf_op jit(solution)/shard_map/ppermute | solution.py:164
  39.8 0.0 collective-permute-done.6.refs_7_
  39.8 2.7 %all-to-all-done.2 = bf16[32,16,128]{2,1,0:T(8,128)(2,1)S(1)} async-done(((bf16[32,16,128]{2,1,0:T(8,128)(2,1)}), bf16[32,16,128]{2,1,0:T(8,128)(2,1)S(1)}, u32[]{:S(2)}, u32[]{:S(2)}) %all-to-all-start.2) | async-done | bytes 131104 | tf_op jit(solution)/shard_map/all_to_all | solution.py:168
  42.5 1.2 %shard_map.85 = (f32[128,128]{1,0:T(8,128)S(1)}, bf16[128,128]{1,0:T(8,128)(2,1)S(1)}, bf16[32,16,128]{2,1,0:T(8,128)(2,1)}) custom-call(bf16[384,1024]{1,0:T(8,128)(2,1)S(1)} %get-tuple-element.53.refs_0_, bf16[512,128]{1,0:T(8,128)(2,1)S(1)} %bitcast.14, f32[128,128]{1,0:T(8,128)S(1)} %get-tuple-element.76.refs_2_, f32[128,128]{1,0:T(8,128)S(1)} %copy-done, ...), custom_call_target="tpu_custom_call" | custom-call | tf_op jit(solution)/shard_map/pallas_call | solution.py:122
  43.6 2.6 %all-to-all-start.3 = ((bf16[32,16,128]{2,1,0:T(8,128)(2,1)}), bf16[32,16,128]{2,1,0:T(8,128)(2,1)S(1)}, u32[]{:S(2)}, u32[]{:S(2)}) async-start(bf16[32,16,128]{2,1,0:T(8,128)(2,1)} %get-tuple-element.80), calls=%async_computation.3 | async-start | bytes 262144 | tf_op jit(solution)/shard_map/all_to_all | solution.py:168
  46.2 1.4 %collective-permute-start.11 = (bf16[128,128]{1,0:T(8,128)(2,1)S(1)}, bf16[128,128]{1,0:T(8,128)(2,1)S(1)}, u32[]{:S(2)}, u32[]{:S(2)}) collective-permute-start(bf16[128,128]{1,0:T(8,128)(2,1)S(1)} %get-tuple-element.81.refs_6_.refs_10_.refs_11_), channel_id=1, source_target_pairs={{0,3},{1,2},{2,1},{3,0},{4,7},{5,6},{6,5},{7,4},{8,11},{9,10},{10,... | collective-permute-start | bytes 98312 | tf_op jit(solution)/shard_map/ppermute | solution.py:164
  47.6 0.4 collective-permute-start.10
  48.0 0.1 collective-permute-start.9
  48.1 1.6 %collective-permute-done.11.refs_9_ = bf16[128,128]{1,0:T(8,128)(2,1)S(1)} collective-permute-done((bf16[128,128]{1,0:T(8,128)(2,1)S(1)}, bf16[128,128]{1,0:T(8,128)(2,1)S(1)}, u32[]{:S(2)}, u32[]{:S(2)}) %collective-permute-start.11) | collective-permute-done | bytes 32800 | tf_op jit(solution)/shard_map/ppermute | solution.py:164
  49.7 2.0 %collective-permute-done.10.refs_8_ = bf16[128,128]{1,0:T(8,128)(2,1)S(1)} collective-permute-done((bf16[128,128]{1,0:T(8,128)(2,1)S(1)}, bf16[128,128]{1,0:T(8,128)(2,1)S(1)}, u32[]{:S(2)}, u32[]{:S(2)}) %collective-permute-start.10) | collective-permute-done | bytes 32800 | tf_op jit(solution)/shard_map/ppermute | solution.py:164
  51.7 0.0 collective-permute-done.9.refs_7_
  51.7 2.7 %all-to-all-done.3 = bf16[32,16,128]{2,1,0:T(8,128)(2,1)S(1)} async-done(((bf16[32,16,128]{2,1,0:T(8,128)(2,1)}), bf16[32,16,128]{2,1,0:T(8,128)(2,1)S(1)}, u32[]{:S(2)}, u32[]{:S(2)}) %all-to-all-start.3) | async-done | bytes 131104 | tf_op jit(solution)/shard_map/all_to_all | solution.py:168
  54.4 1.2 %shard_map.86 = (f32[128,128]{1,0:T(8,128)S(1)}, bf16[128,128]{1,0:T(8,128)(2,1)S(1)}, bf16[32,16,128]{2,1,0:T(8,128)(2,1)}) custom-call(bf16[384,1024]{1,0:T(8,128)(2,1)S(1)} %get-tuple-element.53.refs_0_, bf16[512,128]{1,0:T(8,128)(2,1)S(1)} %bitcast.15, f32[128,128]{1,0:T(8,128)S(1)} %get-tuple-element.83.refs_2_, f32[128,128]{1,0:T(8,128)S(1)} %copy-done, ...), custom_call_target="tpu_custom_call" | custom-call | tf_op jit(solution)/shard_map/pallas_call | solution.py:122
  55.6 2.6 %all-to-all-start.4 = ((bf16[32,16,128]{2,1,0:T(8,128)(2,1)}), bf16[32,16,128]{2,1,0:T(8,128)(2,1)S(1)}, u32[]{:S(2)}, u32[]{:S(2)}) async-start(bf16[32,16,128]{2,1,0:T(8,128)(2,1)} %get-tuple-element.87), calls=%async_computation.4 | async-start | bytes 262144 | tf_op jit(solution)/shard_map/all_to_all | solution.py:168
  58.2 1.4 %collective-permute-start.14 = (bf16[128,128]{1,0:T(8,128)(2,1)S(1)}, bf16[128,128]{1,0:T(8,128)(2,1)S(1)}, u32[]{:S(2)}, u32[]{:S(2)}) collective-permute-start(bf16[128,128]{1,0:T(8,128)(2,1)S(1)} %get-tuple-element.88.refs_6_.refs_10_), channel_id=1, source_target_pairs={{0,3},{1,2},{2,1},{3,0},{4,7},{5,6},{6,5},{7,4},{8,11},{9,10},{10,... | collective-permute-start | bytes 98312 | tf_op jit(solution)/shard_map/ppermute | solution.py:164
  59.6 0.4 collective-permute-start.13
  60.0 0.1 collective-permute-start.12
  60.1 1.6 %collective-permute-done.14.refs_9_ = bf16[128,128]{1,0:T(8,128)(2,1)S(1)} collective-permute-done((bf16[128,128]{1,0:T(8,128)(2,1)S(1)}, bf16[128,128]{1,0:T(8,128)(2,1)S(1)}, u32[]{:S(2)}, u32[]{:S(2)}) %collective-permute-start.14) | collective-permute-done | bytes 32800 | tf_op jit(solution)/shard_map/ppermute | solution.py:164
  61.7 2.0 %collective-permute-done.13.refs_8_ = bf16[128,128]{1,0:T(8,128)(2,1)S(1)} collective-permute-done((bf16[128,128]{1,0:T(8,128)(2,1)S(1)}, bf16[128,128]{1,0:T(8,128)(2,1)S(1)}, u32[]{:S(2)}, u32[]{:S(2)}) %collective-permute-start.13) | collective-permute-done | bytes 32800 | tf_op jit(solution)/shard_map/ppermute | solution.py:164
  63.7 0.0 collective-permute-done.12.refs_7_
  63.7 2.7 %all-to-all-done.4 = bf16[32,16,128]{2,1,0:T(8,128)(2,1)S(1)} async-done(((bf16[32,16,128]{2,1,0:T(8,128)(2,1)}), bf16[32,16,128]{2,1,0:T(8,128)(2,1)S(1)}, u32[]{:S(2)}, u32[]{:S(2)}) %all-to-all-start.4) | async-done | bytes 131104 | tf_op jit(solution)/shard_map/all_to_all | solution.py:168
  66.4 1.2 %shard_map.87 = (f32[128,128]{1,0:T(8,128)S(1)}, bf16[128,128]{1,0:T(8,128)(2,1)S(1)}, bf16[32,16,128]{2,1,0:T(8,128)(2,1)}) custom-call(bf16[384,1024]{1,0:T(8,128)(2,1)S(1)} %get-tuple-element.53.refs_0_, bf16[512,128]{1,0:T(8,128)(2,1)S(1)} %bitcast.16, f32[128,128]{1,0:T(8,128)S(1)} %get-tuple-element.90.refs_2_, f32[128,128]{1,0:T(8,128)S(1)} %copy-done, ...), custom_call_target="tpu_custom_call" | custom-call | tf_op jit(solution)/shard_map/pallas_call | solution.py:122
  67.6 2.6 %all-to-all-start.5 = ((bf16[32,16,128]{2,1,0:T(8,128)(2,1)}), bf16[32,16,128]{2,1,0:T(8,128)(2,1)S(1)}, u32[]{:S(2)}, u32[]{:S(2)}) async-start(bf16[32,16,128]{2,1,0:T(8,128)(2,1)} %get-tuple-element.94), calls=%async_computation.5 | async-start | bytes 262144 | tf_op jit(solution)/shard_map/all_to_all | solution.py:168
  70.1 1.4 %collective-permute-start.17 = (bf16[128,128]{1,0:T(8,128)(2,1)S(1)}, bf16[128,128]{1,0:T(8,128)(2,1)S(1)}, u32[]{:S(2)}, u32[]{:S(2)}) collective-permute-start(bf16[128,128]{1,0:T(8,128)(2,1)S(1)} %get-tuple-element.95.refs_6_), channel_id=1, source_target_pairs={{0,3},{1,2},{2,1},{3,0},{4,7},{5,6},{6,5},{7,4},{8,11},{9,10},{10,... | collective-permute-start | bytes 98312 | tf_op jit(solution)/shard_map/ppermute | solution.py:164
  71.6 0.4 collective-permute-start.16
  71.9 0.1 collective-permute-start.15
  72.1 1.6 %collective-permute-done.17.refs_9_ = bf16[128,128]{1,0:T(8,128)(2,1)S(1)} collective-permute-done((bf16[128,128]{1,0:T(8,128)(2,1)S(1)}, bf16[128,128]{1,0:T(8,128)(2,1)S(1)}, u32[]{:S(2)}, u32[]{:S(2)}) %collective-permute-start.17) | collective-permute-done | bytes 32800 | tf_op jit(solution)/shard_map/ppermute | solution.py:164
  73.7 2.0 %collective-permute-done.16.refs_8_ = bf16[128,128]{1,0:T(8,128)(2,1)S(1)} collective-permute-done((bf16[128,128]{1,0:T(8,128)(2,1)S(1)}, bf16[128,128]{1,0:T(8,128)(2,1)S(1)}, u32[]{:S(2)}, u32[]{:S(2)}) %collective-permute-start.16) | collective-permute-done | bytes 32800 | tf_op jit(solution)/shard_map/ppermute | solution.py:164
  75.7 0.0 collective-permute-done.15.refs_7_
  75.7 2.7 %all-to-all-done.5 = bf16[32,16,128]{2,1,0:T(8,128)(2,1)S(1)} async-done(((bf16[32,16,128]{2,1,0:T(8,128)(2,1)}), bf16[32,16,128]{2,1,0:T(8,128)(2,1)S(1)}, u32[]{:S(2)}, u32[]{:S(2)}) %all-to-all-start.5) | async-done | bytes 131104 | tf_op jit(solution)/shard_map/all_to_all | solution.py:168
  78.3 1.0 %shard_map.88 = f32[128,128]{1,0:T(8,128)} custom-call(bf16[384,1024]{1,0:T(8,128)(2,1)S(1)} %get-tuple-element.53.refs_0_, bf16[512,128]{1,0:T(8,128)(2,1)S(1)} %bitcast.11, f32[128,128]{1,0:T(8,128)S(1)} %get-tuple-element.97.refs_2_, f32[128,128]{1,0:T(8,128)S(1)} %copy-done, f32[128,128]{1,0:T(8,128)S(1)} %get-tuple-element.58.refs_4_, ...), custom_call_target="tpu_custom_call" | custom-call | tf_op jit(solution)/shard_map/pallas_call | solution.py:122
Async XLA Ops:
  3.0 15.6 %copy-start = (f32[128,128]{1,0:T(8,128)S(1)}, f32[128,128]{1,0:T(8,128)}, u32[]{:S(2)}) copy-start(f32[128,128]{1,0:T(8,128)} %refs_3_.11) | copy-start | bytes 196612
  3.0 15.5 %all-to-all-start = ((bf16[32,16,128]{2,1,0:T(8,128)(2,1)}), bf16[32,16,128]{2,1,0:T(8,128)(2,1)S(1)}, u32[]{:S(2)}, u32[]{:S(2)}) async-start(bf16[32,16,128]{2,1,0:T(8,128)(2,1)} %get-tuple-element.54), calls=%async_computation | async-start | bytes 262144 | tf_op jit(solution)/shard_map/all_to_all | solution.py:168
  10.3 3.4 %collective-permute-start.2 = (bf16[128,128]{1,0:T(8,128)(2,1)S(1)}, bf16[128,128]{1,0:T(8,128)(2,1)S(1)}, u32[]{:S(2)}, u32[]{:S(2)}) collective-permute-start(bf16[128,128]{1,0:T(8,128)(2,1)S(1)} %get-tuple-element.55.refs_6_.refs_10_.refs_11_.refs_12_), channel_id=1, source_target_pairs={{0,3},{1,2},{2,1},{3,0},{4,7},{5,6},{6,5},{7,4},{8,11},{9,10},{10,... | collective-permute-start | bytes 98312 | tf_op jit(solution)/shard_map/ppermute | solution.py:164
  11.9 4.1 %collective-permute-start.1 = (bf16[128,128]{1,0:T(8,128)(2,1)S(1)}, bf16[128,128]{1,0:T(8,128)(2,1)S(1)}, u32[]{:S(2)}, u32[]{:S(2)}) collective-permute-start(bf16[128,128]{1,0:T(8,128)(2,1)S(1)} %get-tuple-element.55.refs_6_.refs_10_.refs_11_.refs_12_), channel_id=1, source_target_pairs={{0,2},{1,3},{2,0},{3,1},{4,6},{5,7},{6,4},{7,5},{8,10},{9,11},{10,... | collective-permute-start | bytes 98312 | tf_op jit(solution)/shard_map/ppermute | solution.py:164
  12.3 3.7 %collective-permute-start = (bf16[128,128]{1,0:T(8,128)(2,1)S(1)}, bf16[128,128]{1,0:T(8,128)(2,1)S(1)}, u32[]{:S(2)}, u32[]{:S(2)}) collective-permute-start(bf16[128,128]{1,0:T(8,128)(2,1)S(1)} %get-tuple-element.55.refs_6_.refs_10_.refs_11_.refs_12_), channel_id=1, source_target_pairs={{0,1},{1,0},{2,3},{3,2},{4,5},{5,4},{6,7},{7,6},{8,9},{9,8},{10,11... | collective-permute-start | bytes 98312 | tf_op jit(solution)/shard_map/ppermute | solution.py:164
  19.7 10.8 %all-to-all-start.1 = ((bf16[32,16,128]{2,1,0:T(8,128)(2,1)}), bf16[32,16,128]{2,1,0:T(8,128)(2,1)S(1)}, u32[]{:S(2)}, u32[]{:S(2)}) async-start(bf16[32,16,128]{2,1,0:T(8,128)(2,1)} %get-tuple-element.66), calls=%async_computation.1 | async-start | bytes 262144 | tf_op jit(solution)/shard_map/all_to_all | solution.py:168
  22.3 3.5 %collective-permute-start.5 = (bf16[128,128]{1,0:T(8,128)(2,1)S(1)}, bf16[128,128]{1,0:T(8,128)(2,1)S(1)}, u32[]{:S(2)}, u32[]{:S(2)}) collective-permute-start(bf16[128,128]{1,0:T(8,128)(2,1)S(1)} %get-tuple-element.67.refs_6_.refs_10_.refs_11_.refs_12_), channel_id=1, source_target_pairs={{0,3},{1,2},{2,1},{3,0},{4,7},{5,6},{6,5},{7,4},{8,11},{9,10},{10,... | collective-permute-start | bytes 98312 | tf_op jit(solution)/shard_map/ppermute | solution.py:164
  23.7 4.1 %collective-permute-start.4 = (bf16[128,128]{1,0:T(8,128)(2,1)S(1)}, bf16[128,128]{1,0:T(8,128)(2,1)S(1)}, u32[]{:S(2)}, u32[]{:S(2)}) collective-permute-start(bf16[128,128]{1,0:T(8,128)(2,1)S(1)} %get-tuple-element.67.refs_6_.refs_10_.refs_11_.refs_12_), channel_id=1, source_target_pairs={{0,2},{1,3},{2,0},{3,1},{4,6},{5,7},{6,4},{7,5},{8,10},{9,11},{10,... | collective-permute-start | bytes 98312 | tf_op jit(solution)/shard_map/ppermute | solution.py:164
  24.1 3.7 %collective-permute-start.3 = (bf16[128,128]{1,0:T(8,128)(2,1)S(1)}, bf16[128,128]{1,0:T(8,128)(2,1)S(1)}, u32[]{:S(2)}, u32[]{:S(2)}) collective-permute-start(bf16[128,128]{1,0:T(8,128)(2,1)S(1)} %get-tuple-element.67.refs_6_.refs_10_.refs_11_.refs_12_), channel_id=1, source_target_pairs={{0,1},{1,0},{2,3},{3,2},{4,5},{5,4},{6,7},{7,6},{8,9},{9,8},{10,11... | collective-permute-start | bytes 98312 | tf_op jit(solution)/shard_map/ppermute | solution.py:164
  31.7 10.8 %all-to-all-start.2 = ((bf16[32,16,128]{2,1,0:T(8,128)(2,1)}), bf16[32,16,128]{2,1,0:T(8,128)(2,1)S(1)}, u32[]{:S(2)}, u32[]{:S(2)}) async-start(bf16[32,16,128]{2,1,0:T(8,128)(2,1)} %get-tuple-element.73), calls=%async_computation.2 | async-start | bytes 262144 | tf_op jit(solution)/shard_map/all_to_all | solution.py:168
  34.3 3.5 %collective-permute-start.8 = (bf16[128,128]{1,0:T(8,128)(2,1)S(1)}, bf16[128,128]{1,0:T(8,128)(2,1)S(1)}, u32[]{:S(2)}, u32[]{:S(2)}) collective-permute-start(bf16[128,128]{1,0:T(8,128)(2,1)S(1)} %get-tuple-element.74.refs_6_.refs_10_.refs_11_.refs_12_), channel_id=1, source_target_pairs={{0,3},{1,2},{2,1},{3,0},{4,7},{5,6},{6,5},{7,4},{8,11},{9,10},{10,... | collective-permute-start | bytes 98312 | tf_op jit(solution)/shard_map/ppermute | solution.py:164
  35.7 4.1 %collective-permute-start.7 = (bf16[128,128]{1,0:T(8,128)(2,1)S(1)}, bf16[128,128]{1,0:T(8,128)(2,1)S(1)}, u32[]{:S(2)}, u32[]{:S(2)}) collective-permute-start(bf16[128,128]{1,0:T(8,128)(2,1)S(1)} %get-tuple-element.74.refs_6_.refs_10_.refs_11_.refs_12_), channel_id=1, source_target_pairs={{0,2},{1,3},{2,0},{3,1},{4,6},{5,7},{6,4},{7,5},{8,10},{9,11},{10,... | collective-permute-start | bytes 98312 | tf_op jit(solution)/shard_map/ppermute | solution.py:164
  36.1 3.7 %collective-permute-start.6 = (bf16[128,128]{1,0:T(8,128)(2,1)S(1)}, bf16[128,128]{1,0:T(8,128)(2,1)S(1)}, u32[]{:S(2)}, u32[]{:S(2)}) collective-permute-start(bf16[128,128]{1,0:T(8,128)(2,1)S(1)} %get-tuple-element.74.refs_6_.refs_10_.refs_11_.refs_12_), channel_id=1, source_target_pairs={{0,1},{1,0},{2,3},{3,2},{4,5},{5,4},{6,7},{7,6},{8,9},{9,8},{10,11... | collective-permute-start | bytes 98312 | tf_op jit(solution)/shard_map/ppermute | solution.py:164
  43.6 10.8 %all-to-all-start.3 = ((bf16[32,16,128]{2,1,0:T(8,128)(2,1)}), bf16[32,16,128]{2,1,0:T(8,128)(2,1)S(1)}, u32[]{:S(2)}, u32[]{:S(2)}) async-start(bf16[32,16,128]{2,1,0:T(8,128)(2,1)} %get-tuple-element.80), calls=%async_computation.3 | async-start | bytes 262144 | tf_op jit(solution)/shard_map/all_to_all | solution.py:168
  46.2 3.5 %collective-permute-start.11 = (bf16[128,128]{1,0:T(8,128)(2,1)S(1)}, bf16[128,128]{1,0:T(8,128)(2,1)S(1)}, u32[]{:S(2)}, u32[]{:S(2)}) collective-permute-start(bf16[128,128]{1,0:T(8,128)(2,1)S(1)} %get-tuple-element.81.refs_6_.refs_10_.refs_11_), channel_id=1, source_target_pairs={{0,3},{1,2},{2,1},{3,0},{4,7},{5,6},{6,5},{7,4},{8,11},{9,10},{10,... | collective-permute-start | bytes 98312 | tf_op jit(solution)/shard_map/ppermute | solution.py:164
  47.6 4.1 %collective-permute-start.10 = (bf16[128,128]{1,0:T(8,128)(2,1)S(1)}, bf16[128,128]{1,0:T(8,128)(2,1)S(1)}, u32[]{:S(2)}, u32[]{:S(2)}) collective-permute-start(bf16[128,128]{1,0:T(8,128)(2,1)S(1)} %get-tuple-element.81.refs_6_.refs_10_.refs_11_), channel_id=1, source_target_pairs={{0,2},{1,3},{2,0},{3,1},{4,6},{5,7},{6,4},{7,5},{8,10},{9,11},{10,... | collective-permute-start | bytes 98312 | tf_op jit(solution)/shard_map/ppermute | solution.py:164
  48.0 3.7 %collective-permute-start.9 = (bf16[128,128]{1,0:T(8,128)(2,1)S(1)}, bf16[128,128]{1,0:T(8,128)(2,1)S(1)}, u32[]{:S(2)}, u32[]{:S(2)}) collective-permute-start(bf16[128,128]{1,0:T(8,128)(2,1)S(1)} %get-tuple-element.81.refs_6_.refs_10_.refs_11_), channel_id=1, source_target_pairs={{0,1},{1,0},{2,3},{3,2},{4,5},{5,4},{6,7},{7,6},{8,9},{9,8},{10,11... | collective-permute-start | bytes 98312 | tf_op jit(solution)/shard_map/ppermute | solution.py:164
  55.6 10.8 %all-to-all-start.4 = ((bf16[32,16,128]{2,1,0:T(8,128)(2,1)}), bf16[32,16,128]{2,1,0:T(8,128)(2,1)S(1)}, u32[]{:S(2)}, u32[]{:S(2)}) async-start(bf16[32,16,128]{2,1,0:T(8,128)(2,1)} %get-tuple-element.87), calls=%async_computation.4 | async-start | bytes 262144 | tf_op jit(solution)/shard_map/all_to_all | solution.py:168
  58.2 3.5 %collective-permute-start.14 = (bf16[128,128]{1,0:T(8,128)(2,1)S(1)}, bf16[128,128]{1,0:T(8,128)(2,1)S(1)}, u32[]{:S(2)}, u32[]{:S(2)}) collective-permute-start(bf16[128,128]{1,0:T(8,128)(2,1)S(1)} %get-tuple-element.88.refs_6_.refs_10_), channel_id=1, source_target_pairs={{0,3},{1,2},{2,1},{3,0},{4,7},{5,6},{6,5},{7,4},{8,11},{9,10},{10,... | collective-permute-start | bytes 98312 | tf_op jit(solution)/shard_map/ppermute | solution.py:164
  59.6 4.1 %collective-permute-start.13 = (bf16[128,128]{1,0:T(8,128)(2,1)S(1)}, bf16[128,128]{1,0:T(8,128)(2,1)S(1)}, u32[]{:S(2)}, u32[]{:S(2)}) collective-permute-start(bf16[128,128]{1,0:T(8,128)(2,1)S(1)} %get-tuple-element.88.refs_6_.refs_10_), channel_id=1, source_target_pairs={{0,2},{1,3},{2,0},{3,1},{4,6},{5,7},{6,4},{7,5},{8,10},{9,11},{10,... | collective-permute-start | bytes 98312 | tf_op jit(solution)/shard_map/ppermute | solution.py:164
  60.0 3.7 %collective-permute-start.12 = (bf16[128,128]{1,0:T(8,128)(2,1)S(1)}, bf16[128,128]{1,0:T(8,128)(2,1)S(1)}, u32[]{:S(2)}, u32[]{:S(2)}) collective-permute-start(bf16[128,128]{1,0:T(8,128)(2,1)S(1)} %get-tuple-element.88.refs_6_.refs_10_), channel_id=1, source_target_pairs={{0,1},{1,0},{2,3},{3,2},{4,5},{5,4},{6,7},{7,6},{8,9},{9,8},{10,11... | collective-permute-start | bytes 98312 | tf_op jit(solution)/shard_map/ppermute | solution.py:164
  67.6 10.8 %all-to-all-start.5 = ((bf16[32,16,128]{2,1,0:T(8,128)(2,1)}), bf16[32,16,128]{2,1,0:T(8,128)(2,1)S(1)}, u32[]{:S(2)}, u32[]{:S(2)}) async-start(bf16[32,16,128]{2,1,0:T(8,128)(2,1)} %get-tuple-element.94), calls=%async_computation.5 | async-start | bytes 262144 | tf_op jit(solution)/shard_map/all_to_all | solution.py:168
  70.1 3.5 %collective-permute-start.17 = (bf16[128,128]{1,0:T(8,128)(2,1)S(1)}, bf16[128,128]{1,0:T(8,128)(2,1)S(1)}, u32[]{:S(2)}, u32[]{:S(2)}) collective-permute-start(bf16[128,128]{1,0:T(8,128)(2,1)S(1)} %get-tuple-element.95.refs_6_), channel_id=1, source_target_pairs={{0,3},{1,2},{2,1},{3,0},{4,7},{5,6},{6,5},{7,4},{8,11},{9,10},{10,... | collective-permute-start | bytes 98312 | tf_op jit(solution)/shard_map/ppermute | solution.py:164
  71.6 4.1 %collective-permute-start.16 = (bf16[128,128]{1,0:T(8,128)(2,1)S(1)}, bf16[128,128]{1,0:T(8,128)(2,1)S(1)}, u32[]{:S(2)}, u32[]{:S(2)}) collective-permute-start(bf16[128,128]{1,0:T(8,128)(2,1)S(1)} %get-tuple-element.95.refs_6_), channel_id=1, source_target_pairs={{0,2},{1,3},{2,0},{3,1},{4,6},{5,7},{6,4},{7,5},{8,10},{9,11},{10,... | collective-permute-start | bytes 98312 | tf_op jit(solution)/shard_map/ppermute | solution.py:164
  71.9 3.7 %collective-permute-start.15 = (bf16[128,128]{1,0:T(8,128)(2,1)S(1)}, bf16[128,128]{1,0:T(8,128)(2,1)S(1)}, u32[]{:S(2)}, u32[]{:S(2)}) collective-permute-start(bf16[128,128]{1,0:T(8,128)(2,1)S(1)} %get-tuple-element.95.refs_6_), channel_id=1, source_target_pairs={{0,1},{1,0},{2,3},{3,2},{4,5},{5,4},{6,7},{7,6},{8,9},{9,8},{10,11... | collective-permute-start | bytes 98312 | tf_op jit(solution)/shard_map/ppermute | solution.py:164

commit v3 on v2

--- a/solution.py
+++ b/solution.py
@@ -9,7 +9,7 @@
 from jax.sharding import PartitionSpec as P
 
 STEPS = 6
-SLOT = 16
+PAIR = 2
 TERMS = 3
 F32, BF16 = jnp.float32, jnp.bfloat16
 VMEM = pl.BlockSpec(memory_space=pltpu.VMEM)
@@ -34,9 +34,19 @@
 
 
 def send(picked, out_ref, group):
-    for area in range(out_ref.shape[0] // group):
-        for member in range(group):
-            out_ref[area * group + member] = picked[area * SLOT : (area + 1) * SLOT]
+    stimuli = picked.shape[1]
+    areas = out_ref.shape[0] // group
+    for tile in range(out_ref.shape[2] // stimuli):
+        for area in range(areas):
+            start = (tile * areas + area) * PAIR
+            for member in range(group):
+                spot = (area * group + member, slice(None), slice(tile * stimuli, (tile + 1) * stimuli))
+                out_ref[spot] = picked[start : start + PAIR]
+
+
+def rows_from(chunks, stimuli):
+    tiles = [chunks[:, :, start : start + stimuli] for start in range(0, chunks.shape[2], stimuli)]
+    return jnp.concatenate([tile.reshape(-1, stimuli) for tile in tiles], axis=0)
 
 
 def pack_kernel(group, senders, *refs):
@@ -60,16 +70,21 @@
         past[age][...] = (history[age] * active).astype(BF16)
     rate[...] = jnp.broadcast_to(active * column(leak[...]), rate.shape)
 
-    lines = jnp.concatenate(
-        [table[...].astype(F32), jnp.zeros((areas, SLOT - senders), F32)], axis=1
-    )
-    real = iota((SLOT, 1), 0) < senders
+    tiles = -(-senders // PAIR)
+    wide = (areas * PAIR, areas)
+    mine = iota(wide, 1) == iota(wide, 0) // PAIR
+    spread = jnp.dot(
+        mine.astype(F32).astype(BF16), table[...].astype(F32).astype(BF16), preferred_element_type=F32
+    )
+    delay = jnp.broadcast_to(lags[...].astype(F32) - 1.0, wide)
+    age = jnp.sum(jnp.where(mine, delay, 0.0), axis=1, keepdims=True)
+    half = iota((areas * PAIR, 1), 0) % PAIR
     places = []
-    for area in range(areas):
-        age = lags[0:1, area : area + 1].astype(F32) - 1.0
-        age = jnp.where(real, jnp.broadcast_to(age, real.shape), float(depth))
-        places.append(column(lines[area : area + 1]) + age * block)
-    lanes = iota((areas * SLOT, depth * block), 1).astype(F32)
+    for tile in range(tiles):
+        sender = half * tiles + tile
+        row = jnp.sum(jnp.where(iota(spread.shape, 1) == sender, spread, 0.0), axis=1, keepdims=True)
+        places.append(row + jnp.where(sender < senders, age, float(depth)) * block)
+    lanes = iota(choice.shape, 1).astype(F32)
     choice[...] = (lanes == jnp.concatenate(places, axis=0)).astype(F32).astype(BF16)
     recent = jnp.concatenate([ref[...] for ref in past], axis=0)
     send(jnp.dot(choice[...], recent, preferred_element_type=F32).astype(BF16), outgoing, group)
@@ -77,17 +92,23 @@
     near = w_local.shape[1]
     for term, values in enumerate(terms_of(w_local[...])):
         weights[term * block : (term + 1) * block, :near] = values
-    blank = jnp.zeros((SLOT - senders, block), F32)
+    chunks = areas * group
+    far = tiles * chunks * PAIR
+    last = (tiles - 1) * chunks * PAIR
+    padded[last:, :] = jnp.zeros((padded.shape[0] - last, block), F32)
     for area in range(areas):
         for member in range(group):
-            spot = (area * group + member) * SLOT
-            piece = w_long[member, area * senders : (area + 1) * senders, :]
-            padded[spot : spot + SLOT, :] = jnp.concatenate([piece, blank], axis=0)
+            for side in range(PAIR):
+                first = side * tiles
+                count = min(tiles, senders - first)
+                rows = pl.ds((area * group + member) * PAIR + side, count, stride=chunks * PAIR)
+                padded[rows, :] = w_long[member, pl.ds(area * senders + first, count), :]
     for part in range(padded.shape[0] // block):
         tile = padded[part * block : (part + 1) * block, :].T
+        width = min(block, far - part * block)
         for term, values in enumerate(terms_of(tile)):
             spot = near + part * block
-            weights[term * block : (term + 1) * block, spot : spot + block] = values
+            weights[term * block : (term + 1) * block, spot : spot + width] = values[:, :width]
 
 
 def step_kernel(group, depth, last, *refs):
@@ -101,7 +122,8 @@
         start = pl.multiple_of((me ^ slot) * block, block)
         current[pl.ds(start, block), :] = mates[slot][...]
     total = jnp.dot(weights[:, :near], current[...], preferred_element_type=F32)
-    total += jnp.dot(weights[:, near:], received[...], preferred_element_type=F32)
+    sent = rows_from(received[...], state.shape[1])
+    total += jnp.dot(weights[:, near:], sent, preferred_element_type=F32)
     parts = [total[term * block : (term + 1) * block] for term in range(TERMS)]
     inputs = functools.reduce(lambda a, b: a + b, reversed(parts)) + drive[...]
     old = state[...]
@@ -132,10 +154,11 @@
 def local(group, history, drive, leak, w_local, w_long, sender_rows, delays, area_sizes):
     depth, block, stimuli = history.shape
     areas, senders = sender_rows.shape[1:]
-    near, far = group * block, areas * group * SLOT
+    tiles = -(-senders // PAIR)
+    near, far = group * block, areas * group * tiles * PAIR
     shape = jax.ShapeDtypeStruct
     tile = lambda kind: shape((block, stimuli), kind)
-    sent = shape((areas * group, SLOT, stimuli), BF16)
+    sent = shape((areas * group, PAIR, tiles * stimuli), BF16)
     given = [
         history,
         leak.reshape(1, block),
@@ -152,13 +175,13 @@
             shape((TERMS * block, near + far), BF16),
             tile(F32),
             tile(F32),
-            shape((areas * SLOT, depth * block), BF16),
+            shape((areas * tiles * PAIR, depth * block), BF16),
             sent,
             *[tile(BF16)] * depth,
         ],
         [stay(v) for v in given],
         [pltpu.VMEM(v.shape, v.dtype) for v in given]
-        + [pltpu.VMEM((far, block), F32), pltpu.SemaphoreType.DMA((len(given),))],
+        + [pltpu.VMEM((far + -far % block, block), F32), pltpu.SemaphoreType.DMA((len(given),))],
         in_specs=[pl.BlockSpec(memory_space=pl.ANY)] * len(given),
     )
     swap = lambda v, bits: lax.ppermute(v, "nrn", [(i, i ^ bits) for i in range(group)])
@@ -170,7 +193,7 @@
         result = call(
             functools.partial(step_kernel, group, depth, final),
             [tile(F32)] if final else [tile(F32), tile(BF16), sent],
-            [weights, received.reshape(far, stimuli), state, drive, rate, choice, past[0], *mates, *past[1:]],
+            [weights, received, state, drive, rate, choice, past[0], *mates, *past[1:]],
             [pltpu.VMEM((near, stimuli), BF16)],
         )
         if final:

time: 79.8 us -> 77.3 us (0.969)
  waiting for transfers between devices: 37.6 us -> 33.7 us
  starting transfers between devices: 31.7 us -> 32.9 us
    all_to_all x6, waiting for transfers between devices: 16 us -> 12 us  [local(): lax.all_to_all(outgoing, ('area', 'nrn'), split_axis=0, concat_axis=0, ti...]
    all_to_all x6, starting transfers between devices: 20.1 us -> 21.2 us  [local(): lax.all_to_all(outgoing, ('area', 'nrn'), split_axis=0, concat_axis=0, ti...]
where the time goes in v3:
time: 77.3 us; the launch traced here: 76.9 us
  waiting for transfers between devices  33.7 us (44%)
  starting transfers between devices  32.9 us (43%)
  Pallas kernels  9.46 us (12%)
    ppermute x18, waiting for transfers between devices, local(): lax.ppermute(v, 'nrn', [(i, i ^ bits) for i in range(group)])  21.8 us
    all_to_all x6, starting transfers between devices, local(): lax.all_to_all(outgoing, ('area', 'nrn'), split_axis=0, concat_axis=0, ti...  21.2 us
    all_to_all x6, waiting for transfers between devices, local(): lax.all_to_all(outgoing, ('area', 'nrn'), split_axis=0, concat_axis=0, ti...  12 us
    ppermute x18, starting transfers between devices, local(): lax.ppermute(v, 'nrn', [(i, i ^ bits) for i in range(group)])  11.7 us
    pallas_call x7, Pallas kernels, call(): pl.pallas_call(kernel, out_shape=out_shape, out_specs=[VMEM] * len(out_sh...  9.46 us
  transfers between devices with their start and end apart: 24, of which 18 were waited for; matrix products, arithmetic and copies ran while one was open for 0% of the time, Pallas kernels for 0%

profile of v3, /device:TPU:0, one launch (start us, length us, event | category | flops | bytes accessed | tf_op | source)
XLA Modules:
  0.0 76.9 jit_solution(1566021014332310844)
XLA Ops:
  0.7 2.4 %shard_map.82 = (bf16[384,832]{1,0:T(8,128)(2,1)S(1)}, f32[128,128]{1,0:T(8,128)S(1)}, f32[128,128]{1,0:T(8,128)S(1)}, bf16[80,512]{1,0:T(8,128)(2,1)S(1)}, bf16...) custom-call(f32[4,128,128]{2,1,0:T(8,128)} %refs_0_.1, ...), custom_call_target="tpu_custom_call" | custom-call | tf_op jit(solution)/shard_map/pallas_call | solution.py:144
  3.0 0.0 copy-start
  3.0 7.3 %all-to-all-start = ((bf16[32,2,640]{2,1,0:T(2,128)(2,1)}), bf16[32,2,640]{2,1,0:T(2,128)(2,1)S(1)}, u32[]{:S(2)}, u32[]{:S(2)}) async-start(bf16[32,2,640]{2,1,0:T(2,128)(2,1)} %get-tuple-element.54), calls=%async_computation | async-start | bytes 163840 | tf_op jit(solution)/shard_map/all_to_all | solution.py:191
  10.4 1.6 %collective-permute-start.2 = (bf16[128,128]{1,0:T(8,128)(2,1)S(1)}, bf16[128,128]{1,0:T(8,128)(2,1)S(1)}, u32[]{:S(2)}, u32[]{:S(2)}) collective-permute-start(bf16[128,128]{1,0:T(8,128)(2,1)S(1)} %get-tuple-element.55.refs_6_.refs_10_.refs_11_.refs_12_), channel_id=1, source_target_pairs={{0,3},{1,2},{2,1},{3,0},{4,7},{5,6},{6,5},{7,4},{8,11},{9,10},{10,... | collective-permute-start | bytes 98312 | tf_op jit(solution)/shard_map/ppermute | solution.py:187
  11.9 0.4 collective-permute-start.1
  12.3 0.0 collective-permute-start
  12.3 1.5 %collective-permute-done.2.refs_9_ = bf16[128,128]{1,0:T(8,128)(2,1)S(1)} collective-permute-done((bf16[128,128]{1,0:T(8,128)(2,1)S(1)}, bf16[128,128]{1,0:T(8,128)(2,1)S(1)}, u32[]{:S(2)}, u32[]{:S(2)}) %collective-permute-start.2) | collective-permute-done | bytes 32800 | tf_op jit(solution)/shard_map/ppermute | solution.py:187
  13.8 2.2 %collective-permute-done.1.refs_8_ = bf16[128,128]{1,0:T(8,128)(2,1)S(1)} collective-permute-done((bf16[128,128]{1,0:T(8,128)(2,1)S(1)}, bf16[128,128]{1,0:T(8,128)(2,1)S(1)}, u32[]{:S(2)}, u32[]{:S(2)}) %collective-permute-start.1) | collective-permute-done | bytes 32800 | tf_op jit(solution)/shard_map/ppermute | solution.py:187
  16.0 0.0 collective-permute-done.refs_7_
  16.0 2.0 %all-to-all-done.refs_1_ = bf16[32,2,640]{2,1,0:T(2,128)(2,1)S(1)} async-done(((bf16[32,2,640]{2,1,0:T(2,128)(2,1)}), bf16[32,2,640]{2,1,0:T(2,128)(2,1)S(1)}, u32[]{:S(2)}, u32[]{:S(2)}) %all-to-all-start) | async-done | bytes 81952 | tf_op jit(solution)/shard_map/all_to_all | solution.py:191
  18.0 0.0 copy-done
  18.0 1.2 %shard_map.83 = (f32[128,128]{1,0:T(8,128)S(1)}, bf16[128,128]{1,0:T(8,128)(2,1)S(1)}, bf16[32,2,640]{2,1,0:T(2,128)(2,1)}) custom-call(bf16[384,832]{1,0:T(8,128)(2,1)S(1)} %get-tuple-element.53.refs_0_, bf16[32,2,640]{2,1,0:T(2,128)(2,1)S(1)} %all-to-all-done.refs_1_, f32[128,128]{1,0:T(8,128)S(1)} %get-tuple-element.57.refs_2_, f32[128,128]{1,0:T(8,128)S(1)} %copy-done, ...), custom_call_target="tpu_custom_call" | custom-call | tf_op jit(solution)/shard_map/pallas_call | solution.py:144
  19.2 2.8 %all-to-all-start.1 = ((bf16[32,2,640]{2,1,0:T(2,128)(2,1)}), bf16[32,2,640]{2,1,0:T(2,128)(2,1)S(1)}, u32[]{:S(2)}, u32[]{:S(2)}) async-start(bf16[32,2,640]{2,1,0:T(2,128)(2,1)} %get-tuple-element.66), calls=%async_computation.1 | async-start | bytes 163840 | tf_op jit(solution)/shard_map/all_to_all | solution.py:191
  22.0 1.6 %collective-permute-start.5 = (bf16[128,128]{1,0:T(8,128)(2,1)S(1)}, bf16[128,128]{1,0:T(8,128)(2,1)S(1)}, u32[]{:S(2)}, u32[]{:S(2)}) collective-permute-start(bf16[128,128]{1,0:T(8,128)(2,1)S(1)} %get-tuple-element.67.refs_6_.refs_10_.refs_11_.refs_12_), channel_id=1, source_target_pairs={{0,3},{1,2},{2,1},{3,0},{4,7},{5,6},{6,5},{7,4},{8,11},{9,10},{10,... | collective-permute-start | bytes 98312 | tf_op jit(solution)/shard_map/ppermute | solution.py:187
  23.5 0.4 collective-permute-start.4
  23.9 0.0 collective-permute-start.3
  23.9 1.5 %collective-permute-done.5.refs_9_ = bf16[128,128]{1,0:T(8,128)(2,1)S(1)} collective-permute-done((bf16[128,128]{1,0:T(8,128)(2,1)S(1)}, bf16[128,128]{1,0:T(8,128)(2,1)S(1)}, u32[]{:S(2)}, u32[]{:S(2)}) %collective-permute-start.5) | collective-permute-done | bytes 32800 | tf_op jit(solution)/shard_map/ppermute | solution.py:187
  25.4 2.2 %collective-permute-done.4.refs_8_ = bf16[128,128]{1,0:T(8,128)(2,1)S(1)} collective-permute-done((bf16[128,128]{1,0:T(8,128)(2,1)S(1)}, bf16[128,128]{1,0:T(8,128)(2,1)S(1)}, u32[]{:S(2)}, u32[]{:S(2)}) %collective-permute-start.4) | collective-permute-done | bytes 32800 | tf_op jit(solution)/shard_map/ppermute | solution.py:187
  27.5 0.0 collective-permute-done.3.refs_7_
  27.6 2.0 %all-to-all-done.1.refs_1_ = bf16[32,2,640]{2,1,0:T(2,128)(2,1)S(1)} async-done(((bf16[32,2,640]{2,1,0:T(2,128)(2,1)}), bf16[32,2,640]{2,1,0:T(2,128)(2,1)S(1)}, u32[]{:S(2)}, u32[]{:S(2)}) %all-to-all-start.1) | async-done | bytes 81952 | tf_op jit(solution)/shard_map/all_to_all | solution.py:191
  29.5 1.2 %shard_map.84 = (f32[128,128]{1,0:T(8,128)S(1)}, bf16[128,128]{1,0:T(8,128)(2,1)S(1)}, bf16[32,2,640]{2,1,0:T(2,128)(2,1)}) custom-call(bf16[384,832]{1,0:T(8,128)(2,1)S(1)} %get-tuple-element.53.refs_0_, bf16[32,2,640]{2,1,0:T(2,128)(2,1)S(1)} %all-to-all-done.1.refs_1_, f32[128,128]{1,0:T(8,128)S(1)} %get-tuple-element.69.refs_2_, f32[128,128]{1,0:T(8,128)S(1)} %copy-done, ...), custom_call_target="tpu_custom_call" | custom-call | tf_op jit(solution)/shard_map/pallas_call | solution.py:144
  30.8 2.8 %all-to-all-start.2 = ((bf16[32,2,640]{2,1,0:T(2,128)(2,1)}), bf16[32,2,640]{2,1,0:T(2,128)(2,1)S(1)}, u32[]{:S(2)}, u32[]{:S(2)}) async-start(bf16[32,2,640]{2,1,0:T(2,128)(2,1)} %get-tuple-element.73), calls=%async_computation.2 | async-start | bytes 163840 | tf_op jit(solution)/shard_map/all_to_all | solution.py:191
  33.6 1.6 %collective-permute-start.8 = (bf16[128,128]{1,0:T(8,128)(2,1)S(1)}, bf16[128,128]{1,0:T(8,128)(2,1)S(1)}, u32[]{:S(2)}, u32[]{:S(2)}) collective-permute-start(bf16[128,128]{1,0:T(8,128)(2,1)S(1)} %get-tuple-element.74.refs_6_.refs_10_.refs_11_.refs_12_), channel_id=1, source_target_pairs={{0,3},{1,2},{2,1},{3,0},{4,7},{5,6},{6,5},{7,4},{8,11},{9,10},{10,... | collective-permute-start | bytes 98312 | tf_op jit(solution)/shard_map/ppermute | solution.py:187
  35.1 0.4 collective-permute-start.7
  35.5 0.0 collective-permute-start.6
  35.5 1.5 %collective-permute-done.8.refs_9_ = bf16[128,128]{1,0:T(8,128)(2,1)S(1)} collective-permute-done((bf16[128,128]{1,0:T(8,128)(2,1)S(1)}, bf16[128,128]{1,0:T(8,128)(2,1)S(1)}, u32[]{:S(2)}, u32[]{:S(2)}) %collective-permute-start.8) | collective-permute-done | bytes 32800 | tf_op jit(solution)/shard_map/ppermute | solution.py:187
  37.0 2.2 %collective-permute-done.7.refs_8_ = bf16[128,128]{1,0:T(8,128)(2,1)S(1)} collective-permute-done((bf16[128,128]{1,0:T(8,128)(2,1)S(1)}, bf16[128,128]{1,0:T(8,128)(2,1)S(1)}, u32[]{:S(2)}, u32[]{:S(2)}) %collective-permute-start.7) | collective-permute-done | bytes 32800 | tf_op jit(solution)/shard_map/ppermute | solution.py:187
  39.1 0.0 collective-permute-done.6.refs_7_
  39.1 2.0 %all-to-all-done.2.refs_1_ = bf16[32,2,640]{2,1,0:T(2,128)(2,1)S(1)} async-done(((bf16[32,2,640]{2,1,0:T(2,128)(2,1)}), bf16[32,2,640]{2,1,0:T(2,128)(2,1)S(1)}, u32[]{:S(2)}, u32[]{:S(2)}) %all-to-all-start.2) | async-done | bytes 81952 | tf_op jit(solution)/shard_map/all_to_all | solution.py:191
  41.1 1.2 %shard_map.85 = (f32[128,128]{1,0:T(8,128)S(1)}, bf16[128,128]{1,0:T(8,128)(2,1)S(1)}, bf16[32,2,640]{2,1,0:T(2,128)(2,1)}) custom-call(bf16[384,832]{1,0:T(8,128)(2,1)S(1)} %get-tuple-element.53.refs_0_, bf16[32,2,640]{2,1,0:T(2,128)(2,1)S(1)} %all-to-all-done.2.refs_1_, f32[128,128]{1,0:T(8,128)S(1)} %get-tuple-element.76.refs_2_, f32[128,128]{1,0:T(8,128)S(1)} %copy-done, ...), custom_call_target="tpu_custom_call" | custom-call | tf_op jit(solution)/shard_map/pallas_call | solution.py:144
  42.4 2.8 %all-to-all-start.3 = ((bf16[32,2,640]{2,1,0:T(2,128)(2,1)}), bf16[32,2,640]{2,1,0:T(2,128)(2,1)S(1)}, u32[]{:S(2)}, u32[]{:S(2)}) async-start(bf16[32,2,640]{2,1,0:T(2,128)(2,1)} %get-tuple-element.80), calls=%async_computation.3 | async-start | bytes 163840 | tf_op jit(solution)/shard_map/all_to_all | solution.py:191
  45.1 1.6 %collective-permute-start.11 = (bf16[128,128]{1,0:T(8,128)(2,1)S(1)}, bf16[128,128]{1,0:T(8,128)(2,1)S(1)}, u32[]{:S(2)}, u32[]{:S(2)}) collective-permute-start(bf16[128,128]{1,0:T(8,128)(2,1)S(1)} %get-tuple-element.81.refs_6_.refs_10_.refs_11_), channel_id=1, source_target_pairs={{0,3},{1,2},{2,1},{3,0},{4,7},{5,6},{6,5},{7,4},{8,11},{9,10},{10,... | collective-permute-start | bytes 98312 | tf_op jit(solution)/shard_map/ppermute | solution.py:187
  46.7 0.4 collective-permute-start.10
  47.1 0.0 collective-permute-start.9
  47.1 1.5 %collective-permute-done.11.refs_9_ = bf16[128,128]{1,0:T(8,128)(2,1)S(1)} collective-permute-done((bf16[128,128]{1,0:T(8,128)(2,1)S(1)}, bf16[128,128]{1,0:T(8,128)(2,1)S(1)}, u32[]{:S(2)}, u32[]{:S(2)}) %collective-permute-start.11) | collective-permute-done | bytes 32800 | tf_op jit(solution)/shard_map/ppermute | solution.py:187
  48.5 2.2 %collective-permute-done.10.refs_8_ = bf16[128,128]{1,0:T(8,128)(2,1)S(1)} collective-permute-done((bf16[128,128]{1,0:T(8,128)(2,1)S(1)}, bf16[128,128]{1,0:T(8,128)(2,1)S(1)}, u32[]{:S(2)}, u32[]{:S(2)}) %collective-permute-start.10) | collective-permute-done | bytes 32800 | tf_op jit(solution)/shard_map/ppermute | solution.py:187
  50.7 0.0 collective-permute-done.9.refs_7_
  50.7 2.0 %all-to-all-done.3.refs_1_ = bf16[32,2,640]{2,1,0:T(2,128)(2,1)S(1)} async-done(((bf16[32,2,640]{2,1,0:T(2,128)(2,1)}), bf16[32,2,640]{2,1,0:T(2,128)(2,1)S(1)}, u32[]{:S(2)}, u32[]{:S(2)}) %all-to-all-start.3) | async-done | bytes 81952 | tf_op jit(solution)/shard_map/all_to_all | solution.py:191
  52.7 1.2 %shard_map.86 = (f32[128,128]{1,0:T(8,128)S(1)}, bf16[128,128]{1,0:T(8,128)(2,1)S(1)}, bf16[32,2,640]{2,1,0:T(2,128)(2,1)}) custom-call(bf16[384,832]{1,0:T(8,128)(2,1)S(1)} %get-tuple-element.53.refs_0_, bf16[32,2,640]{2,1,0:T(2,128)(2,1)S(1)} %all-to-all-done.3.refs_1_, f32[128,128]{1,0:T(8,128)S(1)} %get-tuple-element.83.refs_2_, f32[128,128]{1,0:T(8,128)S(1)} %copy-done, ...), custom_call_target="tpu_custom_call" | custom-call | tf_op jit(solution)/shard_map/pallas_call | solution.py:144
  53.9 2.8 %all-to-all-start.4 = ((bf16[32,2,640]{2,1,0:T(2,128)(2,1)}), bf16[32,2,640]{2,1,0:T(2,128)(2,1)S(1)}, u32[]{:S(2)}, u32[]{:S(2)}) async-start(bf16[32,2,640]{2,1,0:T(2,128)(2,1)} %get-tuple-element.87), calls=%async_computation.4 | async-start | bytes 163840 | tf_op jit(solution)/shard_map/all_to_all | solution.py:191
  56.7 1.6 %collective-permute-start.14 = (bf16[128,128]{1,0:T(8,128)(2,1)S(1)}, bf16[128,128]{1,0:T(8,128)(2,1)S(1)}, u32[]{:S(2)}, u32[]{:S(2)}) collective-permute-start(bf16[128,128]{1,0:T(8,128)(2,1)S(1)} %get-tuple-element.88.refs_6_.refs_10_), channel_id=1, source_target_pairs={{0,3},{1,2},{2,1},{3,0},{4,7},{5,6},{6,5},{7,4},{8,11},{9,10},{10,... | collective-permute-start | bytes 98312 | tf_op jit(solution)/shard_map/ppermute | solution.py:187
  58.3 0.4 collective-permute-start.13
  58.7 0.0 collective-permute-start.12
  58.7 1.5 %collective-permute-done.14.refs_9_ = bf16[128,128]{1,0:T(8,128)(2,1)S(1)} collective-permute-done((bf16[128,128]{1,0:T(8,128)(2,1)S(1)}, bf16[128,128]{1,0:T(8,128)(2,1)S(1)}, u32[]{:S(2)}, u32[]{:S(2)}) %collective-permute-start.14) | collective-permute-done | bytes 32800 | tf_op jit(solution)/shard_map/ppermute | solution.py:187
  60.1 2.2 %collective-permute-done.13.refs_8_ = bf16[128,128]{1,0:T(8,128)(2,1)S(1)} collective-permute-done((bf16[128,128]{1,0:T(8,128)(2,1)S(1)}, bf16[128,128]{1,0:T(8,128)(2,1)S(1)}, u32[]{:S(2)}, u32[]{:S(2)}) %collective-permute-start.13) | collective-permute-done | bytes 32800 | tf_op jit(solution)/shard_map/ppermute | solution.py:187
  62.3 0.0 collective-permute-done.12.refs_7_
  62.3 2.0 %all-to-all-done.4.refs_1_ = bf16[32,2,640]{2,1,0:T(2,128)(2,1)S(1)} async-done(((bf16[32,2,640]{2,1,0:T(2,128)(2,1)}), bf16[32,2,640]{2,1,0:T(2,128)(2,1)S(1)}, u32[]{:S(2)}, u32[]{:S(2)}) %all-to-all-start.4) | async-done | bytes 81952 | tf_op jit(solution)/shard_map/all_to_all | solution.py:191
  64.3 1.2 %shard_map.87 = (f32[128,128]{1,0:T(8,128)S(1)}, bf16[128,128]{1,0:T(8,128)(2,1)S(1)}, bf16[32,2,640]{2,1,0:T(2,128)(2,1)}) custom-call(bf16[384,832]{1,0:T(8,128)(2,1)S(1)} %get-tuple-element.53.refs_0_, bf16[32,2,640]{2,1,0:T(2,128)(2,1)S(1)} %all-to-all-done.4.refs_1_, f32[128,128]{1,0:T(8,128)S(1)} %get-tuple-element.90.refs_2_, f32[128,128]{1,0:T(8,128)S(1)} %copy-done, ...), custom_call_target="tpu_custom_call" | custom-call | tf_op jit(solution)/shard_map/pallas_call | solution.py:144
  65.5 2.8 %all-to-all-start.5 = ((bf16[32,2,640]{2,1,0:T(2,128)(2,1)}), bf16[32,2,640]{2,1,0:T(2,128)(2,1)S(1)}, u32[]{:S(2)}, u32[]{:S(2)}) async-start(bf16[32,2,640]{2,1,0:T(2,128)(2,1)} %get-tuple-element.94), calls=%async_computation.5 | async-start | bytes 163840 | tf_op jit(solution)/shard_map/all_to_all | solution.py:191
  68.3 1.6 %collective-permute-start.17 = (bf16[128,128]{1,0:T(8,128)(2,1)S(1)}, bf16[128,128]{1,0:T(8,128)(2,1)S(1)}, u32[]{:S(2)}, u32[]{:S(2)}) collective-permute-start(bf16[128,128]{1,0:T(8,128)(2,1)S(1)} %get-tuple-element.95.refs_6_), channel_id=1, source_target_pairs={{0,3},{1,2},{2,1},{3,0},{4,7},{5,6},{6,5},{7,4},{8,11},{9,10},{10,... | collective-permute-start | bytes 98312 | tf_op jit(solution)/shard_map/ppermute | solution.py:187
  69.9 0.4 collective-permute-start.16
  70.3 0.0 collective-permute-start.15
  70.3 1.5 %collective-permute-done.17.refs_9_ = bf16[128,128]{1,0:T(8,128)(2,1)S(1)} collective-permute-done((bf16[128,128]{1,0:T(8,128)(2,1)S(1)}, bf16[128,128]{1,0:T(8,128)(2,1)S(1)}, u32[]{:S(2)}, u32[]{:S(2)}) %collective-permute-start.17) | collective-permute-done | bytes 32800 | tf_op jit(solution)/shard_map/ppermute | solution.py:187
  71.7 2.2 %collective-permute-done.16.refs_8_ = bf16[128,128]{1,0:T(8,128)(2,1)S(1)} collective-permute-done((bf16[128,128]{1,0:T(8,128)(2,1)S(1)}, bf16[128,128]{1,0:T(8,128)(2,1)S(1)}, u32[]{:S(2)}, u32[]{:S(2)}) %collective-permute-start.16) | collective-permute-done | bytes 32800 | tf_op jit(solution)/shard_map/ppermute | solution.py:187
  73.9 0.0 collective-permute-done.15.refs_7_
  73.9 2.0 %all-to-all-done.5.refs_1_ = bf16[32,2,640]{2,1,0:T(2,128)(2,1)S(1)} async-done(((bf16[32,2,640]{2,1,0:T(2,128)(2,1)}), bf16[32,2,640]{2,1,0:T(2,128)(2,1)S(1)}, u32[]{:S(2)}, u32[]{:S(2)}) %all-to-all-start.5) | async-done | bytes 81952 | tf_op jit(solution)/shard_map/all_to_all | solution.py:191
  75.9 1.0 %shard_map.88 = f32[128,128]{1,0:T(8,128)} custom-call(bf16[384,832]{1,0:T(8,128)(2,1)S(1)} %get-tuple-element.53.refs_0_, bf16[32,2,640]{2,1,0:T(2,128)(2,1)S(1)} %all-to-all-done.5.refs_1_, f32[128,128]{1,0:T(8,128)S(1)} %get-tuple-element.97.refs_2_, f32[128,128]{1,0:T(8,128)S(1)} %copy-done, f32[128,128]{1,0:T(8,128)S(1)} %get-tuple-element.58.refs_4_, ...), custom_call_target="tpu_custom_call" | custom-call | tf_op jit(solution)/shard_map/pallas_call | solution.py:144
Async XLA Ops:
  3.0 14.9 %copy-start = (f32[128,128]{1,0:T(8,128)S(1)}, f32[128,128]{1,0:T(8,128)}, u32[]{:S(2)}) copy-start(f32[128,128]{1,0:T(8,128)} %refs_3_.11) | copy-start | bytes 196612
  3.0 14.9 %all-to-all-start = ((bf16[32,2,640]{2,1,0:T(2,128)(2,1)}), bf16[32,2,640]{2,1,0:T(2,128)(2,1)S(1)}, u32[]{:S(2)}, u32[]{:S(2)}) async-start(bf16[32,2,640]{2,1,0:T(2,128)(2,1)} %get-tuple-element.54), calls=%async_computation | async-start | bytes 163840 | tf_op jit(solution)/shard_map/all_to_all | solution.py:191
  10.4 3.4 %collective-permute-start.2 = (bf16[128,128]{1,0:T(8,128)(2,1)S(1)}, bf16[128,128]{1,0:T(8,128)(2,1)S(1)}, u32[]{:S(2)}, u32[]{:S(2)}) collective-permute-start(bf16[128,128]{1,0:T(8,128)(2,1)S(1)} %get-tuple-element.55.refs_6_.refs_10_.refs_11_.refs_12_), channel_id=1, source_target_pairs={{0,3},{1,2},{2,1},{3,0},{4,7},{5,6},{6,5},{7,4},{8,11},{9,10},{10,... | collective-permute-start | bytes 98312 | tf_op jit(solution)/shard_map/ppermute | solution.py:187
  11.9 4.0 %collective-permute-start.1 = (bf16[128,128]{1,0:T(8,128)(2,1)S(1)}, bf16[128,128]{1,0:T(8,128)(2,1)S(1)}, u32[]{:S(2)}, u32[]{:S(2)}) collective-permute-start(bf16[128,128]{1,0:T(8,128)(2,1)S(1)} %get-tuple-element.55.refs_6_.refs_10_.refs_11_.refs_12_), channel_id=1, source_target_pairs={{0,2},{1,3},{2,0},{3,1},{4,6},{5,7},{6,4},{7,5},{8,10},{9,11},{10,... | collective-permute-start | bytes 98312 | tf_op jit(solution)/shard_map/ppermute | solution.py:187
  12.3 3.6 %collective-permute-start = (bf16[128,128]{1,0:T(8,128)(2,1)S(1)}, bf16[128,128]{1,0:T(8,128)(2,1)S(1)}, u32[]{:S(2)}, u32[]{:S(2)}) collective-permute-start(bf16[128,128]{1,0:T(8,128)(2,1)S(1)} %get-tuple-element.55.refs_6_.refs_10_.refs_11_.refs_12_), channel_id=1, source_target_pairs={{0,1},{1,0},{2,3},{3,2},{4,5},{5,4},{6,7},{7,6},{8,9},{9,8},{10,11... | collective-permute-start | bytes 98312 | tf_op jit(solution)/shard_map/ppermute | solution.py:187
  19.2 10.4 %all-to-all-start.1 = ((bf16[32,2,640]{2,1,0:T(2,128)(2,1)}), bf16[32,2,640]{2,1,0:T(2,128)(2,1)S(1)}, u32[]{:S(2)}, u32[]{:S(2)}) async-start(bf16[32,2,640]{2,1,0:T(2,128)(2,1)} %get-tuple-element.66), calls=%async_computation.1 | async-start | bytes 163840 | tf_op jit(solution)/shard_map/all_to_all | solution.py:191
  22.0 3.4 %collective-permute-start.5 = (bf16[128,128]{1,0:T(8,128)(2,1)S(1)}, bf16[128,128]{1,0:T(8,128)(2,1)S(1)}, u32[]{:S(2)}, u32[]{:S(2)}) collective-permute-start(bf16[128,128]{1,0:T(8,128)(2,1)S(1)} %get-tuple-element.67.refs_6_.refs_10_.refs_11_.refs_12_), channel_id=1, source_target_pairs={{0,3},{1,2},{2,1},{3,0},{4,7},{5,6},{6,5},{7,4},{8,11},{9,10},{10,... | collective-permute-start | bytes 98312 | tf_op jit(solution)/shard_map/ppermute | solution.py:187
  23.5 4.0 %collective-permute-start.4 = (bf16[128,128]{1,0:T(8,128)(2,1)S(1)}, bf16[128,128]{1,0:T(8,128)(2,1)S(1)}, u32[]{:S(2)}, u32[]{:S(2)}) collective-permute-start(bf16[128,128]{1,0:T(8,128)(2,1)S(1)} %get-tuple-element.67.refs_6_.refs_10_.refs_11_.refs_12_), channel_id=1, source_target_pairs={{0,2},{1,3},{2,0},{3,1},{4,6},{5,7},{6,4},{7,5},{8,10},{9,11},{10,... | collective-permute-start | bytes 98312 | tf_op jit(solution)/shard_map/ppermute | solution.py:187
  23.9 3.6 %collective-permute-start.3 = (bf16[128,128]{1,0:T(8,128)(2,1)S(1)}, bf16[128,128]{1,0:T(8,128)(2,1)S(1)}, u32[]{:S(2)}, u32[]{:S(2)}) collective-permute-start(bf16[128,128]{1,0:T(8,128)(2,1)S(1)} %get-tuple-element.67.refs_6_.refs_10_.refs_11_.refs_12_), channel_id=1, source_target_pairs={{0,1},{1,0},{2,3},{3,2},{4,5},{5,4},{6,7},{7,6},{8,9},{9,8},{10,11... | collective-permute-start | bytes 98312 | tf_op jit(solution)/shard_map/ppermute | solution.py:187
  30.8 10.4 %all-to-all-start.2 = ((bf16[32,2,640]{2,1,0:T(2,128)(2,1)}), bf16[32,2,640]{2,1,0:T(2,128)(2,1)S(1)}, u32[]{:S(2)}, u32[]{:S(2)}) async-start(bf16[32,2,640]{2,1,0:T(2,128)(2,1)} %get-tuple-element.73), calls=%async_computation.2 | async-start | bytes 163840 | tf_op jit(solution)/shard_map/all_to_all | solution.py:191
  33.6 3.4 %collective-permute-start.8 = (bf16[128,128]{1,0:T(8,128)(2,1)S(1)}, bf16[128,128]{1,0:T(8,128)(2,1)S(1)}, u32[]{:S(2)}, u32[]{:S(2)}) collective-permute-start(bf16[128,128]{1,0:T(8,128)(2,1)S(1)} %get-tuple-element.74.refs_6_.refs_10_.refs_11_.refs_12_), channel_id=1, source_target_pairs={{0,3},{1,2},{2,1},{3,0},{4,7},{5,6},{6,5},{7,4},{8,11},{9,10},{10,... | collective-permute-start | bytes 98312 | tf_op jit(solution)/shard_map/ppermute | solution.py:187
  35.1 4.0 %collective-permute-start.7 = (bf16[128,128]{1,0:T(8,128)(2,1)S(1)}, bf16[128,128]{1,0:T(8,128)(2,1)S(1)}, u32[]{:S(2)}, u32[]{:S(2)}) collective-permute-start(bf16[128,128]{1,0:T(8,128)(2,1)S(1)} %get-tuple-element.74.refs_6_.refs_10_.refs_11_.refs_12_), channel_id=1, source_target_pairs={{0,2},{1,3},{2,0},{3,1},{4,6},{5,7},{6,4},{7,5},{8,10},{9,11},{10,... | collective-permute-start | bytes 98312 | tf_op jit(solution)/shard_map/ppermute | solution.py:187
  35.5 3.6 %collective-permute-start.6 = (bf16[128,128]{1,0:T(8,128)(2,1)S(1)}, bf16[128,128]{1,0:T(8,128)(2,1)S(1)}, u32[]{:S(2)}, u32[]{:S(2)}) collective-permute-start(bf16[128,128]{1,0:T(8,128)(2,1)S(1)} %get-tuple-element.74.refs_6_.refs_10_.refs_11_.refs_12_), channel_id=1, source_target_pairs={{0,1},{1,0},{2,3},{3,2},{4,5},{5,4},{6,7},{7,6},{8,9},{9,8},{10,11... | collective-permute-start | bytes 98312 | tf_op jit(solution)/shard_map/ppermute | solution.py:187
  42.4 10.4 %all-to-all-start.3 = ((bf16[32,2,640]{2,1,0:T(2,128)(2,1)}), bf16[32,2,640]{2,1,0:T(2,128)(2,1)S(1)}, u32[]{:S(2)}, u32[]{:S(2)}) async-start(bf16[32,2,640]{2,1,0:T(2,128)(2,1)} %get-tuple-element.80), calls=%async_computation.3 | async-start | bytes 163840 | tf_op jit(solution)/shard_map/all_to_all | solution.py:191
  45.1 3.4 %collective-permute-start.11 = (bf16[128,128]{1,0:T(8,128)(2,1)S(1)}, bf16[128,128]{1,0:T(8,128)(2,1)S(1)}, u32[]{:S(2)}, u32[]{:S(2)}) collective-permute-start(bf16[128,128]{1,0:T(8,128)(2,1)S(1)} %get-tuple-element.81.refs_6_.refs_10_.refs_11_), channel_id=1, source_target_pairs={{0,3},{1,2},{2,1},{3,0},{4,7},{5,6},{6,5},{7,4},{8,11},{9,10},{10,... | collective-permute-start | bytes 98312 | tf_op jit(solution)/shard_map/ppermute | solution.py:187
  46.7 4.0 %collective-permute-start.10 = (bf16[128,128]{1,0:T(8,128)(2,1)S(1)}, bf16[128,128]{1,0:T(8,128)(2,1)S(1)}, u32[]{:S(2)}, u32[]{:S(2)}) collective-permute-start(bf16[128,128]{1,0:T(8,128)(2,1)S(1)} %get-tuple-element.81.refs_6_.refs_10_.refs_11_), channel_id=1, source_target_pairs={{0,2},{1,3},{2,0},{3,1},{4,6},{5,7},{6,4},{7,5},{8,10},{9,11},{10,... | collective-permute-start | bytes 98312 | tf_op jit(solution)/shard_map/ppermute | solution.py:187
  47.1 3.6 %collective-permute-start.9 = (bf16[128,128]{1,0:T(8,128)(2,1)S(1)}, bf16[128,128]{1,0:T(8,128)(2,1)S(1)}, u32[]{:S(2)}, u32[]{:S(2)}) collective-permute-start(bf16[128,128]{1,0:T(8,128)(2,1)S(1)} %get-tuple-element.81.refs_6_.refs_10_.refs_11_), channel_id=1, source_target_pairs={{0,1},{1,0},{2,3},{3,2},{4,5},{5,4},{6,7},{7,6},{8,9},{9,8},{10,11... | collective-permute-start | bytes 98312 | tf_op jit(solution)/shard_map/ppermute | solution.py:187
  53.9 10.4 %all-to-all-start.4 = ((bf16[32,2,640]{2,1,0:T(2,128)(2,1)}), bf16[32,2,640]{2,1,0:T(2,128)(2,1)S(1)}, u32[]{:S(2)}, u32[]{:S(2)}) async-start(bf16[32,2,640]{2,1,0:T(2,128)(2,1)} %get-tuple-element.87), calls=%async_computation.4 | async-start | bytes 163840 | tf_op jit(solution)/shard_map/all_to_all | solution.py:191
  56.7 3.4 %collective-permute-start.14 = (bf16[128,128]{1,0:T(8,128)(2,1)S(1)}, bf16[128,128]{1,0:T(8,128)(2,1)S(1)}, u32[]{:S(2)}, u32[]{:S(2)}) collective-permute-start(bf16[128,128]{1,0:T(8,128)(2,1)S(1)} %get-tuple-element.88.refs_6_.refs_10_), channel_id=1, source_target_pairs={{0,3},{1,2},{2,1},{3,0},{4,7},{5,6},{6,5},{7,4},{8,11},{9,10},{10,... | collective-permute-start | bytes 98312 | tf_op jit(solution)/shard_map/ppermute | solution.py:187
  58.3 4.0 %collective-permute-start.13 = (bf16[128,128]{1,0:T(8,128)(2,1)S(1)}, bf16[128,128]{1,0:T(8,128)(2,1)S(1)}, u32[]{:S(2)}, u32[]{:S(2)}) collective-permute-start(bf16[128,128]{1,0:T(8,128)(2,1)S(1)} %get-tuple-element.88.refs_6_.refs_10_), channel_id=1, source_target_pairs={{0,2},{1,3},{2,0},{3,1},{4,6},{5,7},{6,4},{7,5},{8,10},{9,11},{10,... | collective-permute-start | bytes 98312 | tf_op jit(solution)/shard_map/ppermute | solution.py:187
  58.7 3.6 %collective-permute-start.12 = (bf16[128,128]{1,0:T(8,128)(2,1)S(1)}, bf16[128,128]{1,0:T(8,128)(2,1)S(1)}, u32[]{:S(2)}, u32[]{:S(2)}) collective-permute-start(bf16[128,128]{1,0:T(8,128)(2,1)S(1)} %get-tuple-element.88.refs_6_.refs_10_), channel_id=1, source_target_pairs={{0,1},{1,0},{2,3},{3,2},{4,5},{5,4},{6,7},{7,6},{8,9},{9,8},{10,11... | collective-permute-start | bytes 98312 | tf_op jit(solution)/shard_map/ppermute | solution.py:187
  65.5 10.4 %all-to-all-start.5 = ((bf16[32,2,640]{2,1,0:T(2,128)(2,1)}), bf16[32,2,640]{2,1,0:T(2,128)(2,1)S(1)}, u32[]{:S(2)}, u32[]{:S(2)}) async-start(bf16[32,2,640]{2,1,0:T(2,128)(2,1)} %get-tuple-element.94), calls=%async_computation.5 | async-start | bytes 163840 | tf_op jit(solution)/shard_map/all_to_all | solution.py:191
  68.3 3.4 %collective-permute-start.17 = (bf16[128,128]{1,0:T(8,128)(2,1)S(1)}, bf16[128,128]{1,0:T(8,128)(2,1)S(1)}, u32[]{:S(2)}, u32[]{:S(2)}) collective-permute-start(bf16[128,128]{1,0:T(8,128)(2,1)S(1)} %get-tuple-element.95.refs_6_), channel_id=1, source_target_pairs={{0,3},{1,2},{2,1},{3,0},{4,7},{5,6},{6,5},{7,4},{8,11},{9,10},{10,... | collective-permute-start | bytes 98312 | tf_op jit(solution)/shard_map/ppermute | solution.py:187
  69.9 4.0 %collective-permute-start.16 = (bf16[128,128]{1,0:T(8,128)(2,1)S(1)}, bf16[128,128]{1,0:T(8,128)(2,1)S(1)}, u32[]{:S(2)}, u32[]{:S(2)}) collective-permute-start(bf16[128,128]{1,0:T(8,128)(2,1)S(1)} %get-tuple-element.95.refs_6_), channel_id=1, source_target_pairs={{0,2},{1,3},{2,0},{3,1},{4,6},{5,7},{6,4},{7,5},{8,10},{9,11},{10,... | collective-permute-start | bytes 98312 | tf_op jit(solution)/shard_map/ppermute | solution.py:187
  70.3 3.6 %collective-permute-start.15 = (bf16[128,128]{1,0:T(8,128)(2,1)S(1)}, bf16[128,128]{1,0:T(8,128)(2,1)S(1)}, u32[]{:S(2)}, u32[]{:S(2)}) collective-permute-start(bf16[128,128]{1,0:T(8,128)(2,1)S(1)} %get-tuple-element.95.refs_6_), channel_id=1, source_target_pairs={{0,1},{1,0},{2,3},{3,2},{4,5},{5,4},{6,7},{7,6},{8,9},{9,8},{10,11... | collective-permute-start | bytes 98312 | tf_op jit(solution)/shard_map/ppermute | solution.py:187

commit v4 on v3

--- a/solution.py
+++ b/solution.py
@@ -13,6 +13,7 @@
 TERMS = 3
 F32, BF16 = jnp.float32, jnp.bfloat16
 VMEM = pl.BlockSpec(memory_space=pltpu.VMEM)
+HBM = pl.BlockSpec(memory_space=pl.ANY)
 
 
 def iota(shape, axis):
@@ -33,15 +34,20 @@
     return jnp.sum(jnp.where(eye, jnp.broadcast_to(line, eye.shape), 0.0), axis=1, keepdims=True)
 
 
-def send(picked, out_ref, group):
+def send(picked, chunks, out_ref, sems):
     stimuli = picked.shape[1]
-    areas = out_ref.shape[0] // group
-    for tile in range(out_ref.shape[2] // stimuli):
+    areas = chunks.shape[0]
+    for tile in range(chunks.shape[2] // stimuli):
         for area in range(areas):
             start = (tile * areas + area) * PAIR
-            for member in range(group):
-                spot = (area * group + member, slice(None), slice(tile * stimuli, (tile + 1) * stimuli))
-                out_ref[spot] = picked[start : start + PAIR]
+            chunks[area, :, tile * stimuli : (tile + 1) * stimuli] = picked[start : start + PAIR]
+    copies = [
+        pltpu.make_async_copy(chunks, out_ref.at[:, member], sems.at[member])
+        for member in range(out_ref.shape[1])
+    ]
+    for copy in copies:
+        copy.start()
+    return copies
 
 
 def rows_from(chunks, stimuli):
@@ -50,24 +56,22 @@
 
 
 def pack_kernel(group, senders, *refs):
-    given, outs, scratch = refs[:7], refs[7:-9], refs[-9:]
-    held, padded, sems = scratch[:7], scratch[7], scratch[8]
-    weights, state, rate, choice, outgoing, *past = outs
+    given, outs, scratch = refs[:7], refs[7:-11], refs[-11:]
+    held, (padded, chunks_ref, sems, send_sems) = scratch[:7], scratch[7:]
+    outgoing, weights, state, rate, choice, older, *past = outs
     copies = [
         pltpu.make_async_copy(src, dst, sems.at[i]) for i, (src, dst) in enumerate(zip(given, held))
     ]
     for copy in copies:
         copy.start()
-    for copy in copies:
-        copy.wait()
+    for i in (4, 5, 6, 1, 0):
+        copies[i].wait()
     history, leak, w_local, w_long, table, lags, sizes = held
     depth, block = history.shape[:2]
     areas = table.shape[0]
     me = lax.axis_index("nrn")
-    active = (iota((block, 1), 0) + me * block < sizes[0:1, 0:1]).astype(F32)
+    active = (iota((block, 1), 0) + me * block < sizes[0]).astype(F32)
     state[...] = history[0] * active
-    for age in range(depth):
-        past[age][...] = (history[age] * active).astype(BF16)
     rate[...] = jnp.broadcast_to(active * column(leak[...]), rate.shape)
 
     tiles = -(-senders // PAIR)
@@ -86,9 +90,17 @@
         places.append(row + jnp.where(sender < senders, age, float(depth)) * block)
     lanes = iota(choice.shape, 1).astype(F32)
     choice[...] = (lanes == jnp.concatenate(places, axis=0)).astype(F32).astype(BF16)
-    recent = jnp.concatenate([ref[...] for ref in past], axis=0)
-    send(jnp.dot(choice[...], recent, preferred_element_type=F32).astype(BF16), outgoing, group)
-
+    rows = [(history[age] * active).astype(BF16) for age in range(depth)]
+    picked = jnp.dot(choice[...], jnp.concatenate(rows, axis=0), preferred_element_type=F32)
+    sent = send(picked.astype(BF16), chunks_ref, outgoing, send_sems)
+    older[...] = jnp.dot(
+        choice[:, block:], jnp.concatenate(rows[:-1], axis=0), preferred_element_type=F32
+    )
+    for ref, values in zip(past, rows):
+        ref[...] = values
+
+    for i in (2, 3):
+        copies[i].wait()
     near = w_local.shape[1]
     for term, values in enumerate(terms_of(w_local[...])):
         weights[term * block : (term + 1) * block, :near] = values
@@ -109,12 +121,14 @@
         for term, values in enumerate(terms_of(tile)):
             spot = near + part * block
             weights[term * block : (term + 1) * block, spot : spot + width] = values[:, :width]
-
-
-def step_kernel(group, depth, last, *refs):
-    (weights, received, state, drive, rate, choice), refs = refs[:6], refs[6:]
-    mates, past, refs = refs[:group], refs[group : group + depth - 1], refs[group + depth - 1 :]
-    current, outs = refs[-1], refs[:-1]
+    for copy in sent:
+        copy.wait()
+
+
+def step_kernel(group, left, *refs):
+    (weights, received, state, drive, rate), mates = refs[:5], refs[5 : 5 + group]
+    refs = refs[5 + group :]
+    outs, current = refs[:-3] if left else refs[:-1], refs[-1]
     block = state.shape[0]
     near = group * block
     me = lax.axis_index("nrn")
@@ -128,14 +142,20 @@
     inputs = functools.reduce(lambda a, b: a + b, reversed(parts)) + drive[...]
     old = state[...]
     new = old + rate[...] * (jnp.tanh(inputs) - old)
-    if last:
+    if not left:
         outs[0][...] = new
         return
-    new_state, newest, outgoing = outs
+    (choice, older, *past), (outgoing, new_state, newest, *next_older) = outs[:left], outs[left:]
+    rounded = new.astype(BF16)
+    picked = older[...] + jnp.dot(choice[:, :block], rounded, preferred_element_type=F32)
+    copies = send(picked.astype(BF16), refs[-3], outgoing, refs[-2])
     new_state[...] = new
-    newest[...] = new.astype(BF16)
-    recent = jnp.concatenate([new.astype(BF16), mates[0][...]] + [ref[...] for ref in past[:-1]], axis=0)
-    send(jnp.dot(choice[...], recent, preferred_element_type=F32).astype(BF16), outgoing, group)
+    newest[...] = rounded
+    rows = jnp.concatenate([rounded, mates[0][...]] + [ref[...] for ref in past], axis=0)
+    for ref in next_older:
+        ref[...] = jnp.dot(choice[:, block:], rows, preferred_element_type=F32)
+    for copy in copies:
+        copy.wait()
 
 
 def call(kernel, out_shape, operands, scratch=(), **settings):
@@ -144,7 +164,7 @@
     return pl.pallas_call(
         kernel,
         out_shape=out_shape,
-        out_specs=[VMEM] * len(out_shape),
+        out_specs=[HBM if len(value.shape) == 4 else VMEM for value in out_shape],
         compiler_params=pltpu.CompilerParams(vmem_limit_bytes=held + (4 << 20)),
         scratch_shapes=scratch,
         **{"in_specs": [VMEM] * len(operands), **settings},
@@ -158,7 +178,9 @@
     near, far = group * block, areas * group * tiles * PAIR
     shape = jax.ShapeDtypeStruct
     tile = lambda kind: shape((block, stimuli), kind)
-    sent = shape((areas * group, PAIR, tiles * stimuli), BF16)
+    sent = shape((areas, group, PAIR, tiles * stimuli), BF16)
+    elder = shape((areas * tiles * PAIR, stimuli), F32)
+    sending = [pltpu.VMEM((areas, PAIR, tiles * stimuli), BF16), pltpu.SemaphoreType.DMA((group,))]
     given = [
         history,
         leak.reshape(1, block),
@@ -166,39 +188,52 @@
         w_long.transpose(1, 2, 0),
         sender_rows[0],
         delays,
-        area_sizes.reshape(1, 1),
+        area_sizes,
     ]
     stay = lambda v: pltpu.with_memory_space_constraint(v, pltpu.HBM) if v.size > 1 else v
-    weights, state, rate, choice, outgoing, *past = call(
+    outgoing, weights, state, rate, choice, *rest = call(
         functools.partial(pack_kernel, group, senders),
         [
+            sent,
             shape((TERMS * block, near + far), BF16),
             tile(F32),
             tile(F32),
             shape((areas * tiles * PAIR, depth * block), BF16),
-            sent,
-            *[tile(BF16)] * depth,
+            elder,
+            *[tile(BF16)] * (depth - 2),
         ],
         [stay(v) for v in given],
-        [pltpu.VMEM(v.shape, v.dtype) for v in given]
-        + [pltpu.VMEM((far + -far % block, block), F32), pltpu.SemaphoreType.DMA((len(given),))],
-        in_specs=[pl.BlockSpec(memory_space=pl.ANY)] * len(given),
-    )
+        [pltpu.VMEM(v.shape, v.dtype) for v in given[:-1]]
+        + [pltpu.SMEM(area_sizes.shape, area_sizes.dtype)]
+        + [pltpu.VMEM((far + -far % block, block), F32), sending[0]]
+        + [pltpu.SemaphoreType.DMA((len(given),)), sending[1]],
+        in_specs=[HBM] * len(given),
+    )
+    older, past = rest[:1], rest[1:]
     swap = lambda v, bits: lax.ppermute(v, "nrn", [(i, i ^ bits) for i in range(group)])
     for iteration in range(STEPS):
         final = iteration == STEPS - 1
         mates = [swap(past[0], bits) for bits in range(1, group)]
-        received = lax.all_to_all(outgoing, ("area", "nrn"), split_axis=0, concat_axis=0, tiled=True)
+        received = lax.all_to_all(
+            outgoing.reshape(areas * group, PAIR, -1),
+            ("area", "nrn"),
+            split_axis=0,
+            concat_axis=0,
+            tiled=True,
+        )
         received, mates = lax.optimization_barrier((received, mates))
+        more = iteration < STEPS - 2
+        picking = [] if final else [choice, *older, *past[1:]]
         result = call(
-            functools.partial(step_kernel, group, depth, final),
-            [tile(F32)] if final else [tile(F32), tile(BF16), sent],
-            [weights, received, state, drive, rate, choice, past[0], *mates, *past[1:]],
-            [pltpu.VMEM((near, stimuli), BF16)],
+            functools.partial(step_kernel, group, len(picking)),
+            [tile(F32)] if final else [sent, tile(F32), tile(BF16)] + [elder] * more,
+            [weights, received, state, drive, rate, past[0], *mates]
+            + picking,
+            sending * (not final) + [pltpu.VMEM((near, stimuli), BF16)],
         )
         if final:
             return result[0]
-        state, newest, outgoing = result
+        outgoing, state, newest, *older = result
         past = [newest, *past[:-1]]
 
 

time: 77.3 us -> 77.1 us (level)
  no operation moved by 1% of the time
where the time goes in v4:
time: 77.1 us; the launch traced here: 76.6 us
  waiting for transfers between devices  33.7 us (44%)
  starting transfers between devices  33 us (43%)
  Pallas kernels  9.15 us (12%)
  between operations  0.78 us (1%)
    ppermute x18, waiting for transfers between devices, local(): lax.ppermute(v, 'nrn', [(i, i ^ bits) for i in range(group)])  21.8 us
    all_to_all x6, starting transfers between devices, local(): lax.all_to_all(outgoing.reshape(areas * group, PAIR, -1), ('area', 'nrn')...  21.2 us
    all_to_all x6, waiting for transfers between devices, local(): lax.all_to_all(outgoing.reshape(areas * group, PAIR, -1), ('area', 'nrn')...  12 us
    ppermute x18, starting transfers between devices, local(): lax.ppermute(v, 'nrn', [(i, i ^ bits) for i in range(group)])  11.7 us
    pallas_call x7, Pallas kernels, call(): pl.pallas_call(kernel, out_shape=out_shape, out_specs=[HBM if len(value.s...  9.15 us
  transfers between devices with their start and end apart: 24, of which 18 were waited for; matrix products, arithmetic and copies ran while one was open for 0% of the time, Pallas kernels for 0%

profile of v4, /device:TPU:0, one launch (start us, length us, event | category | flops | bytes accessed | tf_op | source)
XLA Modules:
  0.0 76.6 jit_solution(17743955324747518648)
XLA Ops:
  0.7 2.1 %shard_map.82 = (bf16[8,4,2,640]{3,2,1,0:T(2,128)(2,1)}, bf16[384,832]{1,0:T(8,128)(2,1)S(1)}, f32[128,128]{1,0:T(8,128)S(1)}, f32[128,128]{1,0:T(8,128)S(1)}, b...) custom-call(f32[4,128,128]{2,1,0:T(8,128)} %refs_0_.1, ...), custom_call_target="tpu_custom_call" | custom-call | tf_op jit(solution)/shard_map/pallas_call | solution.py:164
  2.8 0.0 copy-start
  2.8 7.3 %all-to-all-start = ((bf16[32,2,640]{2,1,0:T(2,128)(2,1)}), bf16[32,2,640]{2,1,0:T(2,128)(2,1)S(1)}, u32[]{:S(2)}, u32[]{:S(2)}) async-start(bf16[32,2,640]{2,1,0:T(2,128)(2,1)} %bitcast.3), calls=%async_computation | async-start | bytes 163840 | tf_op jit(solution)/shard_map/all_to_all | solution.py:217
  10.1 1.6 %collective-permute-start.2 = (bf16[128,128]{1,0:T(8,128)(2,1)S(1)}, bf16[128,128]{1,0:T(8,128)(2,1)S(1)}, u32[]{:S(2)}, u32[]{:S(2)}) collective-permute-start(bf16[128,128]{1,0:T(8,128)(2,1)S(1)} %get-tuple-element.58.refs_5_.refs_11_), channel_id=1, source_target_pairs={{0,3},{1,2},{2,1},{3,0},{4,7},{5,6},{6,5},{7,4},{8,11},{9,10},{10,... | collective-permute-start | bytes 98312 | tf_op jit(solution)/shard_map/ppermute | solution.py:213
  11.7 0.4 collective-permute-start.1
  12.1 0.0 collective-permute-start
  12.1 1.5 %collective-permute-done.2.refs_8_ = bf16[128,128]{1,0:T(8,128)(2,1)S(1)} collective-permute-done((bf16[128,128]{1,0:T(8,128)(2,1)S(1)}, bf16[128,128]{1,0:T(8,128)(2,1)S(1)}, u32[]{:S(2)}, u32[]{:S(2)}) %collective-permute-start.2) | collective-permute-done | bytes 32800 | tf_op jit(solution)/shard_map/ppermute | solution.py:213
  13.5 2.2 %collective-permute-done.1.refs_7_ = bf16[128,128]{1,0:T(8,128)(2,1)S(1)} collective-permute-done((bf16[128,128]{1,0:T(8,128)(2,1)S(1)}, bf16[128,128]{1,0:T(8,128)(2,1)S(1)}, u32[]{:S(2)}, u32[]{:S(2)}) %collective-permute-start.1) | collective-permute-done | bytes 32800 | tf_op jit(solution)/shard_map/ppermute | solution.py:213
  15.7 0.0 collective-permute-done.refs_6_
  15.7 2.0 %all-to-all-done.refs_1_ = bf16[32,2,640]{2,1,0:T(2,128)(2,1)S(1)} async-done(((bf16[32,2,640]{2,1,0:T(2,128)(2,1)}), bf16[32,2,640]{2,1,0:T(2,128)(2,1)S(1)}, u32[]{:S(2)}, u32[]{:S(2)}) %all-to-all-start) | async-done | bytes 81952 | tf_op jit(solution)/shard_map/all_to_all | solution.py:217
  17.7 0.0 copy-done
  17.7 1.2 %shard_map.83 = (bf16[8,4,2,640]{3,2,1,0:T(2,128)(2,1)}, f32[128,128]{1,0:T(8,128)S(1)}, bf16[128,128]{1,0:T(8,128)(2,1)S(1)}, f32[80,128]{1,0:T(8,128)S(1)}) custom-call(bf16[384,832]{1,0:T(8,128)(2,1)S(1)} %get-tuple-element.56.refs_0_, bf16[32,2,640]{2,1,0:T(2,128)(2,1)S(1)} %all-to-all-done.refs_1_, f32[128,128]{1,0:T(8,128)S(1)} %get-tuple-element.60.refs_2_, ...), custom_call_target="tpu_custom_call" | custom-call | tf_op jit(solution)/shard_map/pallas_call | solution.py:164
  18.9 2.8 %all-to-all-start.1 = ((bf16[32,2,640]{2,1,0:T(2,128)(2,1)}), bf16[32,2,640]{2,1,0:T(2,128)(2,1)S(1)}, u32[]{:S(2)}, u32[]{:S(2)}) async-start(bf16[32,2,640]{2,1,0:T(2,128)(2,1)} %bitcast.4), calls=%async_computation.1 | async-start | bytes 163840 | tf_op jit(solution)/shard_map/all_to_all | solution.py:217
  21.7 1.6 %collective-permute-start.5 = (bf16[128,128]{1,0:T(8,128)(2,1)S(1)}, bf16[128,128]{1,0:T(8,128)(2,1)S(1)}, u32[]{:S(2)}, u32[]{:S(2)}) collective-permute-start(bf16[128,128]{1,0:T(8,128)(2,1)S(1)} %get-tuple-element.69.refs_5_.refs_11_), channel_id=1, source_target_pairs={{0,3},{1,2},{2,1},{3,0},{4,7},{5,6},{6,5},{7,4},{8,11},{9,10},{10,... | collective-permute-start | bytes 98312 | tf_op jit(solution)/shard_map/ppermute | solution.py:213
  23.3 0.4 collective-permute-start.4
  23.7 0.0 collective-permute-start.3
  23.7 1.5 %collective-permute-done.5.refs_8_ = bf16[128,128]{1,0:T(8,128)(2,1)S(1)} collective-permute-done((bf16[128,128]{1,0:T(8,128)(2,1)S(1)}, bf16[128,128]{1,0:T(8,128)(2,1)S(1)}, u32[]{:S(2)}, u32[]{:S(2)}) %collective-permute-start.5) | collective-permute-done | bytes 32800 | tf_op jit(solution)/shard_map/ppermute | solution.py:213
  25.1 2.2 %collective-permute-done.4.refs_7_ = bf16[128,128]{1,0:T(8,128)(2,1)S(1)} collective-permute-done((bf16[128,128]{1,0:T(8,128)(2,1)S(1)}, bf16[128,128]{1,0:T(8,128)(2,1)S(1)}, u32[]{:S(2)}, u32[]{:S(2)}) %collective-permute-start.4) | collective-permute-done | bytes 32800 | tf_op jit(solution)/shard_map/ppermute | solution.py:213
  27.3 0.0 collective-permute-done.3.refs_6_
  27.3 2.0 %all-to-all-done.1.refs_1_ = bf16[32,2,640]{2,1,0:T(2,128)(2,1)S(1)} async-done(((bf16[32,2,640]{2,1,0:T(2,128)(2,1)}), bf16[32,2,640]{2,1,0:T(2,128)(2,1)S(1)}, u32[]{:S(2)}, u32[]{:S(2)}) %all-to-all-start.1) | async-done | bytes 81952 | tf_op jit(solution)/shard_map/all_to_all | solution.py:217
  29.3 1.2 %shard_map.84 = (bf16[8,4,2,640]{3,2,1,0:T(2,128)(2,1)}, f32[128,128]{1,0:T(8,128)S(1)}, bf16[128,128]{1,0:T(8,128)(2,1)S(1)}, f32[80,128]{1,0:T(8,128)S(1)}) custom-call(bf16[384,832]{1,0:T(8,128)(2,1)S(1)} %get-tuple-element.56.refs_0_, bf16[32,2,640]{2,1,0:T(2,128)(2,1)S(1)} %all-to-all-done.1.refs_1_, f32[128,128]{1,0:T(8,128)S(1)} %get-tuple-element.71.refs_2_, ...), custom_call_target="tpu_custom_call" | custom-call | tf_op jit(solution)/shard_map/pallas_call | solution.py:164
  30.5 2.8 %all-to-all-start.2 = ((bf16[32,2,640]{2,1,0:T(2,128)(2,1)}), bf16[32,2,640]{2,1,0:T(2,128)(2,1)S(1)}, u32[]{:S(2)}, u32[]{:S(2)}) async-start(bf16[32,2,640]{2,1,0:T(2,128)(2,1)} %bitcast.5), calls=%async_computation.2 | async-start | bytes 163840 | tf_op jit(solution)/shard_map/all_to_all | solution.py:217
  33.3 1.6 %collective-permute-start.8 = (bf16[128,128]{1,0:T(8,128)(2,1)S(1)}, bf16[128,128]{1,0:T(8,128)(2,1)S(1)}, u32[]{:S(2)}, u32[]{:S(2)}) collective-permute-start(bf16[128,128]{1,0:T(8,128)(2,1)S(1)} %get-tuple-element.77.refs_5_.refs_11_), channel_id=1, source_target_pairs={{0,3},{1,2},{2,1},{3,0},{4,7},{5,6},{6,5},{7,4},{8,11},{9,10},{10,... | collective-permute-start | bytes 98312 | tf_op jit(solution)/shard_map/ppermute | solution.py:213
  34.9 0.4 collective-permute-start.7
  35.3 0.0 collective-permute-start.6
  35.3 1.5 %collective-permute-done.8.refs_8_ = bf16[128,128]{1,0:T(8,128)(2,1)S(1)} collective-permute-done((bf16[128,128]{1,0:T(8,128)(2,1)S(1)}, bf16[128,128]{1,0:T(8,128)(2,1)S(1)}, u32[]{:S(2)}, u32[]{:S(2)}) %collective-permute-start.8) | collective-permute-done | bytes 32800 | tf_op jit(solution)/shard_map/ppermute | solution.py:213
  36.7 2.2 %collective-permute-done.7.refs_7_ = bf16[128,128]{1,0:T(8,128)(2,1)S(1)} collective-permute-done((bf16[128,128]{1,0:T(8,128)(2,1)S(1)}, bf16[128,128]{1,0:T(8,128)(2,1)S(1)}, u32[]{:S(2)}, u32[]{:S(2)}) %collective-permute-start.7) | collective-permute-done | bytes 32800 | tf_op jit(solution)/shard_map/ppermute | solution.py:213
  38.9 0.0 collective-permute-done.6.refs_6_
  38.9 2.0 %all-to-all-done.2.refs_1_ = bf16[32,2,640]{2,1,0:T(2,128)(2,1)S(1)} async-done(((bf16[32,2,640]{2,1,0:T(2,128)(2,1)}), bf16[32,2,640]{2,1,0:T(2,128)(2,1)S(1)}, u32[]{:S(2)}, u32[]{:S(2)}) %all-to-all-start.2) | async-done | bytes 81952 | tf_op jit(solution)/shard_map/all_to_all | solution.py:217
  40.9 1.2 %shard_map.85 = (bf16[8,4,2,640]{3,2,1,0:T(2,128)(2,1)}, f32[128,128]{1,0:T(8,128)S(1)}, bf16[128,128]{1,0:T(8,128)(2,1)S(1)}, f32[80,128]{1,0:T(8,128)S(1)}) custom-call(bf16[384,832]{1,0:T(8,128)(2,1)S(1)} %get-tuple-element.56.refs_0_, bf16[32,2,640]{2,1,0:T(2,128)(2,1)S(1)} %all-to-all-done.2.refs_1_, f32[128,128]{1,0:T(8,128)S(1)} %get-tuple-element.79.refs_2_, ...), custom_call_target="tpu_custom_call" | custom-call | tf_op jit(solution)/shard_map/pallas_call | solution.py:164
  42.1 2.8 %all-to-all-start.3 = ((bf16[32,2,640]{2,1,0:T(2,128)(2,1)}), bf16[32,2,640]{2,1,0:T(2,128)(2,1)S(1)}, u32[]{:S(2)}, u32[]{:S(2)}) async-start(bf16[32,2,640]{2,1,0:T(2,128)(2,1)} %bitcast.6), calls=%async_computation.3 | async-start | bytes 163840 | tf_op jit(solution)/shard_map/all_to_all | solution.py:217
  44.9 1.6 %collective-permute-start.11 = (bf16[128,128]{1,0:T(8,128)(2,1)S(1)}, bf16[128,128]{1,0:T(8,128)(2,1)S(1)}, u32[]{:S(2)}, u32[]{:S(2)}) collective-permute-start(bf16[128,128]{1,0:T(8,128)(2,1)S(1)} %get-tuple-element.85.refs_5_.refs_11_), channel_id=1, source_target_pairs={{0,3},{1,2},{2,1},{3,0},{4,7},{5,6},{6,5},{7,4},{8,11},{9,10},{10,... | collective-permute-start | bytes 98312 | tf_op jit(solution)/shard_map/ppermute | solution.py:213
  46.5 0.4 collective-permute-start.10
  46.9 0.0 collective-permute-start.9
  46.9 1.5 %collective-permute-done.11.refs_8_ = bf16[128,128]{1,0:T(8,128)(2,1)S(1)} collective-permute-done((bf16[128,128]{1,0:T(8,128)(2,1)S(1)}, bf16[128,128]{1,0:T(8,128)(2,1)S(1)}, u32[]{:S(2)}, u32[]{:S(2)}) %collective-permute-start.11) | collective-permute-done | bytes 32800 | tf_op jit(solution)/shard_map/ppermute | solution.py:213
  48.3 2.2 %collective-permute-done.10.refs_7_ = bf16[128,128]{1,0:T(8,128)(2,1)S(1)} collective-permute-done((bf16[128,128]{1,0:T(8,128)(2,1)S(1)}, bf16[128,128]{1,0:T(8,128)(2,1)S(1)}, u32[]{:S(2)}, u32[]{:S(2)}) %collective-permute-start.10) | collective-permute-done | bytes 32800 | tf_op jit(solution)/shard_map/ppermute | solution.py:213
  50.5 0.0 collective-permute-done.9.refs_6_
  50.5 2.0 %all-to-all-done.3.refs_1_ = bf16[32,2,640]{2,1,0:T(2,128)(2,1)S(1)} async-done(((bf16[32,2,640]{2,1,0:T(2,128)(2,1)}), bf16[32,2,640]{2,1,0:T(2,128)(2,1)S(1)}, u32[]{:S(2)}, u32[]{:S(2)}) %all-to-all-start.3) | async-done | bytes 81952 | tf_op jit(solution)/shard_map/all_to_all | solution.py:217
  52.5 1.2 %shard_map.86 = (bf16[8,4,2,640]{3,2,1,0:T(2,128)(2,1)}, f32[128,128]{1,0:T(8,128)S(1)}, bf16[128,128]{1,0:T(8,128)(2,1)S(1)}, f32[80,128]{1,0:T(8,128)S(1)}) custom-call(bf16[384,832]{1,0:T(8,128)(2,1)S(1)} %get-tuple-element.56.refs_0_, bf16[32,2,640]{2,1,0:T(2,128)(2,1)S(1)} %all-to-all-done.3.refs_1_, f32[128,128]{1,0:T(8,128)S(1)} %get-tuple-element.87.refs_2_, ...), custom_call_target="tpu_custom_call" | custom-call | tf_op jit(solution)/shard_map/pallas_call | solution.py:164
  53.7 2.8 %all-to-all-start.4 = ((bf16[32,2,640]{2,1,0:T(2,128)(2,1)}), bf16[32,2,640]{2,1,0:T(2,128)(2,1)S(1)}, u32[]{:S(2)}, u32[]{:S(2)}) async-start(bf16[32,2,640]{2,1,0:T(2,128)(2,1)} %bitcast.7), calls=%async_computation.4 | async-start | bytes 163840 | tf_op jit(solution)/shard_map/all_to_all | solution.py:217
  56.5 1.6 %collective-permute-start.14 = (bf16[128,128]{1,0:T(8,128)(2,1)S(1)}, bf16[128,128]{1,0:T(8,128)(2,1)S(1)}, u32[]{:S(2)}, u32[]{:S(2)}) collective-permute-start(bf16[128,128]{1,0:T(8,128)(2,1)S(1)} %get-tuple-element.93.refs_5_), channel_id=1, source_target_pairs={{0,3},{1,2},{2,1},{3,0},{4,7},{5,6},{6,5},{7,4},{8,11},{9,10},{10,... | collective-permute-start | bytes 98312 | tf_op jit(solution)/shard_map/ppermute | solution.py:213
  58.0 0.4 collective-permute-start.13
  58.4 0.0 collective-permute-start.12
  58.4 1.5 %collective-permute-done.14.refs_8_ = bf16[128,128]{1,0:T(8,128)(2,1)S(1)} collective-permute-done((bf16[128,128]{1,0:T(8,128)(2,1)S(1)}, bf16[128,128]{1,0:T(8,128)(2,1)S(1)}, u32[]{:S(2)}, u32[]{:S(2)}) %collective-permute-start.14) | collective-permute-done | bytes 32800 | tf_op jit(solution)/shard_map/ppermute | solution.py:213
  59.9 2.2 %collective-permute-done.13.refs_7_ = bf16[128,128]{1,0:T(8,128)(2,1)S(1)} collective-permute-done((bf16[128,128]{1,0:T(8,128)(2,1)S(1)}, bf16[128,128]{1,0:T(8,128)(2,1)S(1)}, u32[]{:S(2)}, u32[]{:S(2)}) %collective-permute-start.13) | collective-permute-done | bytes 32800 | tf_op jit(solution)/shard_map/ppermute | solution.py:213
  62.1 0.0 collective-permute-done.12.refs_6_
  62.1 2.0 %all-to-all-done.4.refs_1_ = bf16[32,2,640]{2,1,0:T(2,128)(2,1)S(1)} async-done(((bf16[32,2,640]{2,1,0:T(2,128)(2,1)}), bf16[32,2,640]{2,1,0:T(2,128)(2,1)S(1)}, u32[]{:S(2)}, u32[]{:S(2)}) %all-to-all-start.4) | async-done | bytes 81952 | tf_op jit(solution)/shard_map/all_to_all | solution.py:217
  64.1 1.2 %shard_map.87 = (bf16[8,4,2,640]{3,2,1,0:T(2,128)(2,1)}, f32[128,128]{1,0:T(8,128)S(1)}, bf16[128,128]{1,0:T(8,128)(2,1)S(1)}) custom-call(bf16[384,832]{1,0:T(8,128)(2,1)S(1)} %get-tuple-element.56.refs_0_, bf16[32,2,640]{2,1,0:T(2,128)(2,1)S(1)} %all-to-all-done.4.refs_1_, f32[128,128]{1,0:T(8,128)S(1)} %get-tuple-element.95.refs_2_, ...), custom_call_target="tpu_custom_call" | custom-call | tf_op jit(solution)/shard_map/pallas_call | solution.py:164
  65.3 2.8 %all-to-all-start.5 = ((bf16[32,2,640]{2,1,0:T(2,128)(2,1)}), bf16[32,2,640]{2,1,0:T(2,128)(2,1)S(1)}, u32[]{:S(2)}, u32[]{:S(2)}) async-start(bf16[32,2,640]{2,1,0:T(2,128)(2,1)} %bitcast.8), calls=%async_computation.5 | async-start | bytes 163840 | tf_op jit(solution)/shard_map/all_to_all | solution.py:217
  68.1 1.6 %collective-permute-start.17 = (bf16[128,128]{1,0:T(8,128)(2,1)S(1)}, bf16[128,128]{1,0:T(8,128)(2,1)S(1)}, u32[]{:S(2)}, u32[]{:S(2)}) collective-permute-start(bf16[128,128]{1,0:T(8,128)(2,1)S(1)} %get-tuple-element.101.refs_5_), channel_id=1, source_target_pairs={{0,3},{1,2},{2,1},{3,0},{4,7},{5,6},{6,5},{7,4},{8,11},{9,10},{10,... | collective-permute-start | bytes 98312 | tf_op jit(solution)/shard_map/ppermute | solution.py:213
  69.6 0.4 collective-permute-start.16
  70.0 0.0 collective-permute-start.15
  70.0 1.5 %collective-permute-done.17.refs_8_ = bf16[128,128]{1,0:T(8,128)(2,1)S(1)} collective-permute-done((bf16[128,128]{1,0:T(8,128)(2,1)S(1)}, bf16[128,128]{1,0:T(8,128)(2,1)S(1)}, u32[]{:S(2)}, u32[]{:S(2)}) %collective-permute-start.17) | collective-permute-done | bytes 32800 | tf_op jit(solution)/shard_map/ppermute | solution.py:213
  71.5 2.2 %collective-permute-done.16.refs_7_ = bf16[128,128]{1,0:T(8,128)(2,1)S(1)} collective-permute-done((bf16[128,128]{1,0:T(8,128)(2,1)S(1)}, bf16[128,128]{1,0:T(8,128)(2,1)S(1)}, u32[]{:S(2)}, u32[]{:S(2)}) %collective-permute-start.16) | collective-permute-done | bytes 32800 | tf_op jit(solution)/shard_map/ppermute | solution.py:213
  73.6 0.0 collective-permute-done.15.refs_6_
  73.6 2.0 %all-to-all-done.5.refs_1_ = bf16[32,2,640]{2,1,0:T(2,128)(2,1)S(1)} async-done(((bf16[32,2,640]{2,1,0:T(2,128)(2,1)}), bf16[32,2,640]{2,1,0:T(2,128)(2,1)S(1)}, u32[]{:S(2)}, u32[]{:S(2)}) %all-to-all-start.5) | async-done | bytes 81952 | tf_op jit(solution)/shard_map/all_to_all | solution.py:217
  75.6 1.0 %shard_map.88 = f32[128,128]{1,0:T(8,128)} custom-call(bf16[384,832]{1,0:T(8,128)(2,1)S(1)} %get-tuple-element.56.refs_0_, bf16[32,2,640]{2,1,0:T(2,128)(2,1)S(1)} %all-to-all-done.5.refs_1_, f32[128,128]{1,0:T(8,128)S(1)} %get-tuple-element.103.refs_2_, f32[128,128]{1,0:T(8,128)S(1)} %copy-done, f32[128,128]{1,0:T(8,128)S(1)} %get-tuple-element.61.refs_4_, ...), custom_call_target="tpu_custom_call" | custom-call | tf_op jit(solution)/shard_map/pallas_call | solution.py:164
Async XLA Ops:
  2.8 14.9 %copy-start = (f32[128,128]{1,0:T(8,128)S(1)}, f32[128,128]{1,0:T(8,128)}, u32[]{:S(2)}) copy-start(f32[128,128]{1,0:T(8,128)} %refs_3_.11) | copy-start | bytes 196612
  2.8 14.9 %all-to-all-start = ((bf16[32,2,640]{2,1,0:T(2,128)(2,1)}), bf16[32,2,640]{2,1,0:T(2,128)(2,1)S(1)}, u32[]{:S(2)}, u32[]{:S(2)}) async-start(bf16[32,2,640]{2,1,0:T(2,128)(2,1)} %bitcast.3), calls=%async_computation | async-start | bytes 163840 | tf_op jit(solution)/shard_map/all_to_all | solution.py:217
  10.1 3.4 %collective-permute-start.2 = (bf16[128,128]{1,0:T(8,128)(2,1)S(1)}, bf16[128,128]{1,0:T(8,128)(2,1)S(1)}, u32[]{:S(2)}, u32[]{:S(2)}) collective-permute-start(bf16[128,128]{1,0:T(8,128)(2,1)S(1)} %get-tuple-element.58.refs_5_.refs_11_), channel_id=1, source_target_pairs={{0,3},{1,2},{2,1},{3,0},{4,7},{5,6},{6,5},{7,4},{8,11},{9,10},{10,... | collective-permute-start | bytes 98312 | tf_op jit(solution)/shard_map/ppermute | solution.py:213
  11.7 4.0 %collective-permute-start.1 = (bf16[128,128]{1,0:T(8,128)(2,1)S(1)}, bf16[128,128]{1,0:T(8,128)(2,1)S(1)}, u32[]{:S(2)}, u32[]{:S(2)}) collective-permute-start(bf16[128,128]{1,0:T(8,128)(2,1)S(1)} %get-tuple-element.58.refs_5_.refs_11_), channel_id=1, source_target_pairs={{0,2},{1,3},{2,0},{3,1},{4,6},{5,7},{6,4},{7,5},{8,10},{9,11},{10,... | collective-permute-start | bytes 98312 | tf_op jit(solution)/shard_map/ppermute | solution.py:213
  12.1 3.6 %collective-permute-start = (bf16[128,128]{1,0:T(8,128)(2,1)S(1)}, bf16[128,128]{1,0:T(8,128)(2,1)S(1)}, u32[]{:S(2)}, u32[]{:S(2)}) collective-permute-start(bf16[128,128]{1,0:T(8,128)(2,1)S(1)} %get-tuple-element.58.refs_5_.refs_11_), channel_id=1, source_target_pairs={{0,1},{1,0},{2,3},{3,2},{4,5},{5,4},{6,7},{7,6},{8,9},{9,8},{10,11... | collective-permute-start | bytes 98312 | tf_op jit(solution)/shard_map/ppermute | solution.py:213
  18.9 10.4 %all-to-all-start.1 = ((bf16[32,2,640]{2,1,0:T(2,128)(2,1)}), bf16[32,2,640]{2,1,0:T(2,128)(2,1)S(1)}, u32[]{:S(2)}, u32[]{:S(2)}) async-start(bf16[32,2,640]{2,1,0:T(2,128)(2,1)} %bitcast.4), calls=%async_computation.1 | async-start | bytes 163840 | tf_op jit(solution)/shard_map/all_to_all | solution.py:217
  21.7 3.4 %collective-permute-start.5 = (bf16[128,128]{1,0:T(8,128)(2,1)S(1)}, bf16[128,128]{1,0:T(8,128)(2,1)S(1)}, u32[]{:S(2)}, u32[]{:S(2)}) collective-permute-start(bf16[128,128]{1,0:T(8,128)(2,1)S(1)} %get-tuple-element.69.refs_5_.refs_11_), channel_id=1, source_target_pairs={{0,3},{1,2},{2,1},{3,0},{4,7},{5,6},{6,5},{7,4},{8,11},{9,10},{10,... | collective-permute-start | bytes 98312 | tf_op jit(solution)/shard_map/ppermute | solution.py:213
  23.3 4.0 %collective-permute-start.4 = (bf16[128,128]{1,0:T(8,128)(2,1)S(1)}, bf16[128,128]{1,0:T(8,128)(2,1)S(1)}, u32[]{:S(2)}, u32[]{:S(2)}) collective-permute-start(bf16[128,128]{1,0:T(8,128)(2,1)S(1)} %get-tuple-element.69.refs_5_.refs_11_), channel_id=1, source_target_pairs={{0,2},{1,3},{2,0},{3,1},{4,6},{5,7},{6,4},{7,5},{8,10},{9,11},{10,... | collective-permute-start | bytes 98312 | tf_op jit(solution)/shard_map/ppermute | solution.py:213
  23.7 3.6 %collective-permute-start.3 = (bf16[128,128]{1,0:T(8,128)(2,1)S(1)}, bf16[128,128]{1,0:T(8,128)(2,1)S(1)}, u32[]{:S(2)}, u32[]{:S(2)}) collective-permute-start(bf16[128,128]{1,0:T(8,128)(2,1)S(1)} %get-tuple-element.69.refs_5_.refs_11_), channel_id=1, source_target_pairs={{0,1},{1,0},{2,3},{3,2},{4,5},{5,4},{6,7},{7,6},{8,9},{9,8},{10,11... | collective-permute-start | bytes 98312 | tf_op jit(solution)/shard_map/ppermute | solution.py:213
  30.5 10.4 %all-to-all-start.2 = ((bf16[32,2,640]{2,1,0:T(2,128)(2,1)}), bf16[32,2,640]{2,1,0:T(2,128)(2,1)S(1)}, u32[]{:S(2)}, u32[]{:S(2)}) async-start(bf16[32,2,640]{2,1,0:T(2,128)(2,1)} %bitcast.5), calls=%async_computation.2 | async-start | bytes 163840 | tf_op jit(solution)/shard_map/all_to_all | solution.py:217
  33.3 3.4 %collective-permute-start.8 = (bf16[128,128]{1,0:T(8,128)(2,1)S(1)}, bf16[128,128]{1,0:T(8,128)(2,1)S(1)}, u32[]{:S(2)}, u32[]{:S(2)}) collective-permute-start(bf16[128,128]{1,0:T(8,128)(2,1)S(1)} %get-tuple-element.77.refs_5_.refs_11_), channel_id=1, source_target_pairs={{0,3},{1,2},{2,1},{3,0},{4,7},{5,6},{6,5},{7,4},{8,11},{9,10},{10,... | collective-permute-start | bytes 98312 | tf_op jit(solution)/shard_map/ppermute | solution.py:213
  34.9 4.0 %collective-permute-start.7 = (bf16[128,128]{1,0:T(8,128)(2,1)S(1)}, bf16[128,128]{1,0:T(8,128)(2,1)S(1)}, u32[]{:S(2)}, u32[]{:S(2)}) collective-permute-start(bf16[128,128]{1,0:T(8,128)(2,1)S(1)} %get-tuple-element.77.refs_5_.refs_11_), channel_id=1, source_target_pairs={{0,2},{1,3},{2,0},{3,1},{4,6},{5,7},{6,4},{7,5},{8,10},{9,11},{10,... | collective-permute-start | bytes 98312 | tf_op jit(solution)/shard_map/ppermute | solution.py:213
  35.3 3.6 %collective-permute-start.6 = (bf16[128,128]{1,0:T(8,128)(2,1)S(1)}, bf16[128,128]{1,0:T(8,128)(2,1)S(1)}, u32[]{:S(2)}, u32[]{:S(2)}) collective-permute-start(bf16[128,128]{1,0:T(8,128)(2,1)S(1)} %get-tuple-element.77.refs_5_.refs_11_), channel_id=1, source_target_pairs={{0,1},{1,0},{2,3},{3,2},{4,5},{5,4},{6,7},{7,6},{8,9},{9,8},{10,11... | collective-permute-start | bytes 98312 | tf_op jit(solution)/shard_map/ppermute | solution.py:213
  42.1 10.4 %all-to-all-start.3 = ((bf16[32,2,640]{2,1,0:T(2,128)(2,1)}), bf16[32,2,640]{2,1,0:T(2,128)(2,1)S(1)}, u32[]{:S(2)}, u32[]{:S(2)}) async-start(bf16[32,2,640]{2,1,0:T(2,128)(2,1)} %bitcast.6), calls=%async_computation.3 | async-start | bytes 163840 | tf_op jit(solution)/shard_map/all_to_all | solution.py:217
  44.9 3.4 %collective-permute-start.11 = (bf16[128,128]{1,0:T(8,128)(2,1)S(1)}, bf16[128,128]{1,0:T(8,128)(2,1)S(1)}, u32[]{:S(2)}, u32[]{:S(2)}) collective-permute-start(bf16[128,128]{1,0:T(8,128)(2,1)S(1)} %get-tuple-element.85.refs_5_.refs_11_), channel_id=1, source_target_pairs={{0,3},{1,2},{2,1},{3,0},{4,7},{5,6},{6,5},{7,4},{8,11},{9,10},{10,... | collective-permute-start | bytes 98312 | tf_op jit(solution)/shard_map/ppermute | solution.py:213
  46.5 4.0 %collective-permute-start.10 = (bf16[128,128]{1,0:T(8,128)(2,1)S(1)}, bf16[128,128]{1,0:T(8,128)(2,1)S(1)}, u32[]{:S(2)}, u32[]{:S(2)}) collective-permute-start(bf16[128,128]{1,0:T(8,128)(2,1)S(1)} %get-tuple-element.85.refs_5_.refs_11_), channel_id=1, source_target_pairs={{0,2},{1,3},{2,0},{3,1},{4,6},{5,7},{6,4},{7,5},{8,10},{9,11},{10,... | collective-permute-start | bytes 98312 | tf_op jit(solution)/shard_map/ppermute | solution.py:213
  46.9 3.6 %collective-permute-start.9 = (bf16[128,128]{1,0:T(8,128)(2,1)S(1)}, bf16[128,128]{1,0:T(8,128)(2,1)S(1)}, u32[]{:S(2)}, u32[]{:S(2)}) collective-permute-start(bf16[128,128]{1,0:T(8,128)(2,1)S(1)} %get-tuple-element.85.refs_5_.refs_11_), channel_id=1, source_target_pairs={{0,1},{1,0},{2,3},{3,2},{4,5},{5,4},{6,7},{7,6},{8,9},{9,8},{10,11... | collective-permute-start | bytes 98312 | tf_op jit(solution)/shard_map/ppermute | solution.py:213
  53.7 10.4 %all-to-all-start.4 = ((bf16[32,2,640]{2,1,0:T(2,128)(2,1)}), bf16[32,2,640]{2,1,0:T(2,128)(2,1)S(1)}, u32[]{:S(2)}, u32[]{:S(2)}) async-start(bf16[32,2,640]{2,1,0:T(2,128)(2,1)} %bitcast.7), calls=%async_computation.4 | async-start | bytes 163840 | tf_op jit(solution)/shard_map/all_to_all | solution.py:217
  56.5 3.4 %collective-permute-start.14 = (bf16[128,128]{1,0:T(8,128)(2,1)S(1)}, bf16[128,128]{1,0:T(8,128)(2,1)S(1)}, u32[]{:S(2)}, u32[]{:S(2)}) collective-permute-start(bf16[128,128]{1,0:T(8,128)(2,1)S(1)} %get-tuple-element.93.refs_5_), channel_id=1, source_target_pairs={{0,3},{1,2},{2,1},{3,0},{4,7},{5,6},{6,5},{7,4},{8,11},{9,10},{10,... | collective-permute-start | bytes 98312 | tf_op jit(solution)/shard_map/ppermute | solution.py:213
  58.0 4.0 %collective-permute-start.13 = (bf16[128,128]{1,0:T(8,128)(2,1)S(1)}, bf16[128,128]{1,0:T(8,128)(2,1)S(1)}, u32[]{:S(2)}, u32[]{:S(2)}) collective-permute-start(bf16[128,128]{1,0:T(8,128)(2,1)S(1)} %get-tuple-element.93.refs_5_), channel_id=1, source_target_pairs={{0,2},{1,3},{2,0},{3,1},{4,6},{5,7},{6,4},{7,5},{8,10},{9,11},{10,... | collective-permute-start | bytes 98312 | tf_op jit(solution)/shard_map/ppermute | solution.py:213
  58.4 3.6 %collective-permute-start.12 = (bf16[128,128]{1,0:T(8,128)(2,1)S(1)}, bf16[128,128]{1,0:T(8,128)(2,1)S(1)}, u32[]{:S(2)}, u32[]{:S(2)}) collective-permute-start(bf16[128,128]{1,0:T(8,128)(2,1)S(1)} %get-tuple-element.93.refs_5_), channel_id=1, source_target_pairs={{0,1},{1,0},{2,3},{3,2},{4,5},{5,4},{6,7},{7,6},{8,9},{9,8},{10,11... | collective-permute-start | bytes 98312 | tf_op jit(solution)/shard_map/ppermute | solution.py:213
  65.3 10.4 %all-to-all-start.5 = ((bf16[32,2,640]{2,1,0:T(2,128)(2,1)}), bf16[32,2,640]{2,1,0:T(2,128)(2,1)S(1)}, u32[]{:S(2)}, u32[]{:S(2)}) async-start(bf16[32,2,640]{2,1,0:T(2,128)(2,1)} %bitcast.8), calls=%async_computation.5 | async-start | bytes 163840 | tf_op jit(solution)/shard_map/all_to_all | solution.py:217
  68.1 3.4 %collective-permute-start.17 = (bf16[128,128]{1,0:T(8,128)(2,1)S(1)}, bf16[128,128]{1,0:T(8,128)(2,1)S(1)}, u32[]{:S(2)}, u32[]{:S(2)}) collective-permute-start(bf16[128,128]{1,0:T(8,128)(2,1)S(1)} %get-tuple-element.101.refs_5_), channel_id=1, source_target_pairs={{0,3},{1,2},{2,1},{3,0},{4,7},{5,6},{6,5},{7,4},{8,11},{9,10},{10,... | collective-permute-start | bytes 98312 | tf_op jit(solution)/shard_map/ppermute | solution.py:213
  69.6 4.0 %collective-permute-start.16 = (bf16[128,128]{1,0:T(8,128)(2,1)S(1)}, bf16[128,128]{1,0:T(8,128)(2,1)S(1)}, u32[]{:S(2)}, u32[]{:S(2)}) collective-permute-start(bf16[128,128]{1,0:T(8,128)(2,1)S(1)} %get-tuple-element.101.refs_5_), channel_id=1, source_target_pairs={{0,2},{1,3},{2,0},{3,1},{4,6},{5,7},{6,4},{7,5},{8,10},{9,11},{10,... | collective-permute-start | bytes 98312 | tf_op jit(solution)/shard_map/ppermute | solution.py:213
  70.0 3.6 %collective-permute-start.15 = (bf16[128,128]{1,0:T(8,128)(2,1)S(1)}, bf16[128,128]{1,0:T(8,128)(2,1)S(1)}, u32[]{:S(2)}, u32[]{:S(2)}) collective-permute-start(bf16[128,128]{1,0:T(8,128)(2,1)S(1)} %get-tuple-element.101.refs_5_), channel_id=1, source_target_pairs={{0,1},{1,0},{2,3},{3,2},{4,5},{5,4},{6,7},{7,6},{8,9},{9,8},{10,11... | collective-permute-start | bytes 98312 | tf_op jit(solution)/shard_map/ppermute | solution.py:213

commit v5 on v4

--- a/solution.py
+++ b/solution.py
@@ -42,8 +42,8 @@
             start = (tile * areas + area) * PAIR
             chunks[area, :, tile * stimuli : (tile + 1) * stimuli] = picked[start : start + PAIR]
     copies = [
-        pltpu.make_async_copy(chunks, out_ref.at[:, member], sems.at[member])
-        for member in range(out_ref.shape[1])
+        pltpu.make_async_copy(chunks, out_ref.at[member], sems.at[member])
+        for member in range(out_ref.shape[0])
     ]
     for copy in copies:
         copy.start()
@@ -113,7 +113,7 @@
             for side in range(PAIR):
                 first = side * tiles
                 count = min(tiles, senders - first)
-                rows = pl.ds((area * group + member) * PAIR + side, count, stride=chunks * PAIR)
+                rows = pl.ds((member * areas + area) * PAIR + side, count, stride=chunks * PAIR)
                 padded[rows, :] = w_long[member, pl.ds(area * senders + first, count), :]
     for part in range(padded.shape[0] // block):
         tile = padded[part * block : (part + 1) * block, :].T
@@ -178,7 +178,7 @@
     near, far = group * block, areas * group * tiles * PAIR
     shape = jax.ShapeDtypeStruct
     tile = lambda kind: shape((block, stimuli), kind)
-    sent = shape((areas, group, PAIR, tiles * stimuli), BF16)
+    sent = shape((group, areas, PAIR, tiles * stimuli), BF16)
     elder = shape((areas * tiles * PAIR, stimuli), F32)
     sending = [pltpu.VMEM((areas, PAIR, tiles * stimuli), BF16), pltpu.SemaphoreType.DMA((group,))]
     given = [
@@ -215,8 +215,8 @@
         final = iteration == STEPS - 1
         mates = [swap(past[0], bits) for bits in range(1, group)]
         received = lax.all_to_all(
-            outgoing.reshape(areas * group, PAIR, -1),
-            ("area", "nrn"),
+            outgoing.reshape(group * areas, PAIR, -1),
+            ("nrn", "area"),
             split_axis=0,
             concat_axis=0,
             tiled=True,

time: 77.1 us -> 76.9 us (level)
  waiting for transfers between devices: 33.7 us -> 32.8 us
  starting transfers between devices: 33 us -> 33.8 us
    all_to_all x6, starting transfers between devices: 21.2 us -> 22.1 us  [local(): lax.all_to_all(outgoing.reshape(group * areas, PAIR, -1), ('nrn', 'area')...]
where the time goes in v5:
time: 76.9 us; the launch traced here: 76.5 us
  starting transfers between devices  33.8 us (44%)
  waiting for transfers between devices  32.8 us (43%)
  Pallas kernels  9.15 us (12%)
  between operations  0.78 us (1%)
    all_to_all x6, starting transfers between devices, local(): lax.all_to_all(outgoing.reshape(group * areas, PAIR, -1), ('nrn', 'area')...  22.1 us
    ppermute x18, waiting for transfers between devices, local(): lax.ppermute(v, 'nrn', [(i, i ^ bits) for i in range(group)])  21.4 us
    ppermute x18, starting transfers between devices, local(): lax.ppermute(v, 'nrn', [(i, i ^ bits) for i in range(group)])  11.7 us
    all_to_all x6, waiting for transfers between devices, local(): lax.all_to_all(outgoing.reshape(group * areas, PAIR, -1), ('nrn', 'area')...  11.3 us
    pallas_call x7, Pallas kernels, call(): pl.pallas_call(kernel, out_shape=out_shape, out_specs=[HBM if len(value.s...  9.15 us
  transfers between devices with their start and end apart: 24, of which 18 were waited for; matrix products, arithmetic and copies ran while one was open for 0% of the time, Pallas kernels for 0%

profile of v5, /device:TPU:0, one launch (start us, length us, event | category | flops | bytes accessed | tf_op | source)
XLA Modules:
  0.0 76.5 jit_solution(15412199314315970248)
XLA Ops:
  0.7 2.1 %shard_map.82 = (bf16[4,8,2,640]{3,2,1,0:T(2,128)(2,1)}, bf16[384,832]{1,0:T(8,128)(2,1)S(1)}, f32[128,128]{1,0:T(8,128)S(1)}, f32[128,128]{1,0:T(8,128)S(1)}, b...) custom-call(f32[4,128,128]{2,1,0:T(8,128)} %refs_0_.1, ...), custom_call_target="tpu_custom_call" | custom-call | tf_op jit(solution)/shard_map/pallas_call | solution.py:164
  2.8 0.0 copy-start
  2.8 7.3 %all-to-all-start = ((bf16[32,2,640]{2,1,0:T(2,128)(2,1)}), bf16[32,2,640]{2,1,0:T(2,128)(2,1)S(1)}, u32[]{:S(2)}, u32[]{:S(2)}) async-start(bf16[32,2,640]{2,1,0:T(2,128)(2,1)} %bitcast.3), calls=%async_computation | async-start | bytes 163840 | tf_op jit(solution)/shard_map/all_to_all | solution.py:217
  10.1 1.6 %collective-permute-start.2 = (bf16[128,128]{1,0:T(8,128)(2,1)S(1)}, bf16[128,128]{1,0:T(8,128)(2,1)S(1)}, u32[]{:S(2)}, u32[]{:S(2)}) collective-permute-start(bf16[128,128]{1,0:T(8,128)(2,1)S(1)} %get-tuple-element.58.refs_5_.refs_11_), channel_id=1, source_target_pairs={{0,3},{1,2},{2,1},{3,0},{4,7},{5,6},{6,5},{7,4},{8,11},{9,10},{10,... | collective-permute-start | bytes 98312 | tf_op jit(solution)/shard_map/ppermute | solution.py:213
  11.7 0.4 collective-permute-start.1
  12.1 0.0 collective-permute-start
  12.1 1.5 %collective-permute-done.2.refs_8_ = bf16[128,128]{1,0:T(8,128)(2,1)S(1)} collective-permute-done((bf16[128,128]{1,0:T(8,128)(2,1)S(1)}, bf16[128,128]{1,0:T(8,128)(2,1)S(1)}, u32[]{:S(2)}, u32[]{:S(2)}) %collective-permute-start.2) | collective-permute-done | bytes 32800 | tf_op jit(solution)/shard_map/ppermute | solution.py:213
  13.5 2.1 %collective-permute-done.1.refs_7_ = bf16[128,128]{1,0:T(8,128)(2,1)S(1)} collective-permute-done((bf16[128,128]{1,0:T(8,128)(2,1)S(1)}, bf16[128,128]{1,0:T(8,128)(2,1)S(1)}, u32[]{:S(2)}, u32[]{:S(2)}) %collective-permute-start.1) | collective-permute-done | bytes 32800 | tf_op jit(solution)/shard_map/ppermute | solution.py:213
  15.7 0.0 collective-permute-done.refs_6_
  15.7 1.9 %all-to-all-done.refs_1_ = bf16[32,2,640]{2,1,0:T(2,128)(2,1)S(1)} async-done(((bf16[32,2,640]{2,1,0:T(2,128)(2,1)}), bf16[32,2,640]{2,1,0:T(2,128)(2,1)S(1)}, u32[]{:S(2)}, u32[]{:S(2)}) %all-to-all-start) | async-done | bytes 81952 | tf_op jit(solution)/shard_map/all_to_all | solution.py:217
  17.5 0.0 copy-done
  17.5 1.2 %shard_map.83 = (bf16[4,8,2,640]{3,2,1,0:T(2,128)(2,1)}, f32[128,128]{1,0:T(8,128)S(1)}, bf16[128,128]{1,0:T(8,128)(2,1)S(1)}, f32[80,128]{1,0:T(8,128)S(1)}) custom-call(bf16[384,832]{1,0:T(8,128)(2,1)S(1)} %get-tuple-element.56.refs_0_, bf16[32,2,640]{2,1,0:T(2,128)(2,1)S(1)} %all-to-all-done.refs_1_, f32[128,128]{1,0:T(8,128)S(1)} %get-tuple-element.60.refs_2_, ...), custom_call_target="tpu_custom_call" | custom-call | tf_op jit(solution)/shard_map/pallas_call | solution.py:164
  18.8 3.0 %all-to-all-start.1 = ((bf16[32,2,640]{2,1,0:T(2,128)(2,1)}), bf16[32,2,640]{2,1,0:T(2,128)(2,1)S(1)}, u32[]{:S(2)}, u32[]{:S(2)}) async-start(bf16[32,2,640]{2,1,0:T(2,128)(2,1)} %bitcast.4), calls=%async_computation.1 | async-start | bytes 163840 | tf_op jit(solution)/shard_map/all_to_all | solution.py:217
  21.7 1.6 %collective-permute-start.5 = (bf16[128,128]{1,0:T(8,128)(2,1)S(1)}, bf16[128,128]{1,0:T(8,128)(2,1)S(1)}, u32[]{:S(2)}, u32[]{:S(2)}) collective-permute-start(bf16[128,128]{1,0:T(8,128)(2,1)S(1)} %get-tuple-element.69.refs_5_.refs_11_), channel_id=1, source_target_pairs={{0,3},{1,2},{2,1},{3,0},{4,7},{5,6},{6,5},{7,4},{8,11},{9,10},{10,... | collective-permute-start | bytes 98312 | tf_op jit(solution)/shard_map/ppermute | solution.py:213
  23.3 0.4 collective-permute-start.4
  23.7 0.0 collective-permute-start.3
  23.7 1.5 %collective-permute-done.5.refs_8_ = bf16[128,128]{1,0:T(8,128)(2,1)S(1)} collective-permute-done((bf16[128,128]{1,0:T(8,128)(2,1)S(1)}, bf16[128,128]{1,0:T(8,128)(2,1)S(1)}, u32[]{:S(2)}, u32[]{:S(2)}) %collective-permute-start.5) | collective-permute-done | bytes 32800 | tf_op jit(solution)/shard_map/ppermute | solution.py:213
  25.1 2.1 %collective-permute-done.4.refs_7_ = bf16[128,128]{1,0:T(8,128)(2,1)S(1)} collective-permute-done((bf16[128,128]{1,0:T(8,128)(2,1)S(1)}, bf16[128,128]{1,0:T(8,128)(2,1)S(1)}, u32[]{:S(2)}, u32[]{:S(2)}) %collective-permute-start.4) | collective-permute-done | bytes 32800 | tf_op jit(solution)/shard_map/ppermute | solution.py:213
  27.2 0.0 collective-permute-done.3.refs_6_
  27.3 1.9 %all-to-all-done.1.refs_1_ = bf16[32,2,640]{2,1,0:T(2,128)(2,1)S(1)} async-done(((bf16[32,2,640]{2,1,0:T(2,128)(2,1)}), bf16[32,2,640]{2,1,0:T(2,128)(2,1)S(1)}, u32[]{:S(2)}, u32[]{:S(2)}) %all-to-all-start.1) | async-done | bytes 81952 | tf_op jit(solution)/shard_map/all_to_all | solution.py:217
  29.1 1.2 %shard_map.84 = (bf16[4,8,2,640]{3,2,1,0:T(2,128)(2,1)}, f32[128,128]{1,0:T(8,128)S(1)}, bf16[128,128]{1,0:T(8,128)(2,1)S(1)}, f32[80,128]{1,0:T(8,128)S(1)}) custom-call(bf16[384,832]{1,0:T(8,128)(2,1)S(1)} %get-tuple-element.56.refs_0_, bf16[32,2,640]{2,1,0:T(2,128)(2,1)S(1)} %all-to-all-done.1.refs_1_, f32[128,128]{1,0:T(8,128)S(1)} %get-tuple-element.71.refs_2_, ...), custom_call_target="tpu_custom_call" | custom-call | tf_op jit(solution)/shard_map/pallas_call | solution.py:164
  30.4 2.9 %all-to-all-start.2 = ((bf16[32,2,640]{2,1,0:T(2,128)(2,1)}), bf16[32,2,640]{2,1,0:T(2,128)(2,1)S(1)}, u32[]{:S(2)}, u32[]{:S(2)}) async-start(bf16[32,2,640]{2,1,0:T(2,128)(2,1)} %bitcast.5), calls=%async_computation.2 | async-start | bytes 163840 | tf_op jit(solution)/shard_map/all_to_all | solution.py:217
  33.3 1.6 %collective-permute-start.8 = (bf16[128,128]{1,0:T(8,128)(2,1)S(1)}, bf16[128,128]{1,0:T(8,128)(2,1)S(1)}, u32[]{:S(2)}, u32[]{:S(2)}) collective-permute-start(bf16[128,128]{1,0:T(8,128)(2,1)S(1)} %get-tuple-element.77.refs_5_.refs_11_), channel_id=1, source_target_pairs={{0,3},{1,2},{2,1},{3,0},{4,7},{5,6},{6,5},{7,4},{8,11},{9,10},{10,... | collective-permute-start | bytes 98312 | tf_op jit(solution)/shard_map/ppermute | solution.py:213
  34.9 0.4 collective-permute-start.7
  35.3 0.0 collective-permute-start.6
  35.3 1.5 %collective-permute-done.8.refs_8_ = bf16[128,128]{1,0:T(8,128)(2,1)S(1)} collective-permute-done((bf16[128,128]{1,0:T(8,128)(2,1)S(1)}, bf16[128,128]{1,0:T(8,128)(2,1)S(1)}, u32[]{:S(2)}, u32[]{:S(2)}) %collective-permute-start.8) | collective-permute-done | bytes 32800 | tf_op jit(solution)/shard_map/ppermute | solution.py:213
  36.7 2.1 %collective-permute-done.7.refs_7_ = bf16[128,128]{1,0:T(8,128)(2,1)S(1)} collective-permute-done((bf16[128,128]{1,0:T(8,128)(2,1)S(1)}, bf16[128,128]{1,0:T(8,128)(2,1)S(1)}, u32[]{:S(2)}, u32[]{:S(2)}) %collective-permute-start.7) | collective-permute-done | bytes 32800 | tf_op jit(solution)/shard_map/ppermute | solution.py:213
  38.8 0.0 collective-permute-done.6.refs_6_
  38.8 1.9 %all-to-all-done.2.refs_1_ = bf16[32,2,640]{2,1,0:T(2,128)(2,1)S(1)} async-done(((bf16[32,2,640]{2,1,0:T(2,128)(2,1)}), bf16[32,2,640]{2,1,0:T(2,128)(2,1)S(1)}, u32[]{:S(2)}, u32[]{:S(2)}) %all-to-all-start.2) | async-done | bytes 81952 | tf_op jit(solution)/shard_map/all_to_all | solution.py:217
  40.7 1.2 %shard_map.85 = (bf16[4,8,2,640]{3,2,1,0:T(2,128)(2,1)}, f32[128,128]{1,0:T(8,128)S(1)}, bf16[128,128]{1,0:T(8,128)(2,1)S(1)}, f32[80,128]{1,0:T(8,128)S(1)}) custom-call(bf16[384,832]{1,0:T(8,128)(2,1)S(1)} %get-tuple-element.56.refs_0_, bf16[32,2,640]{2,1,0:T(2,128)(2,1)S(1)} %all-to-all-done.2.refs_1_, f32[128,128]{1,0:T(8,128)S(1)} %get-tuple-element.79.refs_2_, ...), custom_call_target="tpu_custom_call" | custom-call | tf_op jit(solution)/shard_map/pallas_call | solution.py:164
  41.9 2.9 %all-to-all-start.3 = ((bf16[32,2,640]{2,1,0:T(2,128)(2,1)}), bf16[32,2,640]{2,1,0:T(2,128)(2,1)S(1)}, u32[]{:S(2)}, u32[]{:S(2)}) async-start(bf16[32,2,640]{2,1,0:T(2,128)(2,1)} %bitcast.6), calls=%async_computation.3 | async-start | bytes 163840 | tf_op jit(solution)/shard_map/all_to_all | solution.py:217
  44.9 1.6 %collective-permute-start.11 = (bf16[128,128]{1,0:T(8,128)(2,1)S(1)}, bf16[128,128]{1,0:T(8,128)(2,1)S(1)}, u32[]{:S(2)}, u32[]{:S(2)}) collective-permute-start(bf16[128,128]{1,0:T(8,128)(2,1)S(1)} %get-tuple-element.85.refs_5_.refs_11_), channel_id=1, source_target_pairs={{0,3},{1,2},{2,1},{3,0},{4,7},{5,6},{6,5},{7,4},{8,11},{9,10},{10,... | collective-permute-start | bytes 98312 | tf_op jit(solution)/shard_map/ppermute | solution.py:213
  46.5 0.4 collective-permute-start.10
  46.8 0.0 collective-permute-start.9
  46.9 1.5 %collective-permute-done.11.refs_8_ = bf16[128,128]{1,0:T(8,128)(2,1)S(1)} collective-permute-done((bf16[128,128]{1,0:T(8,128)(2,1)S(1)}, bf16[128,128]{1,0:T(8,128)(2,1)S(1)}, u32[]{:S(2)}, u32[]{:S(2)}) %collective-permute-start.11) | collective-permute-done | bytes 32800 | tf_op jit(solution)/shard_map/ppermute | solution.py:213
  48.3 2.1 %collective-permute-done.10.refs_7_ = bf16[128,128]{1,0:T(8,128)(2,1)S(1)} collective-permute-done((bf16[128,128]{1,0:T(8,128)(2,1)S(1)}, bf16[128,128]{1,0:T(8,128)(2,1)S(1)}, u32[]{:S(2)}, u32[]{:S(2)}) %collective-permute-start.10) | collective-permute-done | bytes 32800 | tf_op jit(solution)/shard_map/ppermute | solution.py:213
  50.4 0.0 collective-permute-done.9.refs_6_
  50.4 1.9 %all-to-all-done.3.refs_1_ = bf16[32,2,640]{2,1,0:T(2,128)(2,1)S(1)} async-done(((bf16[32,2,640]{2,1,0:T(2,128)(2,1)}), bf16[32,2,640]{2,1,0:T(2,128)(2,1)S(1)}, u32[]{:S(2)}, u32[]{:S(2)}) %all-to-all-start.3) | async-done | bytes 81952 | tf_op jit(solution)/shard_map/all_to_all | solution.py:217
  52.3 1.2 %shard_map.86 = (bf16[4,8,2,640]{3,2,1,0:T(2,128)(2,1)}, f32[128,128]{1,0:T(8,128)S(1)}, bf16[128,128]{1,0:T(8,128)(2,1)S(1)}, f32[80,128]{1,0:T(8,128)S(1)}) custom-call(bf16[384,832]{1,0:T(8,128)(2,1)S(1)} %get-tuple-element.56.refs_0_, bf16[32,2,640]{2,1,0:T(2,128)(2,1)S(1)} %all-to-all-done.3.refs_1_, f32[128,128]{1,0:T(8,128)S(1)} %get-tuple-element.87.refs_2_, ...), custom_call_target="tpu_custom_call" | custom-call | tf_op jit(solution)/shard_map/pallas_call | solution.py:164
  53.5 2.9 %all-to-all-start.4 = ((bf16[32,2,640]{2,1,0:T(2,128)(2,1)}), bf16[32,2,640]{2,1,0:T(2,128)(2,1)S(1)}, u32[]{:S(2)}, u32[]{:S(2)}) async-start(bf16[32,2,640]{2,1,0:T(2,128)(2,1)} %bitcast.7), calls=%async_computation.4 | async-start | bytes 163840 | tf_op jit(solution)/shard_map/all_to_all | solution.py:217
  56.5 1.6 %collective-permute-start.14 = (bf16[128,128]{1,0:T(8,128)(2,1)S(1)}, bf16[128,128]{1,0:T(8,128)(2,1)S(1)}, u32[]{:S(2)}, u32[]{:S(2)}) collective-permute-start(bf16[128,128]{1,0:T(8,128)(2,1)S(1)} %get-tuple-element.93.refs_5_), channel_id=1, source_target_pairs={{0,3},{1,2},{2,1},{3,0},{4,7},{5,6},{6,5},{7,4},{8,11},{9,10},{10,... | collective-permute-start | bytes 98312 | tf_op jit(solution)/shard_map/ppermute | solution.py:213
  58.0 0.4 collective-permute-start.13
  58.4 0.0 collective-permute-start.12
  58.4 1.5 %collective-permute-done.14.refs_8_ = bf16[128,128]{1,0:T(8,128)(2,1)S(1)} collective-permute-done((bf16[128,128]{1,0:T(8,128)(2,1)S(1)}, bf16[128,128]{1,0:T(8,128)(2,1)S(1)}, u32[]{:S(2)}, u32[]{:S(2)}) %collective-permute-start.14) | collective-permute-done | bytes 32800 | tf_op jit(solution)/shard_map/ppermute | solution.py:213
  59.9 2.1 %collective-permute-done.13.refs_7_ = bf16[128,128]{1,0:T(8,128)(2,1)S(1)} collective-permute-done((bf16[128,128]{1,0:T(8,128)(2,1)S(1)}, bf16[128,128]{1,0:T(8,128)(2,1)S(1)}, u32[]{:S(2)}, u32[]{:S(2)}) %collective-permute-start.13) | collective-permute-done | bytes 32800 | tf_op jit(solution)/shard_map/ppermute | solution.py:213
  62.0 0.0 collective-permute-done.12.refs_6_
  62.0 1.9 %all-to-all-done.4.refs_1_ = bf16[32,2,640]{2,1,0:T(2,128)(2,1)S(1)} async-done(((bf16[32,2,640]{2,1,0:T(2,128)(2,1)}), bf16[32,2,640]{2,1,0:T(2,128)(2,1)S(1)}, u32[]{:S(2)}, u32[]{:S(2)}) %all-to-all-start.4) | async-done | bytes 81952 | tf_op jit(solution)/shard_map/all_to_all | solution.py:217
  63.9 1.2 %shard_map.87 = (bf16[4,8,2,640]{3,2,1,0:T(2,128)(2,1)}, f32[128,128]{1,0:T(8,128)S(1)}, bf16[128,128]{1,0:T(8,128)(2,1)S(1)}) custom-call(bf16[384,832]{1,0:T(8,128)(2,1)S(1)} %get-tuple-element.56.refs_0_, bf16[32,2,640]{2,1,0:T(2,128)(2,1)S(1)} %all-to-all-done.4.refs_1_, f32[128,128]{1,0:T(8,128)S(1)} %get-tuple-element.95.refs_2_, ...), custom_call_target="tpu_custom_call" | custom-call | tf_op jit(solution)/shard_map/pallas_call | solution.py:164
  65.1 2.9 %all-to-all-start.5 = ((bf16[32,2,640]{2,1,0:T(2,128)(2,1)}), bf16[32,2,640]{2,1,0:T(2,128)(2,1)S(1)}, u32[]{:S(2)}, u32[]{:S(2)}) async-start(bf16[32,2,640]{2,1,0:T(2,128)(2,1)} %bitcast.8), calls=%async_computation.5 | async-start | bytes 163840 | tf_op jit(solution)/shard_map/all_to_all | solution.py:217
  68.1 1.6 %collective-permute-start.17 = (bf16[128,128]{1,0:T(8,128)(2,1)S(1)}, bf16[128,128]{1,0:T(8,128)(2,1)S(1)}, u32[]{:S(2)}, u32[]{:S(2)}) collective-permute-start(bf16[128,128]{1,0:T(8,128)(2,1)S(1)} %get-tuple-element.101.refs_5_), channel_id=1, source_target_pairs={{0,3},{1,2},{2,1},{3,0},{4,7},{5,6},{6,5},{7,4},{8,11},{9,10},{10,... | collective-permute-start | bytes 98312 | tf_op jit(solution)/shard_map/ppermute | solution.py:213
  69.6 0.4 collective-permute-start.16
  70.0 0.0 collective-permute-start.15
  70.0 1.5 %collective-permute-done.17.refs_8_ = bf16[128,128]{1,0:T(8,128)(2,1)S(1)} collective-permute-done((bf16[128,128]{1,0:T(8,128)(2,1)S(1)}, bf16[128,128]{1,0:T(8,128)(2,1)S(1)}, u32[]{:S(2)}, u32[]{:S(2)}) %collective-permute-start.17) | collective-permute-done | bytes 32800 | tf_op jit(solution)/shard_map/ppermute | solution.py:213
  71.5 2.1 %collective-permute-done.16.refs_7_ = bf16[128,128]{1,0:T(8,128)(2,1)S(1)} collective-permute-done((bf16[128,128]{1,0:T(8,128)(2,1)S(1)}, bf16[128,128]{1,0:T(8,128)(2,1)S(1)}, u32[]{:S(2)}, u32[]{:S(2)}) %collective-permute-start.16) | collective-permute-done | bytes 32800 | tf_op jit(solution)/shard_map/ppermute | solution.py:213
  73.6 0.0 collective-permute-done.15.refs_6_
  73.6 1.9 %all-to-all-done.5.refs_1_ = bf16[32,2,640]{2,1,0:T(2,128)(2,1)S(1)} async-done(((bf16[32,2,640]{2,1,0:T(2,128)(2,1)}), bf16[32,2,640]{2,1,0:T(2,128)(2,1)S(1)}, u32[]{:S(2)}, u32[]{:S(2)}) %all-to-all-start.5) | async-done | bytes 81952 | tf_op jit(solution)/shard_map/all_to_all | solution.py:217
  75.5 1.0 %shard_map.88 = f32[128,128]{1,0:T(8,128)} custom-call(bf16[384,832]{1,0:T(8,128)(2,1)S(1)} %get-tuple-element.56.refs_0_, bf16[32,2,640]{2,1,0:T(2,128)(2,1)S(1)} %all-to-all-done.5.refs_1_, f32[128,128]{1,0:T(8,128)S(1)} %get-tuple-element.103.refs_2_, f32[128,128]{1,0:T(8,128)S(1)} %copy-done, f32[128,128]{1,0:T(8,128)S(1)} %get-tuple-element.61.refs_4_, ...), custom_call_target="tpu_custom_call" | custom-call | tf_op jit(solution)/shard_map/pallas_call | solution.py:164
Async XLA Ops:
  2.8 14.8 %copy-start = (f32[128,128]{1,0:T(8,128)S(1)}, f32[128,128]{1,0:T(8,128)}, u32[]{:S(2)}) copy-start(f32[128,128]{1,0:T(8,128)} %refs_3_.11) | copy-start | bytes 196612
  2.8 14.8 %all-to-all-start = ((bf16[32,2,640]{2,1,0:T(2,128)(2,1)}), bf16[32,2,640]{2,1,0:T(2,128)(2,1)S(1)}, u32[]{:S(2)}, u32[]{:S(2)}) async-start(bf16[32,2,640]{2,1,0:T(2,128)(2,1)} %bitcast.3), calls=%async_computation | async-start | bytes 163840 | tf_op jit(solution)/shard_map/all_to_all | solution.py:217
  10.1 3.4 %collective-permute-start.2 = (bf16[128,128]{1,0:T(8,128)(2,1)S(1)}, bf16[128,128]{1,0:T(8,128)(2,1)S(1)}, u32[]{:S(2)}, u32[]{:S(2)}) collective-permute-start(bf16[128,128]{1,0:T(8,128)(2,1)S(1)} %get-tuple-element.58.refs_5_.refs_11_), channel_id=1, source_target_pairs={{0,3},{1,2},{2,1},{3,0},{4,7},{5,6},{6,5},{7,4},{8,11},{9,10},{10,... | collective-permute-start | bytes 98312 | tf_op jit(solution)/shard_map/ppermute | solution.py:213
  11.7 4.0 %collective-permute-start.1 = (bf16[128,128]{1,0:T(8,128)(2,1)S(1)}, bf16[128,128]{1,0:T(8,128)(2,1)S(1)}, u32[]{:S(2)}, u32[]{:S(2)}) collective-permute-start(bf16[128,128]{1,0:T(8,128)(2,1)S(1)} %get-tuple-element.58.refs_5_.refs_11_), channel_id=1, source_target_pairs={{0,2},{1,3},{2,0},{3,1},{4,6},{5,7},{6,4},{7,5},{8,10},{9,11},{10,... | collective-permute-start | bytes 98312 | tf_op jit(solution)/shard_map/ppermute | solution.py:213
  12.1 3.6 %collective-permute-start = (bf16[128,128]{1,0:T(8,128)(2,1)S(1)}, bf16[128,128]{1,0:T(8,128)(2,1)S(1)}, u32[]{:S(2)}, u32[]{:S(2)}) collective-permute-start(bf16[128,128]{1,0:T(8,128)(2,1)S(1)} %get-tuple-element.58.refs_5_.refs_11_), channel_id=1, source_target_pairs={{0,1},{1,0},{2,3},{3,2},{4,5},{5,4},{6,7},{7,6},{8,9},{9,8},{10,11... | collective-permute-start | bytes 98312 | tf_op jit(solution)/shard_map/ppermute | solution.py:213
  18.8 10.4 %all-to-all-start.1 = ((bf16[32,2,640]{2,1,0:T(2,128)(2,1)}), bf16[32,2,640]{2,1,0:T(2,128)(2,1)S(1)}, u32[]{:S(2)}, u32[]{:S(2)}) async-start(bf16[32,2,640]{2,1,0:T(2,128)(2,1)} %bitcast.4), calls=%async_computation.1 | async-start | bytes 163840 | tf_op jit(solution)/shard_map/all_to_all | solution.py:217
  21.7 3.4 %collective-permute-start.5 = (bf16[128,128]{1,0:T(8,128)(2,1)S(1)}, bf16[128,128]{1,0:T(8,128)(2,1)S(1)}, u32[]{:S(2)}, u32[]{:S(2)}) collective-permute-start(bf16[128,128]{1,0:T(8,128)(2,1)S(1)} %get-tuple-element.69.refs_5_.refs_11_), channel_id=1, source_target_pairs={{0,3},{1,2},{2,1},{3,0},{4,7},{5,6},{6,5},{7,4},{8,11},{9,10},{10,... | collective-permute-start | bytes 98312 | tf_op jit(solution)/shard_map/ppermute | solution.py:213
  23.3 4.0 %collective-permute-start.4 = (bf16[128,128]{1,0:T(8,128)(2,1)S(1)}, bf16[128,128]{1,0:T(8,128)(2,1)S(1)}, u32[]{:S(2)}, u32[]{:S(2)}) collective-permute-start(bf16[128,128]{1,0:T(8,128)(2,1)S(1)} %get-tuple-element.69.refs_5_.refs_11_), channel_id=1, source_target_pairs={{0,2},{1,3},{2,0},{3,1},{4,6},{5,7},{6,4},{7,5},{8,10},{9,11},{10,... | collective-permute-start | bytes 98312 | tf_op jit(solution)/shard_map/ppermute | solution.py:213
  23.7 3.6 %collective-permute-start.3 = (bf16[128,128]{1,0:T(8,128)(2,1)S(1)}, bf16[128,128]{1,0:T(8,128)(2,1)S(1)}, u32[]{:S(2)}, u32[]{:S(2)}) collective-permute-start(bf16[128,128]{1,0:T(8,128)(2,1)S(1)} %get-tuple-element.69.refs_5_.refs_11_), channel_id=1, source_target_pairs={{0,1},{1,0},{2,3},{3,2},{4,5},{5,4},{6,7},{7,6},{8,9},{9,8},{10,11... | collective-permute-start | bytes 98312 | tf_op jit(solution)/shard_map/ppermute | solution.py:213
  30.4 10.4 %all-to-all-start.2 = ((bf16[32,2,640]{2,1,0:T(2,128)(2,1)}), bf16[32,2,640]{2,1,0:T(2,128)(2,1)S(1)}, u32[]{:S(2)}, u32[]{:S(2)}) async-start(bf16[32,2,640]{2,1,0:T(2,128)(2,1)} %bitcast.5), calls=%async_computation.2 | async-start | bytes 163840 | tf_op jit(solution)/shard_map/all_to_all | solution.py:217
  33.3 3.4 %collective-permute-start.8 = (bf16[128,128]{1,0:T(8,128)(2,1)S(1)}, bf16[128,128]{1,0:T(8,128)(2,1)S(1)}, u32[]{:S(2)}, u32[]{:S(2)}) collective-permute-start(bf16[128,128]{1,0:T(8,128)(2,1)S(1)} %get-tuple-element.77.refs_5_.refs_11_), channel_id=1, source_target_pairs={{0,3},{1,2},{2,1},{3,0},{4,7},{5,6},{6,5},{7,4},{8,11},{9,10},{10,... | collective-permute-start | bytes 98312 | tf_op jit(solution)/shard_map/ppermute | solution.py:213
  34.9 4.0 %collective-permute-start.7 = (bf16[128,128]{1,0:T(8,128)(2,1)S(1)}, bf16[128,128]{1,0:T(8,128)(2,1)S(1)}, u32[]{:S(2)}, u32[]{:S(2)}) collective-permute-start(bf16[128,128]{1,0:T(8,128)(2,1)S(1)} %get-tuple-element.77.refs_5_.refs_11_), channel_id=1, source_target_pairs={{0,2},{1,3},{2,0},{3,1},{4,6},{5,7},{6,4},{7,5},{8,10},{9,11},{10,... | collective-permute-start | bytes 98312 | tf_op jit(solution)/shard_map/ppermute | solution.py:213
  35.3 3.6 %collective-permute-start.6 = (bf16[128,128]{1,0:T(8,128)(2,1)S(1)}, bf16[128,128]{1,0:T(8,128)(2,1)S(1)}, u32[]{:S(2)}, u32[]{:S(2)}) collective-permute-start(bf16[128,128]{1,0:T(8,128)(2,1)S(1)} %get-tuple-element.77.refs_5_.refs_11_), channel_id=1, source_target_pairs={{0,1},{1,0},{2,3},{3,2},{4,5},{5,4},{6,7},{7,6},{8,9},{9,8},{10,11... | collective-permute-start | bytes 98312 | tf_op jit(solution)/shard_map/ppermute | solution.py:213
  41.9 10.4 %all-to-all-start.3 = ((bf16[32,2,640]{2,1,0:T(2,128)(2,1)}), bf16[32,2,640]{2,1,0:T(2,128)(2,1)S(1)}, u32[]{:S(2)}, u32[]{:S(2)}) async-start(bf16[32,2,640]{2,1,0:T(2,128)(2,1)} %bitcast.6), calls=%async_computation.3 | async-start | bytes 163840 | tf_op jit(solution)/shard_map/all_to_all | solution.py:217
  44.9 3.4 %collective-permute-start.11 = (bf16[128,128]{1,0:T(8,128)(2,1)S(1)}, bf16[128,128]{1,0:T(8,128)(2,1)S(1)}, u32[]{:S(2)}, u32[]{:S(2)}) collective-permute-start(bf16[128,128]{1,0:T(8,128)(2,1)S(1)} %get-tuple-element.85.refs_5_.refs_11_), channel_id=1, source_target_pairs={{0,3},{1,2},{2,1},{3,0},{4,7},{5,6},{6,5},{7,4},{8,11},{9,10},{10,... | collective-permute-start | bytes 98312 | tf_op jit(solution)/shard_map/ppermute | solution.py:213
  46.5 4.0 %collective-permute-start.10 = (bf16[128,128]{1,0:T(8,128)(2,1)S(1)}, bf16[128,128]{1,0:T(8,128)(2,1)S(1)}, u32[]{:S(2)}, u32[]{:S(2)}) collective-permute-start(bf16[128,128]{1,0:T(8,128)(2,1)S(1)} %get-tuple-element.85.refs_5_.refs_11_), channel_id=1, source_target_pairs={{0,2},{1,3},{2,0},{3,1},{4,6},{5,7},{6,4},{7,5},{8,10},{9,11},{10,... | collective-permute-start | bytes 98312 | tf_op jit(solution)/shard_map/ppermute | solution.py:213
  46.8 3.6 %collective-permute-start.9 = (bf16[128,128]{1,0:T(8,128)(2,1)S(1)}, bf16[128,128]{1,0:T(8,128)(2,1)S(1)}, u32[]{:S(2)}, u32[]{:S(2)}) collective-permute-start(bf16[128,128]{1,0:T(8,128)(2,1)S(1)} %get-tuple-element.85.refs_5_.refs_11_), channel_id=1, source_target_pairs={{0,1},{1,0},{2,3},{3,2},{4,5},{5,4},{6,7},{7,6},{8,9},{9,8},{10,11... | collective-permute-start | bytes 98312 | tf_op jit(solution)/shard_map/ppermute | solution.py:213
  53.5 10.4 %all-to-all-start.4 = ((bf16[32,2,640]{2,1,0:T(2,128)(2,1)}), bf16[32,2,640]{2,1,0:T(2,128)(2,1)S(1)}, u32[]{:S(2)}, u32[]{:S(2)}) async-start(bf16[32,2,640]{2,1,0:T(2,128)(2,1)} %bitcast.7), calls=%async_computation.4 | async-start | bytes 163840 | tf_op jit(solution)/shard_map/all_to_all | solution.py:217
  56.5 3.4 %collective-permute-start.14 = (bf16[128,128]{1,0:T(8,128)(2,1)S(1)}, bf16[128,128]{1,0:T(8,128)(2,1)S(1)}, u32[]{:S(2)}, u32[]{:S(2)}) collective-permute-start(bf16[128,128]{1,0:T(8,128)(2,1)S(1)} %get-tuple-element.93.refs_5_), channel_id=1, source_target_pairs={{0,3},{1,2},{2,1},{3,0},{4,7},{5,6},{6,5},{7,4},{8,11},{9,10},{10,... | collective-permute-start | bytes 98312 | tf_op jit(solution)/shard_map/ppermute | solution.py:213
  58.0 4.0 %collective-permute-start.13 = (bf16[128,128]{1,0:T(8,128)(2,1)S(1)}, bf16[128,128]{1,0:T(8,128)(2,1)S(1)}, u32[]{:S(2)}, u32[]{:S(2)}) collective-permute-start(bf16[128,128]{1,0:T(8,128)(2,1)S(1)} %get-tuple-element.93.refs_5_), channel_id=1, source_target_pairs={{0,2},{1,3},{2,0},{3,1},{4,6},{5,7},{6,4},{7,5},{8,10},{9,11},{10,... | collective-permute-start | bytes 98312 | tf_op jit(solution)/shard_map/ppermute | solution.py:213
  58.4 3.6 %collective-permute-start.12 = (bf16[128,128]{1,0:T(8,128)(2,1)S(1)}, bf16[128,128]{1,0:T(8,128)(2,1)S(1)}, u32[]{:S(2)}, u32[]{:S(2)}) collective-permute-start(bf16[128,128]{1,0:T(8,128)(2,1)S(1)} %get-tuple-element.93.refs_5_), channel_id=1, source_target_pairs={{0,1},{1,0},{2,3},{3,2},{4,5},{5,4},{6,7},{7,6},{8,9},{9,8},{10,11... | collective-permute-start | bytes 98312 | tf_op jit(solution)/shard_map/ppermute | solution.py:213
  65.1 10.4 %all-to-all-start.5 = ((bf16[32,2,640]{2,1,0:T(2,128)(2,1)}), bf16[32,2,640]{2,1,0:T(2,128)(2,1)S(1)}, u32[]{:S(2)}, u32[]{:S(2)}) async-start(bf16[32,2,640]{2,1,0:T(2,128)(2,1)} %bitcast.8), calls=%async_computation.5 | async-start | bytes 163840 | tf_op jit(solution)/shard_map/all_to_all | solution.py:217
  68.1 3.4 %collective-permute-start.17 = (bf16[128,128]{1,0:T(8,128)(2,1)S(1)}, bf16[128,128]{1,0:T(8,128)(2,1)S(1)}, u32[]{:S(2)}, u32[]{:S(2)}) collective-permute-start(bf16[128,128]{1,0:T(8,128)(2,1)S(1)} %get-tuple-element.101.refs_5_), channel_id=1, source_target_pairs={{0,3},{1,2},{2,1},{3,0},{4,7},{5,6},{6,5},{7,4},{8,11},{9,10},{10,... | collective-permute-start | bytes 98312 | tf_op jit(solution)/shard_map/ppermute | solution.py:213
  69.6 4.0 %collective-permute-start.16 = (bf16[128,128]{1,0:T(8,128)(2,1)S(1)}, bf16[128,128]{1,0:T(8,128)(2,1)S(1)}, u32[]{:S(2)}, u32[]{:S(2)}) collective-permute-start(bf16[128,128]{1,0:T(8,128)(2,1)S(1)} %get-tuple-element.101.refs_5_), channel_id=1, source_target_pairs={{0,2},{1,3},{2,0},{3,1},{4,6},{5,7},{6,4},{7,5},{8,10},{9,11},{10,... | collective-permute-start | bytes 98312 | tf_op jit(solution)/shard_map/ppermute | solution.py:213
  70.0 3.6 %collective-permute-start.15 = (bf16[128,128]{1,0:T(8,128)(2,1)S(1)}, bf16[128,128]{1,0:T(8,128)(2,1)S(1)}, u32[]{:S(2)}, u32[]{:S(2)}) collective-permute-start(bf16[128,128]{1,0:T(8,128)(2,1)S(1)} %get-tuple-element.101.refs_5_), channel_id=1, source_target_pairs={{0,1},{1,0},{2,3},{3,2},{4,5},{5,4},{6,7},{7,6},{8,9},{9,8},{10,11... | collective-permute-start | bytes 98312 | tf_op jit(solution)/shard_map/ppermute | solution.py:213

commit v6 on v5

--- a/solution.py
+++ b/solution.py
@@ -45,8 +45,8 @@
         pltpu.make_async_copy(chunks, out_ref.at[member], sems.at[member])
         for member in range(out_ref.shape[0])
     ]
-    for copy in copies:
-        copy.start()
+    for place, copy in enumerate(copies):
+        copy.start(priority=place % 2)
     return copies
 
 

time: 76.9 us -> 76.9 us (level)
  no operation moved by 1% of the time
where the time goes in v6:
time: 76.9 us; the launch traced here: 76.5 us
  starting transfers between devices  33.8 us (44%)
  waiting for transfers between devices  32.8 us (43%)
  Pallas kernels  9.15 us (12%)
  between operations  0.78 us (1%)
    all_to_all x6, starting transfers between devices, local(): lax.all_to_all(outgoing.reshape(group * areas, PAIR, -1), ('nrn', 'area')...  22.1 us
    ppermute x18, waiting for transfers between devices, local(): lax.ppermute(v, 'nrn', [(i, i ^ bits) for i in range(group)])  21.4 us
    ppermute x18, starting transfers between devices, local(): lax.ppermute(v, 'nrn', [(i, i ^ bits) for i in range(group)])  11.7 us
    all_to_all x6, waiting for transfers between devices, local(): lax.all_to_all(outgoing.reshape(group * areas, PAIR, -1), ('nrn', 'area')...  11.3 us
    pallas_call x7, Pallas kernels, call(): pl.pallas_call(kernel, out_shape=out_shape, out_specs=[HBM if len(value.s...  9.15 us
  transfers between devices with their start and end apart: 24, of which 18 were waited for; matrix products, arithmetic and copies ran while one was open for 0% of the time, Pallas kernels for 0%

profile of v6, /device:TPU:0, one launch (start us, length us, event | category | flops | bytes accessed | tf_op | source)
XLA Modules:
  0.0 76.5 jit_solution(13659683274992193855)
XLA Ops:
  0.7 2.1 %shard_map.82 = (bf16[4,8,2,640]{3,2,1,0:T(2,128)(2,1)}, bf16[384,832]{1,0:T(8,128)(2,1)S(1)}, f32[128,128]{1,0:T(8,128)S(1)}, f32[128,128]{1,0:T(8,128)S(1)}, b...) custom-call(f32[4,128,128]{2,1,0:T(8,128)} %refs_0_.1, ...), custom_call_target="tpu_custom_call" | custom-call | tf_op jit(solution)/shard_map/pallas_call | solution.py:164
  2.8 0.0 copy-start
  2.8 7.3 %all-to-all-start = ((bf16[32,2,640]{2,1,0:T(2,128)(2,1)}), bf16[32,2,640]{2,1,0:T(2,128)(2,1)S(1)}, u32[]{:S(2)}, u32[]{:S(2)}) async-start(bf16[32,2,640]{2,1,0:T(2,128)(2,1)} %bitcast.3), calls=%async_computation | async-start | bytes 163840 | tf_op jit(solution)/shard_map/all_to_all | solution.py:217
  10.1 1.6 %collective-permute-start.2 = (bf16[128,128]{1,0:T(8,128)(2,1)S(1)}, bf16[128,128]{1,0:T(8,128)(2,1)S(1)}, u32[]{:S(2)}, u32[]{:S(2)}) collective-permute-start(bf16[128,128]{1,0:T(8,128)(2,1)S(1)} %get-tuple-element.58.refs_5_.refs_11_), channel_id=1, source_target_pairs={{0,3},{1,2},{2,1},{3,0},{4,7},{5,6},{6,5},{7,4},{8,11},{9,10},{10,... | collective-permute-start | bytes 98312 | tf_op jit(solution)/shard_map/ppermute | solution.py:213
  11.7 0.4 collective-permute-start.1
  12.1 0.0 collective-permute-start
  12.1 1.5 %collective-permute-done.2.refs_8_ = bf16[128,128]{1,0:T(8,128)(2,1)S(1)} collective-permute-done((bf16[128,128]{1,0:T(8,128)(2,1)S(1)}, bf16[128,128]{1,0:T(8,128)(2,1)S(1)}, u32[]{:S(2)}, u32[]{:S(2)}) %collective-permute-start.2) | collective-permute-done | bytes 32800 | tf_op jit(solution)/shard_map/ppermute | solution.py:213
  13.5 2.1 %collective-permute-done.1.refs_7_ = bf16[128,128]{1,0:T(8,128)(2,1)S(1)} collective-permute-done((bf16[128,128]{1,0:T(8,128)(2,1)S(1)}, bf16[128,128]{1,0:T(8,128)(2,1)S(1)}, u32[]{:S(2)}, u32[]{:S(2)}) %collective-permute-start.1) | collective-permute-done | bytes 32800 | tf_op jit(solution)/shard_map/ppermute | solution.py:213
  15.7 0.0 collective-permute-done.refs_6_
  15.7 1.9 %all-to-all-done.refs_1_ = bf16[32,2,640]{2,1,0:T(2,128)(2,1)S(1)} async-done(((bf16[32,2,640]{2,1,0:T(2,128)(2,1)}), bf16[32,2,640]{2,1,0:T(2,128)(2,1)S(1)}, u32[]{:S(2)}, u32[]{:S(2)}) %all-to-all-start) | async-done | bytes 81952 | tf_op jit(solution)/shard_map/all_to_all | solution.py:217
  17.5 0.0 copy-done
  17.5 1.2 %shard_map.83 = (bf16[4,8,2,640]{3,2,1,0:T(2,128)(2,1)}, f32[128,128]{1,0:T(8,128)S(1)}, bf16[128,128]{1,0:T(8,128)(2,1)S(1)}, f32[80,128]{1,0:T(8,128)S(1)}) custom-call(bf16[384,832]{1,0:T(8,128)(2,1)S(1)} %get-tuple-element.56.refs_0_, bf16[32,2,640]{2,1,0:T(2,128)(2,1)S(1)} %all-to-all-done.refs_1_, f32[128,128]{1,0:T(8,128)S(1)} %get-tuple-element.60.refs_2_, ...), custom_call_target="tpu_custom_call" | custom-call | tf_op jit(solution)/shard_map/pallas_call | solution.py:164
  18.8 3.0 %all-to-all-start.1 = ((bf16[32,2,640]{2,1,0:T(2,128)(2,1)}), bf16[32,2,640]{2,1,0:T(2,128)(2,1)S(1)}, u32[]{:S(2)}, u32[]{:S(2)}) async-start(bf16[32,2,640]{2,1,0:T(2,128)(2,1)} %bitcast.4), calls=%async_computation.1 | async-start | bytes 163840 | tf_op jit(solution)/shard_map/all_to_all | solution.py:217
  21.7 1.6 %collective-permute-start.5 = (bf16[128,128]{1,0:T(8,128)(2,1)S(1)}, bf16[128,128]{1,0:T(8,128)(2,1)S(1)}, u32[]{:S(2)}, u32[]{:S(2)}) collective-permute-start(bf16[128,128]{1,0:T(8,128)(2,1)S(1)} %get-tuple-element.69.refs_5_.refs_11_), channel_id=1, source_target_pairs={{0,3},{1,2},{2,1},{3,0},{4,7},{5,6},{6,5},{7,4},{8,11},{9,10},{10,... | collective-permute-start | bytes 98312 | tf_op jit(solution)/shard_map/ppermute | solution.py:213
  23.3 0.4 collective-permute-start.4
  23.7 0.0 collective-permute-start.3
  23.7 1.5 %collective-permute-done.5.refs_8_ = bf16[128,128]{1,0:T(8,128)(2,1)S(1)} collective-permute-done((bf16[128,128]{1,0:T(8,128)(2,1)S(1)}, bf16[128,128]{1,0:T(8,128)(2,1)S(1)}, u32[]{:S(2)}, u32[]{:S(2)}) %collective-permute-start.5) | collective-permute-done | bytes 32800 | tf_op jit(solution)/shard_map/ppermute | solution.py:213
  25.1 2.1 %collective-permute-done.4.refs_7_ = bf16[128,128]{1,0:T(8,128)(2,1)S(1)} collective-permute-done((bf16[128,128]{1,0:T(8,128)(2,1)S(1)}, bf16[128,128]{1,0:T(8,128)(2,1)S(1)}, u32[]{:S(2)}, u32[]{:S(2)}) %collective-permute-start.4) | collective-permute-done | bytes 32800 | tf_op jit(solution)/shard_map/ppermute | solution.py:213
  27.2 0.0 collective-permute-done.3.refs_6_
  27.3 1.9 %all-to-all-done.1.refs_1_ = bf16[32,2,640]{2,1,0:T(2,128)(2,1)S(1)} async-done(((bf16[32,2,640]{2,1,0:T(2,128)(2,1)}), bf16[32,2,640]{2,1,0:T(2,128)(2,1)S(1)}, u32[]{:S(2)}, u32[]{:S(2)}) %all-to-all-start.1) | async-done | bytes 81952 | tf_op jit(solution)/shard_map/all_to_all | solution.py:217
  29.1 1.2 %shard_map.84 = (bf16[4,8,2,640]{3,2,1,0:T(2,128)(2,1)}, f32[128,128]{1,0:T(8,128)S(1)}, bf16[128,128]{1,0:T(8,128)(2,1)S(1)}, f32[80,128]{1,0:T(8,128)S(1)}) custom-call(bf16[384,832]{1,0:T(8,128)(2,1)S(1)} %get-tuple-element.56.refs_0_, bf16[32,2,640]{2,1,0:T(2,128)(2,1)S(1)} %all-to-all-done.1.refs_1_, f32[128,128]{1,0:T(8,128)S(1)} %get-tuple-element.71.refs_2_, ...), custom_call_target="tpu_custom_call" | custom-call | tf_op jit(solution)/shard_map/pallas_call | solution.py:164
  30.4 2.9 %all-to-all-start.2 = ((bf16[32,2,640]{2,1,0:T(2,128)(2,1)}), bf16[32,2,640]{2,1,0:T(2,128)(2,1)S(1)}, u32[]{:S(2)}, u32[]{:S(2)}) async-start(bf16[32,2,640]{2,1,0:T(2,128)(2,1)} %bitcast.5), calls=%async_computation.2 | async-start | bytes 163840 | tf_op jit(solution)/shard_map/all_to_all | solution.py:217
  33.3 1.6 %collective-permute-start.8 = (bf16[128,128]{1,0:T(8,128)(2,1)S(1)}, bf16[128,128]{1,0:T(8,128)(2,1)S(1)}, u32[]{:S(2)}, u32[]{:S(2)}) collective-permute-start(bf16[128,128]{1,0:T(8,128)(2,1)S(1)} %get-tuple-element.77.refs_5_.refs_11_), channel_id=1, source_target_pairs={{0,3},{1,2},{2,1},{3,0},{4,7},{5,6},{6,5},{7,4},{8,11},{9,10},{10,... | collective-permute-start | bytes 98312 | tf_op jit(solution)/shard_map/ppermute | solution.py:213
  34.9 0.4 collective-permute-start.7
  35.3 0.0 collective-permute-start.6
  35.3 1.5 %collective-permute-done.8.refs_8_ = bf16[128,128]{1,0:T(8,128)(2,1)S(1)} collective-permute-done((bf16[128,128]{1,0:T(8,128)(2,1)S(1)}, bf16[128,128]{1,0:T(8,128)(2,1)S(1)}, u32[]{:S(2)}, u32[]{:S(2)}) %collective-permute-start.8) | collective-permute-done | bytes 32800 | tf_op jit(solution)/shard_map/ppermute | solution.py:213
  36.7 2.1 %collective-permute-done.7.refs_7_ = bf16[128,128]{1,0:T(8,128)(2,1)S(1)} collective-permute-done((bf16[128,128]{1,0:T(8,128)(2,1)S(1)}, bf16[128,128]{1,0:T(8,128)(2,1)S(1)}, u32[]{:S(2)}, u32[]{:S(2)}) %collective-permute-start.7) | collective-permute-done | bytes 32800 | tf_op jit(solution)/shard_map/ppermute | solution.py:213
  38.8 0.0 collective-permute-done.6.refs_6_
  38.8 1.9 %all-to-all-done.2.refs_1_ = bf16[32,2,640]{2,1,0:T(2,128)(2,1)S(1)} async-done(((bf16[32,2,640]{2,1,0:T(2,128)(2,1)}), bf16[32,2,640]{2,1,0:T(2,128)(2,1)S(1)}, u32[]{:S(2)}, u32[]{:S(2)}) %all-to-all-start.2) | async-done | bytes 81952 | tf_op jit(solution)/shard_map/all_to_all | solution.py:217
  40.7 1.2 %shard_map.85 = (bf16[4,8,2,640]{3,2,1,0:T(2,128)(2,1)}, f32[128,128]{1,0:T(8,128)S(1)}, bf16[128,128]{1,0:T(8,128)(2,1)S(1)}, f32[80,128]{1,0:T(8,128)S(1)}) custom-call(bf16[384,832]{1,0:T(8,128)(2,1)S(1)} %get-tuple-element.56.refs_0_, bf16[32,2,640]{2,1,0:T(2,128)(2,1)S(1)} %all-to-all-done.2.refs_1_, f32[128,128]{1,0:T(8,128)S(1)} %get-tuple-element.79.refs_2_, ...), custom_call_target="tpu_custom_call" | custom-call | tf_op jit(solution)/shard_map/pallas_call | solution.py:164
  41.9 2.9 %all-to-all-start.3 = ((bf16[32,2,640]{2,1,0:T(2,128)(2,1)}), bf16[32,2,640]{2,1,0:T(2,128)(2,1)S(1)}, u32[]{:S(2)}, u32[]{:S(2)}) async-start(bf16[32,2,640]{2,1,0:T(2,128)(2,1)} %bitcast.6), calls=%async_computation.3 | async-start | bytes 163840 | tf_op jit(solution)/shard_map/all_to_all | solution.py:217
  44.9 1.6 %collective-permute-start.11 = (bf16[128,128]{1,0:T(8,128)(2,1)S(1)}, bf16[128,128]{1,0:T(8,128)(2,1)S(1)}, u32[]{:S(2)}, u32[]{:S(2)}) collective-permute-start(bf16[128,128]{1,0:T(8,128)(2,1)S(1)} %get-tuple-element.85.refs_5_.refs_11_), channel_id=1, source_target_pairs={{0,3},{1,2},{2,1},{3,0},{4,7},{5,6},{6,5},{7,4},{8,11},{9,10},{10,... | collective-permute-start | bytes 98312 | tf_op jit(solution)/shard_map/ppermute | solution.py:213
  46.5 0.4 collective-permute-start.10
  46.8 0.0 collective-permute-start.9
  46.9 1.5 %collective-permute-done.11.refs_8_ = bf16[128,128]{1,0:T(8,128)(2,1)S(1)} collective-permute-done((bf16[128,128]{1,0:T(8,128)(2,1)S(1)}, bf16[128,128]{1,0:T(8,128)(2,1)S(1)}, u32[]{:S(2)}, u32[]{:S(2)}) %collective-permute-start.11) | collective-permute-done | bytes 32800 | tf_op jit(solution)/shard_map/ppermute | solution.py:213
  48.3 2.1 %collective-permute-done.10.refs_7_ = bf16[128,128]{1,0:T(8,128)(2,1)S(1)} collective-permute-done((bf16[128,128]{1,0:T(8,128)(2,1)S(1)}, bf16[128,128]{1,0:T(8,128)(2,1)S(1)}, u32[]{:S(2)}, u32[]{:S(2)}) %collective-permute-start.10) | collective-permute-done | bytes 32800 | tf_op jit(solution)/shard_map/ppermute | solution.py:213
  50.4 0.0 collective-permute-done.9.refs_6_
  50.4 1.9 %all-to-all-done.3.refs_1_ = bf16[32,2,640]{2,1,0:T(2,128)(2,1)S(1)} async-done(((bf16[32,2,640]{2,1,0:T(2,128)(2,1)}), bf16[32,2,640]{2,1,0:T(2,128)(2,1)S(1)}, u32[]{:S(2)}, u32[]{:S(2)}) %all-to-all-start.3) | async-done | bytes 81952 | tf_op jit(solution)/shard_map/all_to_all | solution.py:217
  52.3 1.2 %shard_map.86 = (bf16[4,8,2,640]{3,2,1,0:T(2,128)(2,1)}, f32[128,128]{1,0:T(8,128)S(1)}, bf16[128,128]{1,0:T(8,128)(2,1)S(1)}, f32[80,128]{1,0:T(8,128)S(1)}) custom-call(bf16[384,832]{1,0:T(8,128)(2,1)S(1)} %get-tuple-element.56.refs_0_, bf16[32,2,640]{2,1,0:T(2,128)(2,1)S(1)} %all-to-all-done.3.refs_1_, f32[128,128]{1,0:T(8,128)S(1)} %get-tuple-element.87.refs_2_, ...), custom_call_target="tpu_custom_call" | custom-call | tf_op jit(solution)/shard_map/pallas_call | solution.py:164
  53.5 2.9 %all-to-all-start.4 = ((bf16[32,2,640]{2,1,0:T(2,128)(2,1)}), bf16[32,2,640]{2,1,0:T(2,128)(2,1)S(1)}, u32[]{:S(2)}, u32[]{:S(2)}) async-start(bf16[32,2,640]{2,1,0:T(2,128)(2,1)} %bitcast.7), calls=%async_computation.4 | async-start | bytes 163840 | tf_op jit(solution)/shard_map/all_to_all | solution.py:217
  56.5 1.6 %collective-permute-start.14 = (bf16[128,128]{1,0:T(8,128)(2,1)S(1)}, bf16[128,128]{1,0:T(8,128)(2,1)S(1)}, u32[]{:S(2)}, u32[]{:S(2)}) collective-permute-start(bf16[128,128]{1,0:T(8,128)(2,1)S(1)} %get-tuple-element.93.refs_5_), channel_id=1, source_target_pairs={{0,3},{1,2},{2,1},{3,0},{4,7},{5,6},{6,5},{7,4},{8,11},{9,10},{10,... | collective-permute-start | bytes 98312 | tf_op jit(solution)/shard_map/ppermute | solution.py:213
  58.0 0.4 collective-permute-start.13
  58.4 0.0 collective-permute-start.12
  58.4 1.5 %collective-permute-done.14.refs_8_ = bf16[128,128]{1,0:T(8,128)(2,1)S(1)} collective-permute-done((bf16[128,128]{1,0:T(8,128)(2,1)S(1)}, bf16[128,128]{1,0:T(8,128)(2,1)S(1)}, u32[]{:S(2)}, u32[]{:S(2)}) %collective-permute-start.14) | collective-permute-done | bytes 32800 | tf_op jit(solution)/shard_map/ppermute | solution.py:213
  59.9 2.1 %collective-permute-done.13.refs_7_ = bf16[128,128]{1,0:T(8,128)(2,1)S(1)} collective-permute-done((bf16[128,128]{1,0:T(8,128)(2,1)S(1)}, bf16[128,128]{1,0:T(8,128)(2,1)S(1)}, u32[]{:S(2)}, u32[]{:S(2)}) %collective-permute-start.13) | collective-permute-done | bytes 32800 | tf_op jit(solution)/shard_map/ppermute | solution.py:213
  62.0 0.0 collective-permute-done.12.refs_6_
  62.0 1.9 %all-to-all-done.4.refs_1_ = bf16[32,2,640]{2,1,0:T(2,128)(2,1)S(1)} async-done(((bf16[32,2,640]{2,1,0:T(2,128)(2,1)}), bf16[32,2,640]{2,1,0:T(2,128)(2,1)S(1)}, u32[]{:S(2)}, u32[]{:S(2)}) %all-to-all-start.4) | async-done | bytes 81952 | tf_op jit(solution)/shard_map/all_to_all | solution.py:217
  63.9 1.2 %shard_map.87 = (bf16[4,8,2,640]{3,2,1,0:T(2,128)(2,1)}, f32[128,128]{1,0:T(8,128)S(1)}, bf16[128,128]{1,0:T(8,128)(2,1)S(1)}) custom-call(bf16[384,832]{1,0:T(8,128)(2,1)S(1)} %get-tuple-element.56.refs_0_, bf16[32,2,640]{2,1,0:T(2,128)(2,1)S(1)} %all-to-all-done.4.refs_1_, f32[128,128]{1,0:T(8,128)S(1)} %get-tuple-element.95.refs_2_, ...), custom_call_target="tpu_custom_call" | custom-call | tf_op jit(solution)/shard_map/pallas_call | solution.py:164
  65.1 2.9 %all-to-all-start.5 = ((bf16[32,2,640]{2,1,0:T(2,128)(2,1)}), bf16[32,2,640]{2,1,0:T(2,128)(2,1)S(1)}, u32[]{:S(2)}, u32[]{:S(2)}) async-start(bf16[32,2,640]{2,1,0:T(2,128)(2,1)} %bitcast.8), calls=%async_computation.5 | async-start | bytes 163840 | tf_op jit(solution)/shard_map/all_to_all | solution.py:217
  68.1 1.6 %collective-permute-start.17 = (bf16[128,128]{1,0:T(8,128)(2,1)S(1)}, bf16[128,128]{1,0:T(8,128)(2,1)S(1)}, u32[]{:S(2)}, u32[]{:S(2)}) collective-permute-start(bf16[128,128]{1,0:T(8,128)(2,1)S(1)} %get-tuple-element.101.refs_5_), channel_id=1, source_target_pairs={{0,3},{1,2},{2,1},{3,0},{4,7},{5,6},{6,5},{7,4},{8,11},{9,10},{10,... | collective-permute-start | bytes 98312 | tf_op jit(solution)/shard_map/ppermute | solution.py:213
  69.6 0.4 collective-permute-start.16
  70.0 0.0 collective-permute-start.15
  70.0 1.5 %collective-permute-done.17.refs_8_ = bf16[128,128]{1,0:T(8,128)(2,1)S(1)} collective-permute-done((bf16[128,128]{1,0:T(8,128)(2,1)S(1)}, bf16[128,128]{1,0:T(8,128)(2,1)S(1)}, u32[]{:S(2)}, u32[]{:S(2)}) %collective-permute-start.17) | collective-permute-done | bytes 32800 | tf_op jit(solution)/shard_map/ppermute | solution.py:213
  71.5 2.1 %collective-permute-done.16.refs_7_ = bf16[128,128]{1,0:T(8,128)(2,1)S(1)} collective-permute-done((bf16[128,128]{1,0:T(8,128)(2,1)S(1)}, bf16[128,128]{1,0:T(8,128)(2,1)S(1)}, u32[]{:S(2)}, u32[]{:S(2)}) %collective-permute-start.16) | collective-permute-done | bytes 32800 | tf_op jit(solution)/shard_map/ppermute | solution.py:213
  73.6 0.0 collective-permute-done.15.refs_6_
  73.6 1.9 %all-to-all-done.5.refs_1_ = bf16[32,2,640]{2,1,0:T(2,128)(2,1)S(1)} async-done(((bf16[32,2,640]{2,1,0:T(2,128)(2,1)}), bf16[32,2,640]{2,1,0:T(2,128)(2,1)S(1)}, u32[]{:S(2)}, u32[]{:S(2)}) %all-to-all-start.5) | async-done | bytes 81952 | tf_op jit(solution)/shard_map/all_to_all | solution.py:217
  75.5 1.0 %shard_map.88 = f32[128,128]{1,0:T(8,128)} custom-call(bf16[384,832]{1,0:T(8,128)(2,1)S(1)} %get-tuple-element.56.refs_0_, bf16[32,2,640]{2,1,0:T(2,128)(2,1)S(1)} %all-to-all-done.5.refs_1_, f32[128,128]{1,0:T(8,128)S(1)} %get-tuple-element.103.refs_2_, f32[128,128]{1,0:T(8,128)S(1)} %copy-done, f32[128,128]{1,0:T(8,128)S(1)} %get-tuple-element.61.refs_4_, ...), custom_call_target="tpu_custom_call" | custom-call | tf_op jit(solution)/shard_map/pallas_call | solution.py:164
Async XLA Ops:
  2.8 14.8 %copy-start = (f32[128,128]{1,0:T(8,128)S(1)}, f32[128,128]{1,0:T(8,128)}, u32[]{:S(2)}) copy-start(f32[128,128]{1,0:T(8,128)} %refs_3_.11) | copy-start | bytes 196612
  2.8 14.8 %all-to-all-start = ((bf16[32,2,640]{2,1,0:T(2,128)(2,1)}), bf16[32,2,640]{2,1,0:T(2,128)(2,1)S(1)}, u32[]{:S(2)}, u32[]{:S(2)}) async-start(bf16[32,2,640]{2,1,0:T(2,128)(2,1)} %bitcast.3), calls=%async_computation | async-start | bytes 163840 | tf_op jit(solution)/shard_map/all_to_all | solution.py:217
  10.1 3.4 %collective-permute-start.2 = (bf16[128,128]{1,0:T(8,128)(2,1)S(1)}, bf16[128,128]{1,0:T(8,128)(2,1)S(1)}, u32[]{:S(2)}, u32[]{:S(2)}) collective-permute-start(bf16[128,128]{1,0:T(8,128)(2,1)S(1)} %get-tuple-element.58.refs_5_.refs_11_), channel_id=1, source_target_pairs={{0,3},{1,2},{2,1},{3,0},{4,7},{5,6},{6,5},{7,4},{8,11},{9,10},{10,... | collective-permute-start | bytes 98312 | tf_op jit(solution)/shard_map/ppermute | solution.py:213
  11.7 4.0 %collective-permute-start.1 = (bf16[128,128]{1,0:T(8,128)(2,1)S(1)}, bf16[128,128]{1,0:T(8,128)(2,1)S(1)}, u32[]{:S(2)}, u32[]{:S(2)}) collective-permute-start(bf16[128,128]{1,0:T(8,128)(2,1)S(1)} %get-tuple-element.58.refs_5_.refs_11_), channel_id=1, source_target_pairs={{0,2},{1,3},{2,0},{3,1},{4,6},{5,7},{6,4},{7,5},{8,10},{9,11},{10,... | collective-permute-start | bytes 98312 | tf_op jit(solution)/shard_map/ppermute | solution.py:213
  12.1 3.6 %collective-permute-start = (bf16[128,128]{1,0:T(8,128)(2,1)S(1)}, bf16[128,128]{1,0:T(8,128)(2,1)S(1)}, u32[]{:S(2)}, u32[]{:S(2)}) collective-permute-start(bf16[128,128]{1,0:T(8,128)(2,1)S(1)} %get-tuple-element.58.refs_5_.refs_11_), channel_id=1, source_target_pairs={{0,1},{1,0},{2,3},{3,2},{4,5},{5,4},{6,7},{7,6},{8,9},{9,8},{10,11... | collective-permute-start | bytes 98312 | tf_op jit(solution)/shard_map/ppermute | solution.py:213
  18.8 10.4 %all-to-all-start.1 = ((bf16[32,2,640]{2,1,0:T(2,128)(2,1)}), bf16[32,2,640]{2,1,0:T(2,128)(2,1)S(1)}, u32[]{:S(2)}, u32[]{:S(2)}) async-start(bf16[32,2,640]{2,1,0:T(2,128)(2,1)} %bitcast.4), calls=%async_computation.1 | async-start | bytes 163840 | tf_op jit(solution)/shard_map/all_to_all | solution.py:217
  21.7 3.4 %collective-permute-start.5 = (bf16[128,128]{1,0:T(8,128)(2,1)S(1)}, bf16[128,128]{1,0:T(8,128)(2,1)S(1)}, u32[]{:S(2)}, u32[]{:S(2)}) collective-permute-start(bf16[128,128]{1,0:T(8,128)(2,1)S(1)} %get-tuple-element.69.refs_5_.refs_11_), channel_id=1, source_target_pairs={{0,3},{1,2},{2,1},{3,0},{4,7},{5,6},{6,5},{7,4},{8,11},{9,10},{10,... | collective-permute-start | bytes 98312 | tf_op jit(solution)/shard_map/ppermute | solution.py:213
  23.3 4.0 %collective-permute-start.4 = (bf16[128,128]{1,0:T(8,128)(2,1)S(1)}, bf16[128,128]{1,0:T(8,128)(2,1)S(1)}, u32[]{:S(2)}, u32[]{:S(2)}) collective-permute-start(bf16[128,128]{1,0:T(8,128)(2,1)S(1)} %get-tuple-element.69.refs_5_.refs_11_), channel_id=1, source_target_pairs={{0,2},{1,3},{2,0},{3,1},{4,6},{5,7},{6,4},{7,5},{8,10},{9,11},{10,... | collective-permute-start | bytes 98312 | tf_op jit(solution)/shard_map/ppermute | solution.py:213
  23.7 3.6 %collective-permute-start.3 = (bf16[128,128]{1,0:T(8,128)(2,1)S(1)}, bf16[128,128]{1,0:T(8,128)(2,1)S(1)}, u32[]{:S(2)}, u32[]{:S(2)}) collective-permute-start(bf16[128,128]{1,0:T(8,128)(2,1)S(1)} %get-tuple-element.69.refs_5_.refs_11_), channel_id=1, source_target_pairs={{0,1},{1,0},{2,3},{3,2},{4,5},{5,4},{6,7},{7,6},{8,9},{9,8},{10,11... | collective-permute-start | bytes 98312 | tf_op jit(solution)/shard_map/ppermute | solution.py:213
  30.4 10.4 %all-to-all-start.2 = ((bf16[32,2,640]{2,1,0:T(2,128)(2,1)}), bf16[32,2,640]{2,1,0:T(2,128)(2,1)S(1)}, u32[]{:S(2)}, u32[]{:S(2)}) async-start(bf16[32,2,640]{2,1,0:T(2,128)(2,1)} %bitcast.5), calls=%async_computation.2 | async-start | bytes 163840 | tf_op jit(solution)/shard_map/all_to_all | solution.py:217
  33.3 3.4 %collective-permute-start.8 = (bf16[128,128]{1,0:T(8,128)(2,1)S(1)}, bf16[128,128]{1,0:T(8,128)(2,1)S(1)}, u32[]{:S(2)}, u32[]{:S(2)}) collective-permute-start(bf16[128,128]{1,0:T(8,128)(2,1)S(1)} %get-tuple-element.77.refs_5_.refs_11_), channel_id=1, source_target_pairs={{0,3},{1,2},{2,1},{3,0},{4,7},{5,6},{6,5},{7,4},{8,11},{9,10},{10,... | collective-permute-start | bytes 98312 | tf_op jit(solution)/shard_map/ppermute | solution.py:213
  34.9 4.0 %collective-permute-start.7 = (bf16[128,128]{1,0:T(8,128)(2,1)S(1)}, bf16[128,128]{1,0:T(8,128)(2,1)S(1)}, u32[]{:S(2)}, u32[]{:S(2)}) collective-permute-start(bf16[128,128]{1,0:T(8,128)(2,1)S(1)} %get-tuple-element.77.refs_5_.refs_11_), channel_id=1, source_target_pairs={{0,2},{1,3},{2,0},{3,1},{4,6},{5,7},{6,4},{7,5},{8,10},{9,11},{10,... | collective-permute-start | bytes 98312 | tf_op jit(solution)/shard_map/ppermute | solution.py:213
  35.3 3.6 %collective-permute-start.6 = (bf16[128,128]{1,0:T(8,128)(2,1)S(1)}, bf16[128,128]{1,0:T(8,128)(2,1)S(1)}, u32[]{:S(2)}, u32[]{:S(2)}) collective-permute-start(bf16[128,128]{1,0:T(8,128)(2,1)S(1)} %get-tuple-element.77.refs_5_.refs_11_), channel_id=1, source_target_pairs={{0,1},{1,0},{2,3},{3,2},{4,5},{5,4},{6,7},{7,6},{8,9},{9,8},{10,11... | collective-permute-start | bytes 98312 | tf_op jit(solution)/shard_map/ppermute | solution.py:213
  41.9 10.4 %all-to-all-start.3 = ((bf16[32,2,640]{2,1,0:T(2,128)(2,1)}), bf16[32,2,640]{2,1,0:T(2,128)(2,1)S(1)}, u32[]{:S(2)}, u32[]{:S(2)}) async-start(bf16[32,2,640]{2,1,0:T(2,128)(2,1)} %bitcast.6), calls=%async_computation.3 | async-start | bytes 163840 | tf_op jit(solution)/shard_map/all_to_all | solution.py:217
  44.9 3.4 %collective-permute-start.11 = (bf16[128,128]{1,0:T(8,128)(2,1)S(1)}, bf16[128,128]{1,0:T(8,128)(2,1)S(1)}, u32[]{:S(2)}, u32[]{:S(2)}) collective-permute-start(bf16[128,128]{1,0:T(8,128)(2,1)S(1)} %get-tuple-element.85.refs_5_.refs_11_), channel_id=1, source_target_pairs={{0,3},{1,2},{2,1},{3,0},{4,7},{5,6},{6,5},{7,4},{8,11},{9,10},{10,... | collective-permute-start | bytes 98312 | tf_op jit(solution)/shard_map/ppermute | solution.py:213
  46.5 4.0 %collective-permute-start.10 = (bf16[128,128]{1,0:T(8,128)(2,1)S(1)}, bf16[128,128]{1,0:T(8,128)(2,1)S(1)}, u32[]{:S(2)}, u32[]{:S(2)}) collective-permute-start(bf16[128,128]{1,0:T(8,128)(2,1)S(1)} %get-tuple-element.85.refs_5_.refs_11_), channel_id=1, source_target_pairs={{0,2},{1,3},{2,0},{3,1},{4,6},{5,7},{6,4},{7,5},{8,10},{9,11},{10,... | collective-permute-start | bytes 98312 | tf_op jit(solution)/shard_map/ppermute | solution.py:213
  46.8 3.6 %collective-permute-start.9 = (bf16[128,128]{1,0:T(8,128)(2,1)S(1)}, bf16[128,128]{1,0:T(8,128)(2,1)S(1)}, u32[]{:S(2)}, u32[]{:S(2)}) collective-permute-start(bf16[128,128]{1,0:T(8,128)(2,1)S(1)} %get-tuple-element.85.refs_5_.refs_11_), channel_id=1, source_target_pairs={{0,1},{1,0},{2,3},{3,2},{4,5},{5,4},{6,7},{7,6},{8,9},{9,8},{10,11... | collective-permute-start | bytes 98312 | tf_op jit(solution)/shard_map/ppermute | solution.py:213
  53.5 10.4 %all-to-all-start.4 = ((bf16[32,2,640]{2,1,0:T(2,128)(2,1)}), bf16[32,2,640]{2,1,0:T(2,128)(2,1)S(1)}, u32[]{:S(2)}, u32[]{:S(2)}) async-start(bf16[32,2,640]{2,1,0:T(2,128)(2,1)} %bitcast.7), calls=%async_computation.4 | async-start | bytes 163840 | tf_op jit(solution)/shard_map/all_to_all | solution.py:217
  56.5 3.4 %collective-permute-start.14 = (bf16[128,128]{1,0:T(8,128)(2,1)S(1)}, bf16[128,128]{1,0:T(8,128)(2,1)S(1)}, u32[]{:S(2)}, u32[]{:S(2)}) collective-permute-start(bf16[128,128]{1,0:T(8,128)(2,1)S(1)} %get-tuple-element.93.refs_5_), channel_id=1, source_target_pairs={{0,3},{1,2},{2,1},{3,0},{4,7},{5,6},{6,5},{7,4},{8,11},{9,10},{10,... | collective-permute-start | bytes 98312 | tf_op jit(solution)/shard_map/ppermute | solution.py:213
  58.0 4.0 %collective-permute-start.13 = (bf16[128,128]{1,0:T(8,128)(2,1)S(1)}, bf16[128,128]{1,0:T(8,128)(2,1)S(1)}, u32[]{:S(2)}, u32[]{:S(2)}) collective-permute-start(bf16[128,128]{1,0:T(8,128)(2,1)S(1)} %get-tuple-element.93.refs_5_), channel_id=1, source_target_pairs={{0,2},{1,3},{2,0},{3,1},{4,6},{5,7},{6,4},{7,5},{8,10},{9,11},{10,... | collective-permute-start | bytes 98312 | tf_op jit(solution)/shard_map/ppermute | solution.py:213
  58.4 3.6 %collective-permute-start.12 = (bf16[128,128]{1,0:T(8,128)(2,1)S(1)}, bf16[128,128]{1,0:T(8,128)(2,1)S(1)}, u32[]{:S(2)}, u32[]{:S(2)}) collective-permute-start(bf16[128,128]{1,0:T(8,128)(2,1)S(1)} %get-tuple-element.93.refs_5_), channel_id=1, source_target_pairs={{0,1},{1,0},{2,3},{3,2},{4,5},{5,4},{6,7},{7,6},{8,9},{9,8},{10,11... | collective-permute-start | bytes 98312 | tf_op jit(solution)/shard_map/ppermute | solution.py:213
  65.1 10.4 %all-to-all-start.5 = ((bf16[32,2,640]{2,1,0:T(2,128)(2,1)}), bf16[32,2,640]{2,1,0:T(2,128)(2,1)S(1)}, u32[]{:S(2)}, u32[]{:S(2)}) async-start(bf16[32,2,640]{2,1,0:T(2,128)(2,1)} %bitcast.8), calls=%async_computation.5 | async-start | bytes 163840 | tf_op jit(solution)/shard_map/all_to_all | solution.py:217
  68.1 3.4 %collective-permute-start.17 = (bf16[128,128]{1,0:T(8,128)(2,1)S(1)}, bf16[128,128]{1,0:T(8,128)(2,1)S(1)}, u32[]{:S(2)}, u32[]{:S(2)}) collective-permute-start(bf16[128,128]{1,0:T(8,128)(2,1)S(1)} %get-tuple-element.101.refs_5_), channel_id=1, source_target_pairs={{0,3},{1,2},{2,1},{3,0},{4,7},{5,6},{6,5},{7,4},{8,11},{9,10},{10,... | collective-permute-start | bytes 98312 | tf_op jit(solution)/shard_map/ppermute | solution.py:213
  69.6 4.0 %collective-permute-start.16 = (bf16[128,128]{1,0:T(8,128)(2,1)S(1)}, bf16[128,128]{1,0:T(8,128)(2,1)S(1)}, u32[]{:S(2)}, u32[]{:S(2)}) collective-permute-start(bf16[128,128]{1,0:T(8,128)(2,1)S(1)} %get-tuple-element.101.refs_5_), channel_id=1, source_target_pairs={{0,2},{1,3},{2,0},{3,1},{4,6},{5,7},{6,4},{7,5},{8,10},{9,11},{10,... | collective-permute-start | bytes 98312 | tf_op jit(solution)/shard_map/ppermute | solution.py:213
  70.0 3.6 %collective-permute-start.15 = (bf16[128,128]{1,0:T(8,128)(2,1)S(1)}, bf16[128,128]{1,0:T(8,128)(2,1)S(1)}, u32[]{:S(2)}, u32[]{:S(2)}) collective-permute-start(bf16[128,128]{1,0:T(8,128)(2,1)S(1)} %get-tuple-element.101.refs_5_), channel_id=1, source_target_pairs={{0,1},{1,0},{2,3},{3,2},{4,5},{5,4},{6,7},{7,6},{8,9},{9,8},{10,11... | collective-permute-start | bytes 98312 | tf_op jit(solution)/shard_map/ppermute | solution.py:213

commit v7 on v5

--- a/solution.py
+++ b/solution.py
@@ -135,9 +135,8 @@
     for slot in range(group):
         start = pl.multiple_of((me ^ slot) * block, block)
         current[pl.ds(start, block), :] = mates[slot][...]
-    total = jnp.dot(weights[:, :near], current[...], preferred_element_type=F32)
-    sent = rows_from(received[...], state.shape[1])
-    total += jnp.dot(weights[:, near:], sent, preferred_element_type=F32)
+    current[near:, :] = rows_from(received[...], state.shape[1])
+    total = jnp.dot(weights[...], current[...], preferred_element_type=F32)
     parts = [total[term * block : (term + 1) * block] for term in range(TERMS)]
     inputs = functools.reduce(lambda a, b: a + b, reversed(parts)) + drive[...]
     old = state[...]
@@ -229,7 +228,7 @@
             [tile(F32)] if final else [sent, tile(F32), tile(BF16)] + [elder] * more,
             [weights, received, state, drive, rate, past[0], *mates]
             + picking,
-            sending * (not final) + [pltpu.VMEM((near, stimuli), BF16)],
+            sending * (not final) + [pltpu.VMEM((near + far, stimuli), BF16)],
         )
         if final:
             return result[0]

time: 76.9 us -> 77.1 us (level)
  no operation moved by 1% of the time
where the time goes in v7:
time: 77.1 us; the launch traced here: 76.6 us
  starting transfers between devices  33.8 us (44%)
  waiting for transfers between devices  32.8 us (43%)
  Pallas kernels  9.32 us (12%)
  between operations  0.78 us (1%)
    all_to_all x6, starting transfers between devices, local(): lax.all_to_all(outgoing.reshape(group * areas, PAIR, -1), ('nrn', 'area')...  22.1 us
    ppermute x18, waiting for transfers between devices, local(): lax.ppermute(v, 'nrn', [(i, i ^ bits) for i in range(group)])  21.4 us
    ppermute x18, starting transfers between devices, local(): lax.ppermute(v, 'nrn', [(i, i ^ bits) for i in range(group)])  11.7 us
    all_to_all x6, waiting for transfers between devices, local(): lax.all_to_all(outgoing.reshape(group * areas, PAIR, -1), ('nrn', 'area')...  11.3 us
    pallas_call x7, Pallas kernels, call(): pl.pallas_call(kernel, out_shape=out_shape, out_specs=[HBM if len(value.s...  9.32 us
  transfers between devices with their start and end apart: 24, of which 18 were waited for; matrix products, arithmetic and copies ran while one was open for 0% of the time, Pallas kernels for 0%

profile of v7, /device:TPU:0, one launch (start us, length us, event | category | flops | bytes accessed | tf_op | source)
XLA Modules:
  0.0 76.6 jit_solution(11924257702617124904)
XLA Ops:
  0.7 2.1 %shard_map.82 = (bf16[4,8,2,640]{3,2,1,0:T(2,128)(2,1)}, bf16[384,832]{1,0:T(8,128)(2,1)S(1)}, f32[128,128]{1,0:T(8,128)S(1)}, f32[128,128]{1,0:T(8,128)S(1)}, b...) custom-call(f32[4,128,128]{2,1,0:T(8,128)} %refs_0_.1, ...), custom_call_target="tpu_custom_call" | custom-call | tf_op jit(solution)/shard_map/pallas_call | solution.py:163
  2.8 0.0 copy-start
  2.8 7.3 %all-to-all-start = ((bf16[32,2,640]{2,1,0:T(2,128)(2,1)}), bf16[32,2,640]{2,1,0:T(2,128)(2,1)S(1)}, u32[]{:S(2)}, u32[]{:S(2)}) async-start(bf16[32,2,640]{2,1,0:T(2,128)(2,1)} %bitcast.3), calls=%async_computation | async-start | bytes 163840 | tf_op jit(solution)/shard_map/all_to_all | solution.py:216
  10.1 1.6 %collective-permute-start.2 = (bf16[128,128]{1,0:T(8,128)(2,1)S(1)}, bf16[128,128]{1,0:T(8,128)(2,1)S(1)}, u32[]{:S(2)}, u32[]{:S(2)}) collective-permute-start(bf16[128,128]{1,0:T(8,128)(2,1)S(1)} %get-tuple-element.58.refs_5_.refs_11_), channel_id=1, source_target_pairs={{0,3},{1,2},{2,1},{3,0},{4,7},{5,6},{6,5},{7,4},{8,11},{9,10},{10,... | collective-permute-start | bytes 98312 | tf_op jit(solution)/shard_map/ppermute | solution.py:212
  11.7 0.4 collective-permute-start.1
  12.1 0.0 collective-permute-start
  12.1 1.5 %collective-permute-done.2.refs_8_ = bf16[128,128]{1,0:T(8,128)(2,1)S(1)} collective-permute-done((bf16[128,128]{1,0:T(8,128)(2,1)S(1)}, bf16[128,128]{1,0:T(8,128)(2,1)S(1)}, u32[]{:S(2)}, u32[]{:S(2)}) %collective-permute-start.2) | collective-permute-done | bytes 32800 | tf_op jit(solution)/shard_map/ppermute | solution.py:212
  13.5 2.1 %collective-permute-done.1.refs_7_ = bf16[128,128]{1,0:T(8,128)(2,1)S(1)} collective-permute-done((bf16[128,128]{1,0:T(8,128)(2,1)S(1)}, bf16[128,128]{1,0:T(8,128)(2,1)S(1)}, u32[]{:S(2)}, u32[]{:S(2)}) %collective-permute-start.1) | collective-permute-done | bytes 32800 | tf_op jit(solution)/shard_map/ppermute | solution.py:212
  15.7 0.0 collective-permute-done.refs_6_
  15.7 1.9 %all-to-all-done.refs_1_ = bf16[32,2,640]{2,1,0:T(2,128)(2,1)S(1)} async-done(((bf16[32,2,640]{2,1,0:T(2,128)(2,1)}), bf16[32,2,640]{2,1,0:T(2,128)(2,1)S(1)}, u32[]{:S(2)}, u32[]{:S(2)}) %all-to-all-start) | async-done | bytes 81952 | tf_op jit(solution)/shard_map/all_to_all | solution.py:216
  17.5 0.0 copy-done
  17.5 1.2 %shard_map.83 = (bf16[4,8,2,640]{3,2,1,0:T(2,128)(2,1)}, f32[128,128]{1,0:T(8,128)S(1)}, bf16[128,128]{1,0:T(8,128)(2,1)S(1)}, f32[80,128]{1,0:T(8,128)S(1)}) custom-call(bf16[384,832]{1,0:T(8,128)(2,1)S(1)} %get-tuple-element.56.refs_0_, bf16[32,2,640]{2,1,0:T(2,128)(2,1)S(1)} %all-to-all-done.refs_1_, f32[128,128]{1,0:T(8,128)S(1)} %get-tuple-element.60.refs_2_, ...), custom_call_target="tpu_custom_call" | custom-call | tf_op jit(solution)/shard_map/pallas_call | solution.py:163
  18.8 3.0 %all-to-all-start.1 = ((bf16[32,2,640]{2,1,0:T(2,128)(2,1)}), bf16[32,2,640]{2,1,0:T(2,128)(2,1)S(1)}, u32[]{:S(2)}, u32[]{:S(2)}) async-start(bf16[32,2,640]{2,1,0:T(2,128)(2,1)} %bitcast.4), calls=%async_computation.1 | async-start | bytes 163840 | tf_op jit(solution)/shard_map/all_to_all | solution.py:216
  21.8 1.6 %collective-permute-start.5 = (bf16[128,128]{1,0:T(8,128)(2,1)S(1)}, bf16[128,128]{1,0:T(8,128)(2,1)S(1)}, u32[]{:S(2)}, u32[]{:S(2)}) collective-permute-start(bf16[128,128]{1,0:T(8,128)(2,1)S(1)} %get-tuple-element.69.refs_5_.refs_11_), channel_id=1, source_target_pairs={{0,3},{1,2},{2,1},{3,0},{4,7},{5,6},{6,5},{7,4},{8,11},{9,10},{10,... | collective-permute-start | bytes 98312 | tf_op jit(solution)/shard_map/ppermute | solution.py:212
  23.3 0.4 collective-permute-start.4
  23.7 0.0 collective-permute-start.3
  23.7 1.5 %collective-permute-done.5.refs_8_ = bf16[128,128]{1,0:T(8,128)(2,1)S(1)} collective-permute-done((bf16[128,128]{1,0:T(8,128)(2,1)S(1)}, bf16[128,128]{1,0:T(8,128)(2,1)S(1)}, u32[]{:S(2)}, u32[]{:S(2)}) %collective-permute-start.5) | collective-permute-done | bytes 32800 | tf_op jit(solution)/shard_map/ppermute | solution.py:212
  25.2 2.1 %collective-permute-done.4.refs_7_ = bf16[128,128]{1,0:T(8,128)(2,1)S(1)} collective-permute-done((bf16[128,128]{1,0:T(8,128)(2,1)S(1)}, bf16[128,128]{1,0:T(8,128)(2,1)S(1)}, u32[]{:S(2)}, u32[]{:S(2)}) %collective-permute-start.4) | collective-permute-done | bytes 32800 | tf_op jit(solution)/shard_map/ppermute | solution.py:212
  27.3 0.0 collective-permute-done.3.refs_6_
  27.3 1.9 %all-to-all-done.1.refs_1_ = bf16[32,2,640]{2,1,0:T(2,128)(2,1)S(1)} async-done(((bf16[32,2,640]{2,1,0:T(2,128)(2,1)}), bf16[32,2,640]{2,1,0:T(2,128)(2,1)S(1)}, u32[]{:S(2)}, u32[]{:S(2)}) %all-to-all-start.1) | async-done | bytes 81952 | tf_op jit(solution)/shard_map/all_to_all | solution.py:216
  29.2 1.2 %shard_map.84 = (bf16[4,8,2,640]{3,2,1,0:T(2,128)(2,1)}, f32[128,128]{1,0:T(8,128)S(1)}, bf16[128,128]{1,0:T(8,128)(2,1)S(1)}, f32[80,128]{1,0:T(8,128)S(1)}) custom-call(bf16[384,832]{1,0:T(8,128)(2,1)S(1)} %get-tuple-element.56.refs_0_, bf16[32,2,640]{2,1,0:T(2,128)(2,1)S(1)} %all-to-all-done.1.refs_1_, f32[128,128]{1,0:T(8,128)S(1)} %get-tuple-element.71.refs_2_, ...), custom_call_target="tpu_custom_call" | custom-call | tf_op jit(solution)/shard_map/pallas_call | solution.py:163
  30.4 2.9 %all-to-all-start.2 = ((bf16[32,2,640]{2,1,0:T(2,128)(2,1)}), bf16[32,2,640]{2,1,0:T(2,128)(2,1)S(1)}, u32[]{:S(2)}, u32[]{:S(2)}) async-start(bf16[32,2,640]{2,1,0:T(2,128)(2,1)} %bitcast.5), calls=%async_computation.2 | async-start | bytes 163840 | tf_op jit(solution)/shard_map/all_to_all | solution.py:216
  33.4 1.6 %collective-permute-start.8 = (bf16[128,128]{1,0:T(8,128)(2,1)S(1)}, bf16[128,128]{1,0:T(8,128)(2,1)S(1)}, u32[]{:S(2)}, u32[]{:S(2)}) collective-permute-start(bf16[128,128]{1,0:T(8,128)(2,1)S(1)} %get-tuple-element.77.refs_5_.refs_11_), channel_id=1, source_target_pairs={{0,3},{1,2},{2,1},{3,0},{4,7},{5,6},{6,5},{7,4},{8,11},{9,10},{10,... | collective-permute-start | bytes 98312 | tf_op jit(solution)/shard_map/ppermute | solution.py:212
  34.9 0.4 collective-permute-start.7
  35.3 0.0 collective-permute-start.6
  35.3 1.5 %collective-permute-done.8.refs_8_ = bf16[128,128]{1,0:T(8,128)(2,1)S(1)} collective-permute-done((bf16[128,128]{1,0:T(8,128)(2,1)S(1)}, bf16[128,128]{1,0:T(8,128)(2,1)S(1)}, u32[]{:S(2)}, u32[]{:S(2)}) %collective-permute-start.8) | collective-permute-done | bytes 32800 | tf_op jit(solution)/shard_map/ppermute | solution.py:212
  36.8 2.1 %collective-permute-done.7.refs_7_ = bf16[128,128]{1,0:T(8,128)(2,1)S(1)} collective-permute-done((bf16[128,128]{1,0:T(8,128)(2,1)S(1)}, bf16[128,128]{1,0:T(8,128)(2,1)S(1)}, u32[]{:S(2)}, u32[]{:S(2)}) %collective-permute-start.7) | collective-permute-done | bytes 32800 | tf_op jit(solution)/shard_map/ppermute | solution.py:212
  38.9 0.0 collective-permute-done.6.refs_6_
  38.9 1.9 %all-to-all-done.2.refs_1_ = bf16[32,2,640]{2,1,0:T(2,128)(2,1)S(1)} async-done(((bf16[32,2,640]{2,1,0:T(2,128)(2,1)}), bf16[32,2,640]{2,1,0:T(2,128)(2,1)S(1)}, u32[]{:S(2)}, u32[]{:S(2)}) %all-to-all-start.2) | async-done | bytes 81952 | tf_op jit(solution)/shard_map/all_to_all | solution.py:216
  40.8 1.2 %shard_map.85 = (bf16[4,8,2,640]{3,2,1,0:T(2,128)(2,1)}, f32[128,128]{1,0:T(8,128)S(1)}, bf16[128,128]{1,0:T(8,128)(2,1)S(1)}, f32[80,128]{1,0:T(8,128)S(1)}) custom-call(bf16[384,832]{1,0:T(8,128)(2,1)S(1)} %get-tuple-element.56.refs_0_, bf16[32,2,640]{2,1,0:T(2,128)(2,1)S(1)} %all-to-all-done.2.refs_1_, f32[128,128]{1,0:T(8,128)S(1)} %get-tuple-element.79.refs_2_, ...), custom_call_target="tpu_custom_call" | custom-call | tf_op jit(solution)/shard_map/pallas_call | solution.py:163
  42.0 2.9 %all-to-all-start.3 = ((bf16[32,2,640]{2,1,0:T(2,128)(2,1)}), bf16[32,2,640]{2,1,0:T(2,128)(2,1)S(1)}, u32[]{:S(2)}, u32[]{:S(2)}) async-start(bf16[32,2,640]{2,1,0:T(2,128)(2,1)} %bitcast.6), calls=%async_computation.3 | async-start | bytes 163840 | tf_op jit(solution)/shard_map/all_to_all | solution.py:216
  45.0 1.6 %collective-permute-start.11 = (bf16[128,128]{1,0:T(8,128)(2,1)S(1)}, bf16[128,128]{1,0:T(8,128)(2,1)S(1)}, u32[]{:S(2)}, u32[]{:S(2)}) collective-permute-start(bf16[128,128]{1,0:T(8,128)(2,1)S(1)} %get-tuple-element.85.refs_5_.refs_11_), channel_id=1, source_target_pairs={{0,3},{1,2},{2,1},{3,0},{4,7},{5,6},{6,5},{7,4},{8,11},{9,10},{10,... | collective-permute-start | bytes 98312 | tf_op jit(solution)/shard_map/ppermute | solution.py:212
  46.6 0.4 collective-permute-start.10
  47.0 0.0 collective-permute-start.9
  47.0 1.5 %collective-permute-done.11.refs_8_ = bf16[128,128]{1,0:T(8,128)(2,1)S(1)} collective-permute-done((bf16[128,128]{1,0:T(8,128)(2,1)S(1)}, bf16[128,128]{1,0:T(8,128)(2,1)S(1)}, u32[]{:S(2)}, u32[]{:S(2)}) %collective-permute-start.11) | collective-permute-done | bytes 32800 | tf_op jit(solution)/shard_map/ppermute | solution.py:212
  48.4 2.1 %collective-permute-done.10.refs_7_ = bf16[128,128]{1,0:T(8,128)(2,1)S(1)} collective-permute-done((bf16[128,128]{1,0:T(8,128)(2,1)S(1)}, bf16[128,128]{1,0:T(8,128)(2,1)S(1)}, u32[]{:S(2)}, u32[]{:S(2)}) %collective-permute-start.10) | collective-permute-done | bytes 32800 | tf_op jit(solution)/shard_map/ppermute | solution.py:212
  50.5 0.0 collective-permute-done.9.refs_6_
  50.5 1.9 %all-to-all-done.3.refs_1_ = bf16[32,2,640]{2,1,0:T(2,128)(2,1)S(1)} async-done(((bf16[32,2,640]{2,1,0:T(2,128)(2,1)}), bf16[32,2,640]{2,1,0:T(2,128)(2,1)S(1)}, u32[]{:S(2)}, u32[]{:S(2)}) %all-to-all-start.3) | async-done | bytes 81952 | tf_op jit(solution)/shard_map/all_to_all | solution.py:216
  52.4 1.2 %shard_map.86 = (bf16[4,8,2,640]{3,2,1,0:T(2,128)(2,1)}, f32[128,128]{1,0:T(8,128)S(1)}, bf16[128,128]{1,0:T(8,128)(2,1)S(1)}, f32[80,128]{1,0:T(8,128)S(1)}) custom-call(bf16[384,832]{1,0:T(8,128)(2,1)S(1)} %get-tuple-element.56.refs_0_, bf16[32,2,640]{2,1,0:T(2,128)(2,1)S(1)} %all-to-all-done.3.refs_1_, f32[128,128]{1,0:T(8,128)S(1)} %get-tuple-element.87.refs_2_, ...), custom_call_target="tpu_custom_call" | custom-call | tf_op jit(solution)/shard_map/pallas_call | solution.py:163
  53.7 2.9 %all-to-all-start.4 = ((bf16[32,2,640]{2,1,0:T(2,128)(2,1)}), bf16[32,2,640]{2,1,0:T(2,128)(2,1)S(1)}, u32[]{:S(2)}, u32[]{:S(2)}) async-start(bf16[32,2,640]{2,1,0:T(2,128)(2,1)} %bitcast.7), calls=%async_computation.4 | async-start | bytes 163840 | tf_op jit(solution)/shard_map/all_to_all | solution.py:216
  56.6 1.6 %collective-permute-start.14 = (bf16[128,128]{1,0:T(8,128)(2,1)S(1)}, bf16[128,128]{1,0:T(8,128)(2,1)S(1)}, u32[]{:S(2)}, u32[]{:S(2)}) collective-permute-start(bf16[128,128]{1,0:T(8,128)(2,1)S(1)} %get-tuple-element.93.refs_5_), channel_id=1, source_target_pairs={{0,3},{1,2},{2,1},{3,0},{4,7},{5,6},{6,5},{7,4},{8,11},{9,10},{10,... | collective-permute-start | bytes 98312 | tf_op jit(solution)/shard_map/ppermute | solution.py:212
  58.2 0.4 collective-permute-start.13
  58.6 0.0 collective-permute-start.12
  58.6 1.5 %collective-permute-done.14.refs_8_ = bf16[128,128]{1,0:T(8,128)(2,1)S(1)} collective-permute-done((bf16[128,128]{1,0:T(8,128)(2,1)S(1)}, bf16[128,128]{1,0:T(8,128)(2,1)S(1)}, u32[]{:S(2)}, u32[]{:S(2)}) %collective-permute-start.14) | collective-permute-done | bytes 32800 | tf_op jit(solution)/shard_map/ppermute | solution.py:212
  60.0 2.1 %collective-permute-done.13.refs_7_ = bf16[128,128]{1,0:T(8,128)(2,1)S(1)} collective-permute-done((bf16[128,128]{1,0:T(8,128)(2,1)S(1)}, bf16[128,128]{1,0:T(8,128)(2,1)S(1)}, u32[]{:S(2)}, u32[]{:S(2)}) %collective-permute-start.13) | collective-permute-done | bytes 32800 | tf_op jit(solution)/shard_map/ppermute | solution.py:212
  62.1 0.0 collective-permute-done.12.refs_6_
  62.1 1.9 %all-to-all-done.4.refs_1_ = bf16[32,2,640]{2,1,0:T(2,128)(2,1)S(1)} async-done(((bf16[32,2,640]{2,1,0:T(2,128)(2,1)}), bf16[32,2,640]{2,1,0:T(2,128)(2,1)S(1)}, u32[]{:S(2)}, u32[]{:S(2)}) %all-to-all-start.4) | async-done | bytes 81952 | tf_op jit(solution)/shard_map/all_to_all | solution.py:216
  64.0 1.2 %shard_map.87 = (bf16[4,8,2,640]{3,2,1,0:T(2,128)(2,1)}, f32[128,128]{1,0:T(8,128)S(1)}, bf16[128,128]{1,0:T(8,128)(2,1)S(1)}) custom-call(bf16[384,832]{1,0:T(8,128)(2,1)S(1)} %get-tuple-element.56.refs_0_, bf16[32,2,640]{2,1,0:T(2,128)(2,1)S(1)} %all-to-all-done.4.refs_1_, f32[128,128]{1,0:T(8,128)S(1)} %get-tuple-element.95.refs_2_, ...), custom_call_target="tpu_custom_call" | custom-call | tf_op jit(solution)/shard_map/pallas_call | solution.py:163
  65.3 2.9 %all-to-all-start.5 = ((bf16[32,2,640]{2,1,0:T(2,128)(2,1)}), bf16[32,2,640]{2,1,0:T(2,128)(2,1)S(1)}, u32[]{:S(2)}, u32[]{:S(2)}) async-start(bf16[32,2,640]{2,1,0:T(2,128)(2,1)} %bitcast.8), calls=%async_computation.5 | async-start | bytes 163840 | tf_op jit(solution)/shard_map/all_to_all | solution.py:216
  68.2 1.6 %collective-permute-start.17 = (bf16[128,128]{1,0:T(8,128)(2,1)S(1)}, bf16[128,128]{1,0:T(8,128)(2,1)S(1)}, u32[]{:S(2)}, u32[]{:S(2)}) collective-permute-start(bf16[128,128]{1,0:T(8,128)(2,1)S(1)} %get-tuple-element.101.refs_5_), channel_id=1, source_target_pairs={{0,3},{1,2},{2,1},{3,0},{4,7},{5,6},{6,5},{7,4},{8,11},{9,10},{10,... | collective-permute-start | bytes 98312 | tf_op jit(solution)/shard_map/ppermute | solution.py:212
  69.8 0.4 collective-permute-start.16
  70.2 0.0 collective-permute-start.15
  70.2 1.5 %collective-permute-done.17.refs_8_ = bf16[128,128]{1,0:T(8,128)(2,1)S(1)} collective-permute-done((bf16[128,128]{1,0:T(8,128)(2,1)S(1)}, bf16[128,128]{1,0:T(8,128)(2,1)S(1)}, u32[]{:S(2)}, u32[]{:S(2)}) %collective-permute-start.17) | collective-permute-done | bytes 32800 | tf_op jit(solution)/shard_map/ppermute | solution.py:212
  71.6 2.1 %collective-permute-done.16.refs_7_ = bf16[128,128]{1,0:T(8,128)(2,1)S(1)} collective-permute-done((bf16[128,128]{1,0:T(8,128)(2,1)S(1)}, bf16[128,128]{1,0:T(8,128)(2,1)S(1)}, u32[]{:S(2)}, u32[]{:S(2)}) %collective-permute-start.16) | collective-permute-done | bytes 32800 | tf_op jit(solution)/shard_map/ppermute | solution.py:212
  73.7 0.0 collective-permute-done.15.refs_6_
  73.7 1.9 %all-to-all-done.5.refs_1_ = bf16[32,2,640]{2,1,0:T(2,128)(2,1)S(1)} async-done(((bf16[32,2,640]{2,1,0:T(2,128)(2,1)}), bf16[32,2,640]{2,1,0:T(2,128)(2,1)S(1)}, u32[]{:S(2)}, u32[]{:S(2)}) %all-to-all-start.5) | async-done | bytes 81952 | tf_op jit(solution)/shard_map/all_to_all | solution.py:216
  75.6 1.0 %shard_map.88 = f32[128,128]{1,0:T(8,128)} custom-call(bf16[384,832]{1,0:T(8,128)(2,1)S(1)} %get-tuple-element.56.refs_0_, bf16[32,2,640]{2,1,0:T(2,128)(2,1)S(1)} %all-to-all-done.5.refs_1_, f32[128,128]{1,0:T(8,128)S(1)} %get-tuple-element.103.refs_2_, f32[128,128]{1,0:T(8,128)S(1)} %copy-done, f32[128,128]{1,0:T(8,128)S(1)} %get-tuple-element.61.refs_4_, ...), custom_call_target="tpu_custom_call" | custom-call | tf_op jit(solution)/shard_map/pallas_call | solution.py:163
Async XLA Ops:
  2.8 14.8 %copy-start = (f32[128,128]{1,0:T(8,128)S(1)}, f32[128,128]{1,0:T(8,128)}, u32[]{:S(2)}) copy-start(f32[128,128]{1,0:T(8,128)} %refs_3_.11) | copy-start | bytes 196612
  2.8 14.8 %all-to-all-start = ((bf16[32,2,640]{2,1,0:T(2,128)(2,1)}), bf16[32,2,640]{2,1,0:T(2,128)(2,1)S(1)}, u32[]{:S(2)}, u32[]{:S(2)}) async-start(bf16[32,2,640]{2,1,0:T(2,128)(2,1)} %bitcast.3), calls=%async_computation | async-start | bytes 163840 | tf_op jit(solution)/shard_map/all_to_all | solution.py:216
  10.1 3.4 %collective-permute-start.2 = (bf16[128,128]{1,0:T(8,128)(2,1)S(1)}, bf16[128,128]{1,0:T(8,128)(2,1)S(1)}, u32[]{:S(2)}, u32[]{:S(2)}) collective-permute-start(bf16[128,128]{1,0:T(8,128)(2,1)S(1)} %get-tuple-element.58.refs_5_.refs_11_), channel_id=1, source_target_pairs={{0,3},{1,2},{2,1},{3,0},{4,7},{5,6},{6,5},{7,4},{8,11},{9,10},{10,... | collective-permute-start | bytes 98312 | tf_op jit(solution)/shard_map/ppermute | solution.py:212
  11.7 4.0 %collective-permute-start.1 = (bf16[128,128]{1,0:T(8,128)(2,1)S(1)}, bf16[128,128]{1,0:T(8,128)(2,1)S(1)}, u32[]{:S(2)}, u32[]{:S(2)}) collective-permute-start(bf16[128,128]{1,0:T(8,128)(2,1)S(1)} %get-tuple-element.58.refs_5_.refs_11_), channel_id=1, source_target_pairs={{0,2},{1,3},{2,0},{3,1},{4,6},{5,7},{6,4},{7,5},{8,10},{9,11},{10,... | collective-permute-start | bytes 98312 | tf_op jit(solution)/shard_map/ppermute | solution.py:212
  12.1 3.6 %collective-permute-start = (bf16[128,128]{1,0:T(8,128)(2,1)S(1)}, bf16[128,128]{1,0:T(8,128)(2,1)S(1)}, u32[]{:S(2)}, u32[]{:S(2)}) collective-permute-start(bf16[128,128]{1,0:T(8,128)(2,1)S(1)} %get-tuple-element.58.refs_5_.refs_11_), channel_id=1, source_target_pairs={{0,1},{1,0},{2,3},{3,2},{4,5},{5,4},{6,7},{7,6},{8,9},{9,8},{10,11... | collective-permute-start | bytes 98312 | tf_op jit(solution)/shard_map/ppermute | solution.py:212
  18.8 10.4 %all-to-all-start.1 = ((bf16[32,2,640]{2,1,0:T(2,128)(2,1)}), bf16[32,2,640]{2,1,0:T(2,128)(2,1)S(1)}, u32[]{:S(2)}, u32[]{:S(2)}) async-start(bf16[32,2,640]{2,1,0:T(2,128)(2,1)} %bitcast.4), calls=%async_computation.1 | async-start | bytes 163840 | tf_op jit(solution)/shard_map/all_to_all | solution.py:216
  21.8 3.4 %collective-permute-start.5 = (bf16[128,128]{1,0:T(8,128)(2,1)S(1)}, bf16[128,128]{1,0:T(8,128)(2,1)S(1)}, u32[]{:S(2)}, u32[]{:S(2)}) collective-permute-start(bf16[128,128]{1,0:T(8,128)(2,1)S(1)} %get-tuple-element.69.refs_5_.refs_11_), channel_id=1, source_target_pairs={{0,3},{1,2},{2,1},{3,0},{4,7},{5,6},{6,5},{7,4},{8,11},{9,10},{10,... | collective-permute-start | bytes 98312 | tf_op jit(solution)/shard_map/ppermute | solution.py:212
  23.3 4.0 %collective-permute-start.4 = (bf16[128,128]{1,0:T(8,128)(2,1)S(1)}, bf16[128,128]{1,0:T(8,128)(2,1)S(1)}, u32[]{:S(2)}, u32[]{:S(2)}) collective-permute-start(bf16[128,128]{1,0:T(8,128)(2,1)S(1)} %get-tuple-element.69.refs_5_.refs_11_), channel_id=1, source_target_pairs={{0,2},{1,3},{2,0},{3,1},{4,6},{5,7},{6,4},{7,5},{8,10},{9,11},{10,... | collective-permute-start | bytes 98312 | tf_op jit(solution)/shard_map/ppermute | solution.py:212
  23.7 3.6 %collective-permute-start.3 = (bf16[128,128]{1,0:T(8,128)(2,1)S(1)}, bf16[128,128]{1,0:T(8,128)(2,1)S(1)}, u32[]{:S(2)}, u32[]{:S(2)}) collective-permute-start(bf16[128,128]{1,0:T(8,128)(2,1)S(1)} %get-tuple-element.69.refs_5_.refs_11_), channel_id=1, source_target_pairs={{0,1},{1,0},{2,3},{3,2},{4,5},{5,4},{6,7},{7,6},{8,9},{9,8},{10,11... | collective-permute-start | bytes 98312 | tf_op jit(solution)/shard_map/ppermute | solution.py:212
  30.4 10.4 %all-to-all-start.2 = ((bf16[32,2,640]{2,1,0:T(2,128)(2,1)}), bf16[32,2,640]{2,1,0:T(2,128)(2,1)S(1)}, u32[]{:S(2)}, u32[]{:S(2)}) async-start(bf16[32,2,640]{2,1,0:T(2,128)(2,1)} %bitcast.5), calls=%async_computation.2 | async-start | bytes 163840 | tf_op jit(solution)/shard_map/all_to_all | solution.py:216
  33.4 3.4 %collective-permute-start.8 = (bf16[128,128]{1,0:T(8,128)(2,1)S(1)}, bf16[128,128]{1,0:T(8,128)(2,1)S(1)}, u32[]{:S(2)}, u32[]{:S(2)}) collective-permute-start(bf16[128,128]{1,0:T(8,128)(2,1)S(1)} %get-tuple-element.77.refs_5_.refs_11_), channel_id=1, source_target_pairs={{0,3},{1,2},{2,1},{3,0},{4,7},{5,6},{6,5},{7,4},{8,11},{9,10},{10,... | collective-permute-start | bytes 98312 | tf_op jit(solution)/shard_map/ppermute | solution.py:212
  34.9 4.0 %collective-permute-start.7 = (bf16[128,128]{1,0:T(8,128)(2,1)S(1)}, bf16[128,128]{1,0:T(8,128)(2,1)S(1)}, u32[]{:S(2)}, u32[]{:S(2)}) collective-permute-start(bf16[128,128]{1,0:T(8,128)(2,1)S(1)} %get-tuple-element.77.refs_5_.refs_11_), channel_id=1, source_target_pairs={{0,2},{1,3},{2,0},{3,1},{4,6},{5,7},{6,4},{7,5},{8,10},{9,11},{10,... | collective-permute-start | bytes 98312 | tf_op jit(solution)/shard_map/ppermute | solution.py:212
  35.3 3.6 %collective-permute-start.6 = (bf16[128,128]{1,0:T(8,128)(2,1)S(1)}, bf16[128,128]{1,0:T(8,128)(2,1)S(1)}, u32[]{:S(2)}, u32[]{:S(2)}) collective-permute-start(bf16[128,128]{1,0:T(8,128)(2,1)S(1)} %get-tuple-element.77.refs_5_.refs_11_), channel_id=1, source_target_pairs={{0,1},{1,0},{2,3},{3,2},{4,5},{5,4},{6,7},{7,6},{8,9},{9,8},{10,11... | collective-permute-start | bytes 98312 | tf_op jit(solution)/shard_map/ppermute | solution.py:212
  42.0 10.4 %all-to-all-start.3 = ((bf16[32,2,640]{2,1,0:T(2,128)(2,1)}), bf16[32,2,640]{2,1,0:T(2,128)(2,1)S(1)}, u32[]{:S(2)}, u32[]{:S(2)}) async-start(bf16[32,2,640]{2,1,0:T(2,128)(2,1)} %bitcast.6), calls=%async_computation.3 | async-start | bytes 163840 | tf_op jit(solution)/shard_map/all_to_all | solution.py:216
  45.0 3.4 %collective-permute-start.11 = (bf16[128,128]{1,0:T(8,128)(2,1)S(1)}, bf16[128,128]{1,0:T(8,128)(2,1)S(1)}, u32[]{:S(2)}, u32[]{:S(2)}) collective-permute-start(bf16[128,128]{1,0:T(8,128)(2,1)S(1)} %get-tuple-element.85.refs_5_.refs_11_), channel_id=1, source_target_pairs={{0,3},{1,2},{2,1},{3,0},{4,7},{5,6},{6,5},{7,4},{8,11},{9,10},{10,... | collective-permute-start | bytes 98312 | tf_op jit(solution)/shard_map/ppermute | solution.py:212
  46.6 4.0 %collective-permute-start.10 = (bf16[128,128]{1,0:T(8,128)(2,1)S(1)}, bf16[128,128]{1,0:T(8,128)(2,1)S(1)}, u32[]{:S(2)}, u32[]{:S(2)}) collective-permute-start(bf16[128,128]{1,0:T(8,128)(2,1)S(1)} %get-tuple-element.85.refs_5_.refs_11_), channel_id=1, source_target_pairs={{0,2},{1,3},{2,0},{3,1},{4,6},{5,7},{6,4},{7,5},{8,10},{9,11},{10,... | collective-permute-start | bytes 98312 | tf_op jit(solution)/shard_map/ppermute | solution.py:212
  47.0 3.6 %collective-permute-start.9 = (bf16[128,128]{1,0:T(8,128)(2,1)S(1)}, bf16[128,128]{1,0:T(8,128)(2,1)S(1)}, u32[]{:S(2)}, u32[]{:S(2)}) collective-permute-start(bf16[128,128]{1,0:T(8,128)(2,1)S(1)} %get-tuple-element.85.refs_5_.refs_11_), channel_id=1, source_target_pairs={{0,1},{1,0},{2,3},{3,2},{4,5},{5,4},{6,7},{7,6},{8,9},{9,8},{10,11... | collective-permute-start | bytes 98312 | tf_op jit(solution)/shard_map/ppermute | solution.py:212
  53.7 10.4 %all-to-all-start.4 = ((bf16[32,2,640]{2,1,0:T(2,128)(2,1)}), bf16[32,2,640]{2,1,0:T(2,128)(2,1)S(1)}, u32[]{:S(2)}, u32[]{:S(2)}) async-start(bf16[32,2,640]{2,1,0:T(2,128)(2,1)} %bitcast.7), calls=%async_computation.4 | async-start | bytes 163840 | tf_op jit(solution)/shard_map/all_to_all | solution.py:216
  56.6 3.4 %collective-permute-start.14 = (bf16[128,128]{1,0:T(8,128)(2,1)S(1)}, bf16[128,128]{1,0:T(8,128)(2,1)S(1)}, u32[]{:S(2)}, u32[]{:S(2)}) collective-permute-start(bf16[128,128]{1,0:T(8,128)(2,1)S(1)} %get-tuple-element.93.refs_5_), channel_id=1, source_target_pairs={{0,3},{1,2},{2,1},{3,0},{4,7},{5,6},{6,5},{7,4},{8,11},{9,10},{10,... | collective-permute-start | bytes 98312 | tf_op jit(solution)/shard_map/ppermute | solution.py:212
  58.2 4.0 %collective-permute-start.13 = (bf16[128,128]{1,0:T(8,128)(2,1)S(1)}, bf16[128,128]{1,0:T(8,128)(2,1)S(1)}, u32[]{:S(2)}, u32[]{:S(2)}) collective-permute-start(bf16[128,128]{1,0:T(8,128)(2,1)S(1)} %get-tuple-element.93.refs_5_), channel_id=1, source_target_pairs={{0,2},{1,3},{2,0},{3,1},{4,6},{5,7},{6,4},{7,5},{8,10},{9,11},{10,... | collective-permute-start | bytes 98312 | tf_op jit(solution)/shard_map/ppermute | solution.py:212
  58.6 3.6 %collective-permute-start.12 = (bf16[128,128]{1,0:T(8,128)(2,1)S(1)}, bf16[128,128]{1,0:T(8,128)(2,1)S(1)}, u32[]{:S(2)}, u32[]{:S(2)}) collective-permute-start(bf16[128,128]{1,0:T(8,128)(2,1)S(1)} %get-tuple-element.93.refs_5_), channel_id=1, source_target_pairs={{0,1},{1,0},{2,3},{3,2},{4,5},{5,4},{6,7},{7,6},{8,9},{9,8},{10,11... | collective-permute-start | bytes 98312 | tf_op jit(solution)/shard_map/ppermute | solution.py:212
  65.3 10.4 %all-to-all-start.5 = ((bf16[32,2,640]{2,1,0:T(2,128)(2,1)}), bf16[32,2,640]{2,1,0:T(2,128)(2,1)S(1)}, u32[]{:S(2)}, u32[]{:S(2)}) async-start(bf16[32,2,640]{2,1,0:T(2,128)(2,1)} %bitcast.8), calls=%async_computation.5 | async-start | bytes 163840 | tf_op jit(solution)/shard_map/all_to_all | solution.py:216
  68.2 3.4 %collective-permute-start.17 = (bf16[128,128]{1,0:T(8,128)(2,1)S(1)}, bf16[128,128]{1,0:T(8,128)(2,1)S(1)}, u32[]{:S(2)}, u32[]{:S(2)}) collective-permute-start(bf16[128,128]{1,0:T(8,128)(2,1)S(1)} %get-tuple-element.101.refs_5_), channel_id=1, source_target_pairs={{0,3},{1,2},{2,1},{3,0},{4,7},{5,6},{6,5},{7,4},{8,11},{9,10},{10,... | collective-permute-start | bytes 98312 | tf_op jit(solution)/shard_map/ppermute | solution.py:212
  69.8 4.0 %collective-permute-start.16 = (bf16[128,128]{1,0:T(8,128)(2,1)S(1)}, bf16[128,128]{1,0:T(8,128)(2,1)S(1)}, u32[]{:S(2)}, u32[]{:S(2)}) collective-permute-start(bf16[128,128]{1,0:T(8,128)(2,1)S(1)} %get-tuple-element.101.refs_5_), channel_id=1, source_target_pairs={{0,2},{1,3},{2,0},{3,1},{4,6},{5,7},{6,4},{7,5},{8,10},{9,11},{10,... | collective-permute-start | bytes 98312 | tf_op jit(solution)/shard_map/ppermute | solution.py:212
  70.2 3.6 %collective-permute-start.15 = (bf16[128,128]{1,0:T(8,128)(2,1)S(1)}, bf16[128,128]{1,0:T(8,128)(2,1)S(1)}, u32[]{:S(2)}, u32[]{:S(2)}) collective-permute-start(bf16[128,128]{1,0:T(8,128)(2,1)S(1)} %get-tuple-element.101.refs_5_), channel_id=1, source_target_pairs={{0,1},{1,0},{2,3},{3,2},{4,5},{5,4},{6,7},{7,6},{8,9},{9,8},{10,11... | collective-permute-start | bytes 98312 | tf_op jit(solution)/shard_map/ppermute | solution.py:212
